TPU v7x, 256 devices: a whole 4x4x8 slice. The times are simulated.
256 devices in a mesh: clip: 32 (over z_hi, x, y), tm: 8 (over z_lo, core).
Axes of the slice: x: 4, y: 4, z: 8 (z_hi: 2, z_lo: 4; z = z_hi * 4 + z_lo), core: 2. Of those that a mesh axis runs over, the one named last changes fastest.
Arguments:
- audio_feats: bfloat16 [128, 2048, 256], P('clip', 'tm'), may hold values from -6 to 6
- lip_feats: bfloat16 [128, 2048, 256], P('clip', 'tm'), may hold values from -6 to 6
- lengths: int32 [128], P('clip'), may hold values from 1024 to 2048
- labels: int32 [128], P('clip'), may hold values from -15 to 15
- w_audio_conv: bfloat16 [3, 256, 512], replicated, may hold values from -0.21875 to 0.21875
- w_audio_proj: bfloat16 [512, 512], replicated, may hold values from -0.25 to 0.25
- w_lip_conv: bfloat16 [3, 256, 512], replicated, may hold values from -0.21875 to 0.21875
- w_lip_proj: bfloat16 [512, 512], replicated, may hold values from -0.25 to 0.25
Outputs:
- loss: float32 [], replicated
- grad_audio_conv: float32 [3, 256, 512], replicated
- grad_audio_proj: float32 [512, 512], replicated
- grad_lip_conv: float32 [3, 256, 512], replicated
- grad_lip_proj: float32 [512, 512], replicated
All inputs are finite; a program needn't handle non-finite values.
Results may differ from a plain program's by a relative error of at most 0.0075.
Values may be sent and summed in bfloat16 or wider, within the bound.
A program may use at most 64 MiB of HBM per device.

v0:
```python
import jax
import jax.numpy as jnp
from jax import lax
from jax.sharding import PartitionSpec as P

SPAN = 15


logit_sharpening_divisor = 10.0
loss_scale = 1024.0
epsilon = 1e-06


def padded_2(cells, sides, width):
    for axis, dim in sides:
        count = lax.axis_size(axis)
        ends = count - 1
        head = lax.slice_in_dim(cells, 0, width, axis=dim)
        tail = lax.slice_in_dim(cells, cells.shape[dim] - width, cells.shape[dim], axis=dim)
        cells = jnp.concatenate(
            [
                lax.ppermute(tail, axis, [(i, (i + 1) % count) for i in range(ends)]),
                cells,
                lax.ppermute(head, axis, [((i + 1) % count, i) for i in range(ends)]),
            ],
            axis=dim,
        )
    return cells


def from_behind(value, axis, steps):
    count = lax.axis_size(axis)
    initial, last = (max(0, -steps), min(count, count - steps))
    return lax.ppermute(value, axis, [(source, source + steps) for source in range(initial, last)])


def silu_slope(values):
    sigma = jax.nn.sigmoid(values)
    return sigma * (1.0 + values * (1.0 - sigma))


def encoder(padded, w_conv, w_proj):
    clip_num, frame_pad, chan_num = padded.shape
    frame_num = frame_pad - 2
    columns = jnp.concatenate(
        [padded[:, 0:frame_num], padded[:, 1 : frame_num + 1], padded[:, 2 : frame_num + 2]], axis=2
    )
    before = jnp.einsum(
        "cfk,ke->cfe",
        columns,
        w_conv.reshape(3 * chan_num, w_conv.shape[2]),
        preferred_element_type=jnp.float32,
    )
    hidden = jax.nn.silu(before).astype(jnp.bfloat16)
    embedded = jnp.einsum("cfe,eg->cfg", hidden, w_proj, preferred_element_type=jnp.float32).astype(
        jnp.bfloat16
    )
    return (columns, before, hidden, embedded)


def inverse_norm(embedded):
    values = embedded.astype(jnp.float32)
    return lax.rsqrt(jnp.sum(values * values, axis=-1) + epsilon)


def spread_band(band, wide_len):
    clip_num, row_num, band_len = band.shape
    full_band = jnp.pad(band, ((0, 0), (0, 0), (0, wide_len + 1 - band_len)))
    flat_band = full_band.reshape(clip_num, row_num * (wide_len + 1))[:, : row_num * wide_len]
    return flat_band.reshape(clip_num, row_num, wide_len)


def narrow_band(matrix, band_len):
    clip_num, row_num, wide_len = matrix.shape
    flat_mat = jnp.pad(matrix.reshape(clip_num, row_num * wide_len), ((0, 0), (0, row_num)))
    return flat_mat.reshape(clip_num, row_num, wide_len + 1)[:, :, :band_len]


def flatten_rows(values):
    return values.reshape(values.shape[0] * values.shape[1], values.shape[2])


def proj_grad(hidden, grad_emb):
    return jnp.einsum("re,rf->ef", hidden, grad_emb, preferred_element_type=jnp.float32)


def conv_grad(columns, before, grad_emb, w_proj, w_conv):
    grad_hidden = jnp.einsum("rf,ef->re", grad_emb, w_proj, preferred_element_type=jnp.float32)
    grad_before = (grad_hidden * silu_slope(before)).astype(jnp.bfloat16)
    grad_conv = jnp.einsum("rk,re->ke", columns, grad_before, preferred_element_type=jnp.float32)
    return grad_conv.reshape(w_conv.shape)


def shards(
    audio_feats, lip_feats, lengths, labels, w_audio_conv, w_audio_proj, w_lip_conv, w_lip_proj
):
    clip_num, frame_num, chan_num = audio_feats.shape
    width = w_audio_proj.shape[1]
    offsets = 2 * SPAN + 1
    wide_len = frame_num + 2 * SPAN
    first_frame = lax.axis_index("tm") * frame_num
    stacked = jnp.stack([audio_feats, lip_feats])
    padded = padded_2(stacked, (("tm", 2),), 1)
    cols_a, pre_a, hid_a, emb_a = encoder(padded[0], w_audio_conv, w_audio_proj)
    cols_v, pre_v, hid_v, emb_v = encoder(padded[1], w_lip_conv, w_lip_proj)
    window = padded_2(emb_a, (("tm", 1),), SPAN)
    cols_a, pre_a, hid_a = (flatten_rows(cols_a), flatten_rows(pre_a), flatten_rows(hid_a))
    cols_v, pre_v, hid_v = (flatten_rows(cols_v), flatten_rows(pre_v), flatten_rows(hid_v))
    count = lax.psum(jnp.sum((lengths - jnp.abs(labels)).astype(jnp.float32)), "clip")
    matrix = jnp.einsum("cfe,cwe->cfw", emb_v, window, preferred_element_type=jnp.float32)
    lagged_inner_terms = narrow_band(matrix, offsets)
    inv_win = inverse_norm(window)
    reciprocal_visual_length = inverse_norm(emb_v)
    reciprocal_lag_strip = jnp.stack(
        [inv_win[:, offset : offset + frame_num] for offset in range(offsets)], axis=2
    )
    frame_ids = first_frame + jnp.arange(frame_num, dtype=jnp.int32)
    shifts = jnp.arange(offsets, dtype=jnp.int32) - SPAN
    positions = frame_ids[:, None] + shifts[None, :]
    inside = frame_ids[None, :] < lengths[:, None]
    valid = inside[:, :, None] & (positions[None] >= 0) & (positions[None] < lengths[:, None, None])
    target_pos = frame_ids[None, :] + labels[:, None]
    counted = inside & (target_pos >= 0) & (target_pos < lengths[:, None])
    correct_lag_position = (shifts[None, :] == labels[:, None]).astype(jnp.float32)
    lag_similarity_logits = (
        logit_sharpening_divisor
        * lagged_inner_terms
        * reciprocal_visual_length[:, :, None]
        * reciprocal_lag_strip
    )
    exponentiated_logits = jnp.where(valid, jnp.exp(lag_similarity_logits), 0.0)
    partition_sums = jnp.where(inside, jnp.sum(exponentiated_logits, axis=2), 1.0)
    picked = jnp.sum(lag_similarity_logits * correct_lag_position[:, None, :], axis=2)
    loss_local = jnp.sum(jnp.where(counted, jnp.log(partition_sums) - picked, 0.0))
    normalized_probabilities = jnp.where(counted, loss_scale / count, 0.0)
    logit_derivative = (
        logit_sharpening_divisor
        * normalized_probabilities[:, :, None]
        * (exponentiated_logits / partition_sums[:, :, None] - correct_lag_position[:, None, :])
    )
    grad_dots = (
        logit_derivative * reciprocal_visual_length[:, :, None] * reciprocal_lag_strip
    ).astype(jnp.bfloat16)
    grad_inv_v = jnp.sum(logit_derivative * lagged_inner_terms * reciprocal_lag_strip, axis=2)
    grad_inv_win = jnp.sum(
        spread_band(
            logit_derivative * lagged_inner_terms * reciprocal_visual_length[:, :, None], wide_len
        ),
        axis=1,
    )
    band_full = spread_band(grad_dots, wide_len)
    lip_sum = jnp.einsum("cfw,cwe->cfe", band_full, window, preferred_element_type=jnp.float32)
    lip_vals = emb_v.astype(jnp.float32)
    grad_lip = (
        lip_sum
        - (
            reciprocal_visual_length
            * reciprocal_visual_length
            * reciprocal_visual_length
            * grad_inv_v
        )[:, :, None]
        * lip_vals
    ).astype(jnp.bfloat16)
    win_sum = jnp.einsum("cfw,cfe->cwe", band_full, emb_v, preferred_element_type=jnp.float32)
    win_sum = win_sum - (inv_win * inv_win * inv_win * grad_inv_win)[:, :, None] * window.astype(
        jnp.float32
    )
    own_grad = win_sum[:, SPAN : SPAN + frame_num]
    from_after = from_behind(win_sum[:, :SPAN], "tm", -1)
    from_before = from_behind(win_sum[:, frame_num + SPAN :], "tm", 1)
    own_grad = own_grad.at[:, frame_num - SPAN :].add(from_after)
    own_grad = own_grad.at[:, :SPAN].add(from_before)
    grad_audio = own_grad.astype(jnp.bfloat16).reshape(clip_num * frame_num, width)
    grad_lip = grad_lip.reshape(clip_num * frame_num, width)
    grad_ap = proj_grad(hid_a, grad_audio)
    grad_vp = proj_grad(hid_v, grad_lip)
    grad_ac = conv_grad(cols_a, pre_a, grad_audio, w_audio_proj, w_audio_conv)
    grad_vc = conv_grad(cols_v, pre_v, grad_lip, w_lip_proj, w_lip_conv)
    grad_ac, grad_vc, grad_ap, grad_vp, loss_sum = lax.psum(
        (grad_ac, grad_vc, grad_ap, grad_vp, loss_local), ("clip", "tm")
    )
    return (loss_sum / count, grad_ac, grad_ap, grad_vc, grad_vp)


def solution(mesh):
    placed = (
        P("clip", "tm", None),
        P("clip", "tm", None),
        P("clip"),
        P("clip"),
        P(),
        P(),
        P(),
        P(),
    )
    return jax.shard_map(
        shards, mesh=mesh, in_specs=placed, out_specs=(P(), P(), P(), P(), P()), check_vma=False
    )
```

profile of v0, /device:TPU:1, one launch (start us, length us, event | category | flops | bytes accessed | tf_op | source)
XLA Modules:
  0.0 491.1 jit_solution(7356766110926714444)
XLA Ops:
  7.2 0.8 pad_maximum_fusion.5
  8.1 4.9 %collective-permute-start = (bf16[2,4,1,256]{3,2,1,0:T(2,128)(2,1)S(1)}, bf16[2,4,1,256]{3,2,1,0:T(2,128)(2,1)S(1)}, u32[]{:S(2)}, u32[]{:S(2)}) collective-permute-start(bf16[2,4,1,256]{3,2,1,0:T(2,128)(2,1)S(1)} %get-tuple-element.45), channel_id=1, source_target_pairs={{0,1},{1,2},{2,3},{3,4},{4,5},{5,6},{6,7},{8,9},{9,10},{10,11},{11... | collective-permute-start | bytes 12296 | tf_op jit(solution)/shard_map/ppermute | solution.py:22
  13.0 1.9 collective-permute-start.1
  15.0 0.7 broadcast_compare_fusion
  15.8 1.3 compare_convert_fusion
  17.1 1.3 convert_reduce_fusion
  18.4 1.2 broadcast_compare_fusion.1
  19.6 106.0 %psum.43 = f32[]{:T(128)} all-reduce(f32[]{:T(128)} %convert_reduce_fusion), channel_id=1, replica_groups=mesh['clip'=32,'tm'=8] {'clip'}, use_global_device_ids=true, to_apply=%region_7.8 | all-reduce | flops 1 | bytes 8 | tf_op jit(solution)/shard_map/psum | solution.py:109
  126.3 1.5 pad_maximum_fusion.3
  127.8 0.6 fusion.33
  128.4 0.1 pad_maximum_fusion
  128.6 1.0 fusion.30
  129.6 1.8 fusion.2
  131.4 0.6 add_rsqrt_fusion.1
  132.0 1.0 fusion.29
  133.0 0.7 convolution_convert_fusion
  133.8 0.6 copy-done.27
  134.4 0.7 fusion.32
  135.1 17.3 %collective-permute-start.2 = (bf16[4,15,512]{2,1,0:T(8,128)(2,1)}, bf16[4,15,512]{2,1,0:T(8,128)(2,1)}, u32[]{:S(2)}, u32[]{:S(2)}) collective-permute-start(bf16[4,15,512]{2,1,0:T(8,128)(2,1)} %get-tuple-element.43), channel_id=1, source_target_pairs={{0,1},{1,2},{2,3},{3,4},{4,5},{5,6},{6,7},{8,9},{9,10},{10,11},{11... | collective-permute-start | bytes 184328 | tf_op jit(solution)/shard_map/ppermute | solution.py:22
  152.4 1.9 collective-permute-start.3
  154.3 1.2 pad_maximum_fusion.1
  155.6 1.7 copy.1171
  157.2 2.6 copy.1167
  159.8 1.4 fusion
  163.5 0.3 copy.1166
  163.8 2.3 fusion.28
  166.1 2.5 reshape.357
  168.6 1.5 pad.16
  170.2 2.6 reshape.358
  172.8 1.6 fusion.23
  174.5 2.8 multiply_reduce_fusion
  177.3 0.1 pad.17
  177.4 1.2 reshape.360
  178.6 0.2 slice.289
  178.8 1.7 reshape.361
  180.5 2.7 fusion.4
  183.3 1.7 convolution_bitcast_fusion
  185.0 2.2 fusion.20
  187.3 1.4 reshape.362
  188.7 1.1 slice.290
  189.8 3.1 reshape.363
  193.1 2.4 fusion.1
  195.5 3.6 collective-permute-start.5
  199.1 1.9 collective-permute-start.4
  201.0 2.2 fusion.36
  203.2 0.2 slice.291
  203.5 1.9 collective-permute-done.4
  205.4 0.5 scatter-add.6
  206.0 0.4 scatter-add.9
  206.3 0.1 convert_element_type.60
  206.5 1.4 copy-done.28
  207.9 1.7 convolution_bitcast_fusion.1
  209.7 1.2 fusion.19
  210.9 0.2 copy-done.1
  211.1 2.1 fusion.35
  213.2 0.6 copy-done.12
  213.9 0.7 select_reduce_fusion
  214.6 72.8 %psum.42 = f32[]{:T(128)} all-reduce(f32[]{:T(128)} %select_reduce_fusion), channel_id=1, replica_groups=mesh['clip'=32,'tm'=8] {'clip','tm'}, use_global_device_ids=true, to_apply=%region_5.6 | all-reduce | flops 1 | bytes 8 | tf_op jit(solution)/shard_map/psum | solution.py:179
  288.7 187.8 %all-reduce.6.cloned.1.call-done = (f32[3,256,512]{2,1,0:T(8,128)}, f32[512,512]{1,0:T(8,128)}, f32[3,256,512]{2,1,0:T(8,128)}, f32[512,512]{1,0:T(8,128)}) async-done(((f32[3,256,512]{2,1,0:T(8,128)}, f32[512,512]{1,0:T(8,128)}, f32[3,256,512]{2,1,0:T(8,128)}, f32[512,512]{1,0:T(8,128)}), (f32[3,256,512]{2,1,0:T(8,128)}, f32[512,512]{1,0:T(8,128)}, f32[3,256,512]{2,1,0:T(8,128)}, ...) | async-done | bytes 5242896 | tf_op jit(solution)/shard_map/psum | solution.py:179
  476.6 2.8 copy.1216
  479.4 1.0 copy.1217
  480.4 1.1 copy.1218
  481.5 0.6 copy-done.6
  482.1 1.0 copy.1219
  (108 shorter events, 3.2 us)
Async XLA Ops:
  7.2 121.4 %copy-start = (bf16[3,256,512]{2,1,0:T(8,128)(2,1)S(1)}, bf16[3,256,512]{2,1,0:T(8,128)(2,1)}, u32[]{:S(2)}) copy-start(bf16[3,256,512]{2,1,0:T(8,128)(2,1)} %param.18) | copy-start | bytes 2359300
  7.2 469.4 %all-reduce.6.cloned.1.call-start = ((), (), s32[]{:S(2)}) async-start(), calls=%async_computation | async-start | bytes 10485760 | tf_op jit(solution)/shard_map/psum | solution.py:179
  8.1 118.2 %collective-permute-start = (bf16[2,4,1,256]{3,2,1,0:T(2,128)(2,1)S(1)}, bf16[2,4,1,256]{3,2,1,0:T(2,128)(2,1)S(1)}, u32[]{:S(2)}, u32[]{:S(2)}) collective-permute-start(bf16[2,4,1,256]{3,2,1,0:T(2,128)(2,1)S(1)} %get-tuple-element.45), channel_id=1, source_target_pairs={{0,1},{1,2},{2,3},{3,4},{4,5},{5,6},{6,7},{8,9},{9,10},{10,11},{11... | collective-permute-start | bytes 12296 | tf_op jit(solution)/shard_map/ppermute | solution.py:22
  13.0 113.2 %collective-permute-start.1 = (bf16[2,4,1,256]{3,2,1,0:T(2,128)(2,1)S(1)}, bf16[2,4,1,256]{3,2,1,0:T(2,128)(2,1)S(1)}, u32[]{:S(2)}, u32[]{:S(2)}) collective-permute-start(bf16[2,4,1,256]{3,2,1,0:T(2,128)(2,1)S(1)} %get-tuple-element.46), channel_id=1, source_target_pairs={{1,0},{2,1},{3,2},{4,3},{5,4},{6,5},{7,6},{9,8},{10,9},{11,10},{12... | collective-permute-start | bytes 12296 | tf_op jit(solution)/shard_map/ppermute | solution.py:24
  128.6 1.0 copy-start.22
  129.6 1.8 copy-start.29
  129.6 2.4 copy-start.21
  131.4 1.6 copy-start.13
  132.0 1.0 copy-start.24
  133.0 1.3 copy-start.27
  134.4 25.4 %copy-start.4 = (bf16[4,256,512]{2,1,0:T(8,128)(2,1)}, bf16[4,256,512]{2,1,0:T(8,128)(2,1)S(1)}, u32[]{:S(2)}) copy-start(bf16[4,256,512]{2,1,0:T(8,128)(2,1)S(1)} %convolution_convert_fusion) | copy-start | bytes 3145732
  135.1 24.7 %collective-permute-start.2 = (bf16[4,15,512]{2,1,0:T(8,128)(2,1)}, bf16[4,15,512]{2,1,0:T(8,128)(2,1)}, u32[]{:S(2)}, u32[]{:S(2)}) collective-permute-start(bf16[4,15,512]{2,1,0:T(8,128)(2,1)} %get-tuple-element.43), channel_id=1, source_target_pairs={{0,1},{1,2},{2,3},{3,4},{4,5},{5,6},{6,7},{8,9},{9,10},{10,11},{11... | collective-permute-start | bytes 184328 | tf_op jit(solution)/shard_map/ppermute | solution.py:22
  152.4 7.4 %collective-permute-start.3 = (bf16[4,15,512]{2,1,0:T(8,128)(2,1)}, bf16[4,15,512]{2,1,0:T(8,128)(2,1)}, u32[]{:S(2)}, u32[]{:S(2)}) collective-permute-start(bf16[4,15,512]{2,1,0:T(8,128)(2,1)} %get-tuple-element.44), channel_id=1, source_target_pairs={{1,0},{2,1},{3,2},{4,3},{5,4},{6,5},{7,6},{9,8},{10,9},{11,10},{12... | collective-permute-start | bytes 184328 | tf_op jit(solution)/shard_map/ppermute | solution.py:24
  168.6 4.2 copy-start.9
  168.6 4.2 copy-start.11
  168.6 4.2 copy-start.15
  168.6 4.2 copy-start.17
  170.1 4.3 copy-start.19
  170.2 4.3 copy-start.10
  170.2 4.3 copy-start.18
  172.8 4.5 copy-start.14
  180.5 2.7 copy-start.8
  180.5 2.7 copy-start.30
  183.3 1.8 copy-start.23
  189.8 3.2 copy-start.5
  193.0 8.0 %copy-start.2 = (bf16[768,1024]{1,0:T(8,128)(2,1)S(1)}, bf16[768,1024]{1,0:T(8,128)(2,1)}, u32[]{:S(2)}) copy-start(bf16[768,1024]{1,0:T(8,128)(2,1)} %copy.1171) | copy-start | bytes 4718596
  193.0 8.0 %copy-start.26 = (bf16[1024,512,1]{1,0,2:T(8,128)(2,1)S(1)}, bf16[1024,512,1]{1,0,2:T(8,128)(2,1)}, u32[]{:S(2)}) copy-start(bf16[1024,512,1]{1,0,2:T(8,128)(2,1)} %fusion.20) | copy-start | bytes 3145732
  195.5 10.5 %collective-permute-start.5 = (f32[4,15,512]{2,1,0:T(8,128)S(1)}, f32[4,15,512]{2,1,0:T(8,128)S(1)}, u32[]{:S(2)}, u32[]{:S(2)}) collective-permute-start(f32[4,15,512]{2,1,0:T(8,128)S(1)} %get-tuple-element.37), channel_id=1, source_target_pairs={{0,1},{1,2},{2,3},{3,4},{4,5},{5,6},{6,7},{8,9},{9,10},{10,11},{11... | collective-permute-start | bytes 368648 | tf_op jit(solution)/shard_map/ppermute | solution.py:34
  199.1 6.3 %collective-permute-start.4 = (f32[4,15,512]{2,1,0:T(8,128)S(1)}, f32[4,15,512]{2,1,0:T(8,128)S(1)}, u32[]{:S(2)}, u32[]{:S(2)}) collective-permute-start(f32[4,15,512]{2,1,0:T(8,128)S(1)} %get-tuple-element.38), channel_id=1, source_target_pairs={{1,0},{2,1},{3,2},{4,3},{5,4},{6,5},{7,6},{9,8},{10,9},{11,10},{12... | collective-permute-start | bytes 368648 | tf_op jit(solution)/shard_map/ppermute | solution.py:34
  206.3 1.6 copy-start.28
  207.9 1.8 copy-start.25
  209.7 1.4 copy-start.1
  213.2 0.7 copy-start.12
  213.2 0.7 copy-start.16
  213.2 0.7 copy-start.20
  476.6 2.8 copy-start.7
  476.6 3.8 copy-start.3
  480.4 1.8 copy-start.6
Sparse Core Ops, SparseCore 0:
  213.4 263.1 all-reduce.5
where the time goes:
time: 493 us; the launch traced here: 491 us
  waiting for transfers between devices  190 us (39%)
  blocking collectives  179 us (36%)
  local copies, waits for them, and re-layouts  34.6 us (7%)
  starting transfers between devices  31.7 us (6%)
  matrix products  22.9 us (5%)
  between operations  17.7 us (4%)
  other arithmetic  15.7 us (3%)
    psum x1, waiting for transfers between devices, shards(): lax.psum((grad_ac, grad_vc, grad_ap, grad_vp, loss_local), ('clip', 'tm'))  188 us
    psum x1, blocking collectives, shards(): lax.psum(jnp.sum((lengths - jnp.abs(labels)).astype(jnp.float32)), 'clip')  106 us
    psum x1, blocking collectives, shards(): lax.psum((grad_ac, grad_vc, grad_ap, grad_vp, loss_local), ('clip', 'tm'))  72.8 us
    ppermute x2, starting transfers between devices, padded_2(): lax.ppermute(tail, axis, [(i, (i + 1) % count) for i in range(ends)])  22.2 us
    unnamed x96, local copies, waits for them, and re-layouts  12 us
  transfers between devices with their start and end apart: 7, of which 2 were waited for; matrix products, arithmetic and copies ran while one was open for 3% of the time, Pallas kernels for 0%

commit v1 on v0

--- a/solution.py
+++ b/solution.py
@@ -2,8 +2,161 @@
 import jax.numpy as jnp
 from jax import lax
 from jax.sharding import PartitionSpec as P
+import functools
+from jax.experimental import pallas as pl
+from jax.experimental.pallas import tpu as pltpu
 
 SPAN = 15
+
+
+MESH_ID = pl.DeviceIdType.MESH
+
+
+def _coords():
+    ci = lax.axis_index("clip")
+    ti = lax.axis_index("tm")
+    y = ci % 4
+    x = (ci // 4) % 4
+    zh = ci // 16
+    core = ti % 2
+    zl = ti // 2
+    return ci, ti, y, x, zh, core, zl
+
+
+def _levels(rows):
+    ci, ti, y, x, zh, core, zl = _coords()
+    z = zh * 4 + zl
+
+    def at_y(v):
+        return (zh * 16 + x * 4 + v % 4, ti)
+
+    def at_x(v):
+        return (zh * 16 + (v % 4) * 4 + y, ti)
+
+    def at_z(v):
+        w = v % 8
+        return ((w // 4) * 16 + x * 4 + y, (w % 4) * 2 + core)
+
+    def at_c(v):
+        return (ci, zl * 2 + v % 2)
+
+    return [("c", 2, core, at_c, 1), ("y", 4, y, at_y, 2), ("x", 4, x, at_x, 2), ("z", 8, z, at_z, 1)]
+
+
+def _kernel(rows, x_ref, o_ref, work, rbuf, send_sem, recv_sem):
+    levels = _levels(rows)
+    barrier = pltpu.get_barrier_semaphore()
+    peers = []
+    for name, n, me, nbr, ndir in levels:
+        peers.append(nbr(me + 1))
+        if n > 2:
+            peers.append(nbr(me - 1))
+    for p in peers:
+        pl.semaphore_signal(barrier, inc=1, device_id=p, device_id_type=MESH_ID)
+    pl.semaphore_wait(barrier, len(peers))
+
+    base = 0
+    size = rows
+    slot = 0
+    sem = 0
+    plan = []
+    for li, (name, n, me, nbr, ndir) in enumerate(levels):
+        chunk = size // n
+        piece = chunk // ndir
+        own = x_ref if li == 0 else work
+
+        def pos(k, d, base=base, chunk=chunk, piece=piece):
+            return pl.multiple_of(base + k * chunk + d * piece, 8)
+
+        for s in range(n - 1):
+            copies = []
+            for d in range(ndir):
+                sign = 1 if d == 0 else -1
+                send_k = (me - sign * (s + 1)) % n
+                recv_k = (me - sign * (s + 2)) % n
+                src = own if s == 0 else work
+                c = pltpu.make_async_remote_copy(
+                    src_ref=src.at[pl.ds(pos(send_k, d), piece)],
+                    dst_ref=rbuf.at[pl.ds(slot, piece)],
+                    send_sem=send_sem.at[sem],
+                    recv_sem=recv_sem.at[sem],
+                    device_id=nbr(me + sign),
+                    device_id_type=MESH_ID,
+                )
+                c.start()
+                copies.append((c, slot, recv_k, d))
+                slot += piece
+                sem += 1
+            for c, sl, recv_k, d in copies:
+                c.wait_recv()
+                at = pl.ds(pos(recv_k, d), piece)
+                work[at] = rbuf[pl.ds(sl, piece)] + own[at]
+            for c, sl, recv_k, d in copies:
+                c.wait_send()
+        plan.append((name, n, me, nbr, ndir, base, chunk, piece))
+        base = base + me * chunk
+        size = chunk
+
+    fin = pl.ds(pl.multiple_of(base, 8), size)
+    o_ref[fin] = work[fin]
+    for name, n, me, nbr, ndir, lbase, chunk, piece in reversed(plan):
+
+        def pos(k, d, base=lbase, chunk=chunk, piece=piece):
+            return pl.multiple_of(base + k * chunk + d * piece, 8)
+
+        for s in range(n - 1):
+            copies = []
+            for d in range(ndir):
+                sign = 1 if d == 0 else -1
+                send_k = (me - sign * s) % n
+                at = pl.ds(pos(send_k, d), piece)
+                c = pltpu.make_async_remote_copy(
+                    src_ref=o_ref.at[at],
+                    dst_ref=o_ref.at[at],
+                    send_sem=send_sem.at[sem],
+                    recv_sem=recv_sem.at[sem],
+                    device_id=nbr(me + sign),
+                    device_id_type=MESH_ID,
+                )
+                c.start()
+                copies.append(c)
+                sem += 1
+            for c in copies:
+                c.wait()
+    return None
+
+
+def _counts(rows):
+    slot = 0
+    sem = 0
+    size = rows
+    for name, n, ndir in (("c", 2, 1), ("y", 4, 2), ("x", 4, 2), ("z", 8, 1)):
+        chunk = size // n
+        piece = chunk // ndir
+        slot += piece * ndir * (n - 1)
+        sem += 2 * ndir * (n - 1)
+        size = chunk
+    return slot, sem
+
+
+def all_sum(flat):
+    rows = flat.shape[0]
+    slots, sems = _counts(rows)
+    return pl.pallas_call(
+        functools.partial(_kernel, rows),
+        out_shape=jax.ShapeDtypeStruct(flat.shape, flat.dtype),
+        in_specs=[pl.BlockSpec(memory_space=pltpu.VMEM)],
+        out_specs=pl.BlockSpec(memory_space=pltpu.VMEM),
+        scratch_shapes=[
+            pltpu.VMEM(flat.shape, flat.dtype),
+            pltpu.VMEM((slots, flat.shape[1]), flat.dtype),
+            pltpu.SemaphoreType.DMA((sems,)),
+            pltpu.SemaphoreType.DMA((sems,)),
+        ],
+        compiler_params=pltpu.CompilerParams(
+            collective_id=0, has_side_effects=True, vmem_limit_bytes=48 * 1024 * 1024
+        ),
+    )(flat)
 
 
 logit_sharpening_divisor = 10.0
@@ -106,7 +259,8 @@
     window = padded_2(emb_a, (("tm", 1),), SPAN)
     cols_a, pre_a, hid_a = (flatten_rows(cols_a), flatten_rows(pre_a), flatten_rows(hid_a))
     cols_v, pre_v, hid_v = (flatten_rows(cols_v), flatten_rows(pre_v), flatten_rows(hid_v))
-    count = lax.psum(jnp.sum((lengths - jnp.abs(labels)).astype(jnp.float32)), "clip")
+    count_part = jnp.sum(lengths - jnp.abs(labels))
+    count = jnp.sum(lax.all_gather(count_part, "clip")).astype(jnp.float32)
     matrix = jnp.einsum("cfe,cwe->cfw", emb_v, window, preferred_element_type=jnp.float32)
     lagged_inner_terms = narrow_band(matrix, offsets)
     inv_win = inverse_norm(window)
@@ -176,9 +330,17 @@
     grad_vp = proj_grad(hid_v, grad_lip)
     grad_ac = conv_grad(cols_a, pre_a, grad_audio, w_audio_proj, w_audio_conv)
     grad_vc = conv_grad(cols_v, pre_v, grad_lip, w_lip_proj, w_lip_conv)
-    grad_ac, grad_vc, grad_ap, grad_vp, loss_sum = lax.psum(
-        (grad_ac, grad_vc, grad_ap, grad_vp, loss_local), ("clip", "tm")
-    )
+    parts = (grad_ac, grad_vc, grad_ap, grad_vp)
+    flat = jnp.concatenate([g.reshape(-1, 128) for g in parts], axis=0)
+    total = all_sum(flat)
+    outs = []
+    start = 0
+    for g in parts:
+        rows = g.size // 128
+        outs.append(total[start : start + rows].reshape(g.shape))
+        start += rows
+    grad_ac, grad_vc, grad_ap, grad_vp = outs
+    loss_sum = jnp.sum(lax.all_gather(loss_local, ("clip", "tm")))
     return (loss_sum / count, grad_ac, grad_ap, grad_vc, grad_vp)
 
 

time: 493 us -> 335 us (0.68)
  waiting for transfers between devices: 190 us -> 2.87 us
  Pallas kernels: 0 us -> 130 us
  blocking collectives: 179 us -> 92.2 us
  between operations: 17.7 us -> 3.69 us
  starting transfers between devices: 31.7 us -> 22.9 us
  local copies, waits for them, and re-layouts: 34.6 us -> 42.1 us
    psum x1 -> x0, waiting for transfers between devices: 188 us -> none  [shards(): lax.psum((grad_ac, grad_vc, grad_ap, grad_vp, loss_local), ('clip', 'tm'))]
    psum x2 -> x0, blocking collectives: 179 us -> none  [the longest x1 106 us: shards(): lax.psum(jnp.sum((lengths - jnp.abs(labels)).astype(jnp.float32)), 'clip')]
    pallas_call x0 -> x1, Pallas kernels: none -> 130 us  [all_sum(): pl.pallas_call(functools.partial(_kernel, rows), out_shape=jax.ShapeDtype...]
    unnamed x0 -> x2, blocking collectives: none -> 92.2 us
    reshape x0 -> x6, local copies, waits for them, and re-layouts: none -> 10.7 us  [the longest x4 7.41 us: shards(): outs.append(total[start:start + rows].reshape(g.shape))]
    ppermute x2, starting transfers between devices: 22.2 us -> 13 us  [padded_2(): lax.ppermute(tail, axis, [(i, (i + 1) % count) for i in range(ends)])]
    concatenate x0 -> x1, other arithmetic: none -> 5.68 us  [shards(): flat = jnp.concatenate([g.reshape(-1, 128) for g in parts], axis=0)]
    unnamed x96 -> x97, local copies, waits for them, and re-layouts: 12 us -> 9.37 us
  transfers between devices with their start and end apart: 7 -> 6, of which waited for: 2 -> 2; matrix products, arithmetic and copies ran while one was open for 3% -> 5% of each run, Pallas kernels for 0% -> 0%
where the time goes in v1:
time: 335 us; the launch traced here: 334 us
  Pallas kernels  130 us (39%)
  blocking collectives  92.2 us (28%)
  local copies, waits for them, and re-layouts  42.1 us (13%)
  starting transfers between devices  22.9 us (7%)
  matrix products  20.8 us (6%)
  other arithmetic  19.5 us (6%)
  between operations  3.69 us (1%)
    pallas_call x1, Pallas kernels, all_sum(): pl.pallas_call(functools.partial(_kernel, rows), out_shape=jax.ShapeDtype...  130 us
    unnamed x2, blocking collectives  92.2 us
    ppermute x2, starting transfers between devices, padded_2(): lax.ppermute(tail, axis, [(i, (i + 1) % count) for i in range(ends)])  13 us
    unnamed x97, local copies, waits for them, and re-layouts  9.37 us
    reshape x4, local copies, waits for them, and re-layouts, shards(): outs.append(total[start:start + rows].reshape(g.shape))  7.41 us
  transfers between devices with their start and end apart: 6, of which 2 were waited for; matrix products, arithmetic and copies ran while one was open for 5% of the time, Pallas kernels for 0%

profile of v1, /device:TPU:1, one launch (start us, length us, event | category | flops | bytes accessed | tf_op | source)
XLA Modules:
  0.0 333.7 jit_solution(7878852485140679263)
XLA Ops:
  0.6 0.9 pad_maximum_fusion.6
  1.5 4.9 %collective-permute-start = (bf16[2,4,1,256]{3,2,1,0:T(2,128)(2,1)S(1)}, bf16[2,4,1,256]{3,2,1,0:T(2,128)(2,1)S(1)}, u32[]{:S(2)}, u32[]{:S(2)}) collective-permute-start(bf16[2,4,1,256]{3,2,1,0:T(2,128)(2,1)S(1)} %get-tuple-element.45), channel_id=1, source_target_pairs={{0,1},{1,2},{2,3},{3,4},{4,5},{5,6},{6,7},{8,9},{9,10},{10,11},{11... | collective-permute-start | bytes 12296 | tf_op jit(solution)/shard_map/ppermute | solution.py:175
  6.5 1.9 collective-permute-start.1
  8.6 0.7 broadcast_compare_fusion.1
  9.4 0.7 compare_convert_fusion
  10.1 1.3 subtract_reduce_fusion
  11.4 1.3 dynamic-slice.16
  12.7 1.4 dynamic-update-slice.7
  14.1 19.9 %all-reduce.4 = s32[32]{0:T(128)S(1)} all-reduce(s32[32]{0:T(128)S(1)} %dynamic-update-slice.7), channel_id=1, replica_groups=mesh['clip'=32,'tm'=8] {'clip'}, use_global_device_ids=true, to_apply=%add.4 | all-reduce | flops 32 | bytes 256
  34.0 0.6 reduce_sum.97
  35.3 1.5 pad_maximum_fusion.4
  36.9 0.6 fusion.33
  37.5 1.2 pad_maximum_fusion.1
  38.7 1.0 fusion.28
  39.8 0.9 fusion.2
  40.7 0.4 copy-done.29
  41.5 1.0 fusion.27
  42.5 0.7 convolution_convert_fusion
  43.3 0.6 copy-done.27
  43.8 8.1 %collective-permute-start.2 = (bf16[4,15,512]{2,1,0:T(8,128)(2,1)S(1)}, bf16[4,15,512]{2,1,0:T(8,128)(2,1)S(1)}, u32[]{:S(2)}, u32[]{:S(2)}) collective-permute-start(bf16[4,15,512]{2,1,0:T(8,128)(2,1)S(1)} %get-tuple-element.43), channel_id=1, source_target_pairs={{0,1},{1,2},{2,3},{3,4},{4,5},{5,6},{6,7},{8,9},{9,10},{10,11},{11... | collective-permute-start | bytes 184328 | tf_op jit(solution)/shard_map/ppermute | solution.py:175
  51.9 1.9 collective-permute-start.3
  53.8 1.3 pad_maximum_fusion.2
  55.1 2.4 collective-permute-done.3
  57.5 0.5 fusion
  60.7 1.9 fusion.26
  62.5 2.9 reshape.371
  65.7 1.5 reshape.372
  67.2 0.5 fusion.21
  67.8 1.8 multiply_reduce_fusion
  69.7 1.2 reshape.374
  71.1 1.7 reshape.375
  72.8 2.1 fusion.4
  75.0 1.8 convolution_bitcast_fusion
  76.8 2.2 fusion.11
  79.0 1.4 reshape.376
  80.5 1.1 slice.306
  81.6 3.1 reshape.377
  84.8 2.1 fusion.1
  87.0 1.9 collective-permute-start.4
  89.0 2.1 fusion.36
  91.8 0.7 select_reduce_fusion
  92.5 0.8 dynamic-update-slice.6
  93.2 72.2 %all-reduce.3 = f32[256]{0:T(256)S(1)} all-reduce(f32[256]{0:T(256)S(1)} %dynamic-update-slice.6), channel_id=1, replica_groups=mesh['clip'=32,'tm'=8] {'clip','tm'}, use_global_device_ids=true, to_apply=%add.3 | all-reduce | flops 256 | bytes 2048
  165.5 0.6 reduce_sum.95
  166.7 2.4 reshape_reshape.7
  169.2 1.0 reshape.384
  170.2 4.1 %collective-permute-start.5 = (f32[4,15,512]{2,1,0:T(8,128)S(1)}, f32[4,15,512]{2,1,0:T(8,128)S(1)}, u32[]{:S(2)}, u32[]{:S(2)}) collective-permute-start(f32[4,15,512]{2,1,0:T(8,128)S(1)} %get-tuple-element.37), channel_id=1, source_target_pairs={{0,1},{1,2},{2,3},{3,4},{4,5},{5,6},{6,7},{8,9},{9,10},{10,11},{11... | collective-permute-start | bytes 368648 | tf_op jit(solution)/shard_map/ppermute | solution.py:187
  174.3 0.9 slice_add_fusion.1
  175.3 0.5 scatter-add.6
  175.8 0.5 collective-permute-done.5
  176.8 1.4 copy-done.28
  178.2 1.7 convolution_bitcast_fusion.1
  180.0 1.2 fusion.18
  181.4 2.1 fusion.35
  183.6 1.5 reshape_reshape.6
  185.1 2.3 reshape.383
  187.4 5.7 %pad_maximum_fusion.x_ref = f32[10240,128]{1,0:T(8,128)} fusion(f32[2048,128]{1,0:T(8,128)} %reshape.384, f32[2048,128]{1,0:T(8,128)} %reshape.383, f32[3072,128]{1,0:T(8,128)S(1)} %copy-done.2, f32[3072,128]{1,0:T(8,128)S(1)} %reshape_reshape.6), kind=kLoop, calls=%fused_computation | loop fusion | flops 3932160 | bytes 10485760 | tf_op jit(solution)/shard_map/concatenate | solution.py:334
  193.0 129.6 %shard_map.119 = f32[10240,128]{1,0:T(8,128)S(1)} custom-call(f32[10240,128]{1,0:T(8,128)} %pad_maximum_fusion.x_ref), custom_call_target="tpu_custom_call" | custom-call | tf_op jit(solution)/shard_map/pallas_call | solution.py:145
  322.7 1.1 fusion.29
  323.8 1.3 fusion.30
  325.1 2.5 reshape.387
  327.7 2.4 reshape.388
  330.0 1.1 reshape.386
  331.2 1.4 reshape.385
  (118 shorter events, 5.8 us)
Async XLA Ops:
  0.6 38.1 %copy-start = (bf16[3,256,512]{2,1,0:T(8,128)(2,1)S(1)}, bf16[3,256,512]{2,1,0:T(8,128)(2,1)}, u32[]{:S(2)}) copy-start(bf16[3,256,512]{2,1,0:T(8,128)(2,1)} %param.18) | copy-start | bytes 2359300
  1.5 33.8 %collective-permute-start = (bf16[2,4,1,256]{3,2,1,0:T(2,128)(2,1)S(1)}, bf16[2,4,1,256]{3,2,1,0:T(2,128)(2,1)S(1)}, u32[]{:S(2)}, u32[]{:S(2)}) collective-permute-start(bf16[2,4,1,256]{3,2,1,0:T(2,128)(2,1)S(1)} %get-tuple-element.45), channel_id=1, source_target_pairs={{0,1},{1,2},{2,3},{3,4},{4,5},{5,6},{6,7},{8,9},{9,10},{10,11},{11... | collective-permute-start | bytes 12296 | tf_op jit(solution)/shard_map/ppermute | solution.py:175
  6.5 28.9 %collective-permute-start.1 = (bf16[2,4,1,256]{3,2,1,0:T(2,128)(2,1)S(1)}, bf16[2,4,1,256]{3,2,1,0:T(2,128)(2,1)S(1)}, u32[]{:S(2)}, u32[]{:S(2)}) collective-permute-start(bf16[2,4,1,256]{3,2,1,0:T(2,128)(2,1)S(1)} %get-tuple-element.46), channel_id=1, source_target_pairs={{1,0},{2,1},{3,2},{4,3},{5,4},{6,5},{7,6},{9,8},{10,9},{11,10},{12... | collective-permute-start | bytes 12296 | tf_op jit(solution)/shard_map/ppermute | solution.py:177
  38.7 1.0 copy-start.21
  39.8 1.3 copy-start.29
  39.8 1.7 copy-start.20
  41.1 19.5 %copy-start.25 = (bf16[4,256,512]{2,1,0:T(8,128)(2,1)}, bf16[4,256,512]{2,1,0:T(8,128)(2,1)S(1)}, u32[]{:S(2)}) copy-start(bf16[4,256,512]{2,1,0:T(8,128)(2,1)S(1)} %get-tuple-element.58) | copy-start | bytes 3145732
  41.5 1.1 copy-start.23
  42.5 1.3 copy-start.27
  43.8 16.8 %copy-start.7 = (bf16[4,256,512]{2,1,0:T(8,128)(2,1)}, bf16[4,256,512]{2,1,0:T(8,128)(2,1)S(1)}, u32[]{:S(2)}) copy-start(bf16[4,256,512]{2,1,0:T(8,128)(2,1)S(1)} %convolution_convert_fusion) | copy-start | bytes 3145732
  43.8 11.3 %collective-permute-start.2 = (bf16[4,15,512]{2,1,0:T(8,128)(2,1)S(1)}, bf16[4,15,512]{2,1,0:T(8,128)(2,1)S(1)}, u32[]{:S(2)}, u32[]{:S(2)}) collective-permute-start(bf16[4,15,512]{2,1,0:T(8,128)(2,1)S(1)} %get-tuple-element.43), channel_id=1, source_target_pairs={{0,1},{1,2},{2,3},{3,4},{4,5},{5,6},{6,7},{8,9},{9,10},{10,11},{11... | collective-permute-start | bytes 184328 | tf_op jit(solution)/shard_map/ppermute | solution.py:175
  51.9 5.6 %collective-permute-start.3 = (bf16[4,15,512]{2,1,0:T(8,128)(2,1)S(1)}, bf16[4,15,512]{2,1,0:T(8,128)(2,1)S(1)}, u32[]{:S(2)}, u32[]{:S(2)}) collective-permute-start(bf16[4,15,512]{2,1,0:T(8,128)(2,1)S(1)} %get-tuple-element.44), channel_id=1, source_target_pairs={{1,0},{2,1},{3,2},{4,3},{5,4},{6,5},{7,6},{9,8},{10,9},{11,10},{12... | collective-permute-start | bytes 184328 | tf_op jit(solution)/shard_map/ppermute | solution.py:177
  55.1 5.5 %copy-start.11 = (bf16[4,15,512]{2,1,0:T(8,128)(2,1)}, bf16[4,15,512]{2,1,0:T(8,128)(2,1)S(1)}, u32[]{:S(2)}) copy-start(bf16[4,15,512]{2,1,0:T(8,128)(2,1)S(1)} %collective-permute-done.2) | copy-start | bytes 184324
  57.5 3.2 copy-start.14
  65.4 1.7 copy-start.16
  65.7 2.1 copy-start.18
  69.7 3.1 copy-start.8
  69.7 3.1 copy-start.12
  69.7 3.1 copy-start.15
  72.8 2.2 copy-start.30
  75.0 1.8 copy-start.22
  76.8 2.2 copy-start.4
  81.6 3.2 copy-start.9
  81.6 3.2 copy-start.13
  84.8 4.1 %copy-start.6 = (bf16[4,256,768]{2,1,0:T(8,128)(2,1)S(1)}, bf16[4,256,768]{2,1,0:T(8,128)(2,1)}, u32[]{:S(2)}) copy-start(bf16[4,256,768]{2,1,0:T(8,128)(2,1)} %pad_maximum_fusion.1) | copy-start | bytes 4718596
  84.8 4.1 %copy-start.26 = (bf16[1024,512]{1,0:T(8,128)(2,1)S(1)}, bf16[1024,512]{1,0:T(8,128)(2,1)}, u32[]{:S(2)}) copy-start(bf16[1024,512]{1,0:T(8,128)(2,1)} %fusion.11) | copy-start | bytes 3145732
  87.0 4.1 %copy-start.3 = (f32[4,286,512]{2,1,0:T(8,128)}, f32[4,286,512]{2,1,0:T(8,128)S(1)}, u32[]{:S(2)}) copy-start(f32[4,286,512]{2,1,0:T(8,128)S(1)} %fusion.1) | copy-start | bytes 7028740
  87.0 87.3 %collective-permute-start.4 = (f32[4,15,512]{2,1,0:T(8,128)S(1)}, f32[4,15,512]{2,1,0:T(8,128)S(1)}, u32[]{:S(2)}, u32[]{:S(2)}) collective-permute-start(f32[4,15,512]{2,1,0:T(8,128)S(1)} %get-tuple-element.38), channel_id=1, source_target_pairs={{1,0},{2,1},{3,2},{4,3},{5,4},{6,5},{7,6},{9,8},{10,9},{11,10},{12... | collective-permute-start | bytes 368648 | tf_op jit(solution)/shard_map/ppermute | solution.py:187
  91.1 0.7 copy-start.17
  91.1 0.7 copy-start.19
  91.4 77.8 %copy-start.10 = (f32[512,512]{1,0:T(8,128)S(1)}, f32[512,512]{1,0:T(8,128)}, u32[]{:S(2)}) copy-start(f32[512,512]{1,0:T(8,128)} %convolution_bitcast_fusion) | copy-start | bytes 3145732
  170.2 6.0 %collective-permute-start.5 = (f32[4,15,512]{2,1,0:T(8,128)S(1)}, f32[4,15,512]{2,1,0:T(8,128)S(1)}, u32[]{:S(2)}, u32[]{:S(2)}) collective-permute-start(f32[4,15,512]{2,1,0:T(8,128)S(1)} %get-tuple-element.37), channel_id=1, source_target_pairs={{0,1},{1,2},{2,3},{3,4},{4,5},{5,6},{6,7},{8,9},{9,10},{10,11},{11... | collective-permute-start | bytes 368648 | tf_op jit(solution)/shard_map/ppermute | solution.py:187
  176.7 1.6 copy-start.28
  178.2 1.8 copy-start.24
  180.0 1.4 copy-start.5
  183.6 3.8 %copy-start.2 = (f32[3072,128]{1,0:T(8,128)S(1)}, f32[3072,128]{1,0:T(8,128)}, u32[]{:S(2)}) copy-start(f32[3072,128]{1,0:T(8,128)} %reshape_reshape.7) | copy-start | bytes 4718596
  330.0 2.5 copy-start.1

commit v2 on v1

--- a/solution.py
+++ b/solution.py
@@ -15,15 +15,10 @@
 def _coords():
     ci = lax.axis_index("clip")
     ti = lax.axis_index("tm")
-    y = ci % 4
-    x = (ci // 4) % 4
-    zh = ci // 16
-    core = ti % 2
-    zl = ti // 2
-    return ci, ti, y, x, zh, core, zl
-
-
-def _levels(rows):
+    return ci, ti, ci % 4, (ci // 4) % 4, ci // 16, ti % 2, ti // 2
+
+
+def _levels():
     ci, ti, y, x, zh, core, zl = _coords()
     z = zh * 4 + zl
 
@@ -40,14 +35,22 @@
     def at_c(v):
         return (ci, zl * 2 + v % 2)
 
-    return [("c", 2, core, at_c, 1), ("y", 4, y, at_y, 2), ("x", 4, x, at_x, 2), ("z", 8, z, at_z, 1)]
-
-
-def _kernel(rows, x_ref, o_ref, work, rbuf, send_sem, recv_sem):
-    levels = _levels(rows)
+    def at_h(v):
+        return ((v % 2) * 16 + x * 4 + y, ti)
+
+    return {
+        "c": (2, core, at_c, 1),
+        "y": (4, y, at_y, 2),
+        "x": (4, x, at_x, 2),
+        "z": (8, z, at_z, 1),
+        "h": (2, zh, at_h, 1),
+    }
+
+
+def _barrier(levels):
     barrier = pltpu.get_barrier_semaphore()
     peers = []
-    for name, n, me, nbr, ndir in levels:
+    for n, me, nbr, ndir in levels:
         peers.append(nbr(me + 1))
         if n > 2:
             peers.append(nbr(me - 1))
@@ -55,15 +58,82 @@
         pl.semaphore_signal(barrier, inc=1, device_id=p, device_id_type=MESH_ID)
     pl.semaphore_wait(barrier, len(peers))
 
+
+def _small_start(n, me, nbr, s, tbuf, toff, tsend, trecv, tsem):
+    at = toff + (me - s) % n
+    c = pltpu.make_async_remote_copy(
+        src_ref=tbuf.at[at],
+        dst_ref=tbuf.at[at],
+        send_sem=tsend.at[tsem],
+        recv_sem=trecv.at[tsem],
+        device_id=nbr(me + 1),
+        device_id_type=MESH_ID,
+    )
+    c.start()
+    return c
+
+
+def _small_sum(n, tbuf, toff):
+    acc = tbuf[toff]
+    for k in range(1, n):
+        acc = acc + tbuf[toff + k]
+    return acc
+
+
+def _small_kernel(names, t_ref, to_ref, tbuf, tsend, trecv):
+    table = _levels()
+    levels = [table[k] for k in names]
+    _barrier(levels)
+    toff = 0
+    tsem = 0
+    for li, (n, me, nbr, ndir) in enumerate(levels):
+        tbuf[toff + me] = t_ref[...] if li == 0 else to_ref[...]
+        for s in range(n - 1):
+            c = _small_start(n, me, nbr, s, tbuf, toff, tsend, trecv, tsem)
+            c.wait()
+            tsem += 1
+        to_ref[...] = _small_sum(n, tbuf, toff)
+        toff += n
+
+
+def small_sum(t, names, cid):
+    table_n = {"c": 2, "y": 4, "x": 4, "z": 8, "h": 2}
+    slots = sum(table_n[k] for k in names)
+    sems = sum(table_n[k] - 1 for k in names)
+    return pl.pallas_call(
+        functools.partial(_small_kernel, names),
+        out_shape=jax.ShapeDtypeStruct(t.shape, t.dtype),
+        in_specs=[pl.BlockSpec(memory_space=pltpu.VMEM)],
+        out_specs=pl.BlockSpec(memory_space=pltpu.VMEM),
+        scratch_shapes=[
+            pltpu.VMEM((slots,) + t.shape, t.dtype),
+            pltpu.SemaphoreType.DMA((sems,)),
+            pltpu.SemaphoreType.DMA((sems,)),
+        ],
+        compiler_params=pltpu.CompilerParams(collective_id=cid, has_side_effects=True),
+    )(t)
+
+
+BIG_LEVELS = ("c", "y", "x", "z")
+
+
+def _kernel(rows, x_ref, t_ref, o_ref, to_ref, work, rbuf, send_sem, recv_sem, tbuf, tsend, trecv):
+    table = _levels()
+    levels = [table[k] for k in BIG_LEVELS]
+    _barrier(levels)
+
     base = 0
     size = rows
     slot = 0
     sem = 0
+    toff = 0
+    tsem = 0
     plan = []
-    for li, (name, n, me, nbr, ndir) in enumerate(levels):
+    for li, (n, me, nbr, ndir) in enumerate(levels):
         chunk = size // n
         piece = chunk // ndir
         own = x_ref if li == 0 else work
+        tbuf[toff + me] = t_ref[...] if li == 0 else to_ref[...]
 
         def pos(k, d, base=base, chunk=chunk, piece=piece):
             return pl.multiple_of(base + k * chunk + d * piece, 8)
@@ -87,19 +157,24 @@
                 copies.append((c, slot, recv_k, d))
                 slot += piece
                 sem += 1
+            tc = _small_start(n, me, nbr, s, tbuf, toff, tsend, trecv, tsem)
+            tsem += 1
             for c, sl, recv_k, d in copies:
                 c.wait_recv()
                 at = pl.ds(pos(recv_k, d), piece)
                 work[at] = rbuf[pl.ds(sl, piece)] + own[at]
             for c, sl, recv_k, d in copies:
                 c.wait_send()
-        plan.append((name, n, me, nbr, ndir, base, chunk, piece))
+            tc.wait()
+        to_ref[...] = _small_sum(n, tbuf, toff)
+        toff += n
+        plan.append((n, me, nbr, ndir, base, chunk, piece))
         base = base + me * chunk
         size = chunk
 
     fin = pl.ds(pl.multiple_of(base, 8), size)
     o_ref[fin] = work[fin]
-    for name, n, me, nbr, ndir, lbase, chunk, piece in reversed(plan):
+    for n, me, nbr, ndir, lbase, chunk, piece in reversed(plan):
 
         def pos(k, d, base=lbase, chunk=chunk, piece=piece):
             return pl.multiple_of(base + k * chunk + d * piece, 8)
@@ -123,40 +198,49 @@
                 sem += 1
             for c in copies:
                 c.wait()
-    return None
 
 
 def _counts(rows):
     slot = 0
     sem = 0
+    tslots = 0
+    tsems = 0
     size = rows
-    for name, n, ndir in (("c", 2, 1), ("y", 4, 2), ("x", 4, 2), ("z", 8, 1)):
+    for n, ndir in ((2, 1), (4, 2), (4, 2), (8, 1)):
         chunk = size // n
         piece = chunk // ndir
         slot += piece * ndir * (n - 1)
         sem += 2 * ndir * (n - 1)
+        tslots += n
+        tsems += n - 1
         size = chunk
-    return slot, sem
-
-
-def all_sum(flat):
+    return slot, sem, tslots, tsems
+
+
+def all_sum(flat, small):
     rows = flat.shape[0]
-    slots, sems = _counts(rows)
+    slots, sems, tslots, tsems = _counts(rows)
     return pl.pallas_call(
         functools.partial(_kernel, rows),
-        out_shape=jax.ShapeDtypeStruct(flat.shape, flat.dtype),
-        in_specs=[pl.BlockSpec(memory_space=pltpu.VMEM)],
-        out_specs=pl.BlockSpec(memory_space=pltpu.VMEM),
+        out_shape=(
+            jax.ShapeDtypeStruct(flat.shape, flat.dtype),
+            jax.ShapeDtypeStruct(small.shape, small.dtype),
+        ),
+        in_specs=[pl.BlockSpec(memory_space=pltpu.VMEM)] * 2,
+        out_specs=(pl.BlockSpec(memory_space=pltpu.VMEM),) * 2,
         scratch_shapes=[
             pltpu.VMEM(flat.shape, flat.dtype),
             pltpu.VMEM((slots, flat.shape[1]), flat.dtype),
             pltpu.SemaphoreType.DMA((sems,)),
             pltpu.SemaphoreType.DMA((sems,)),
+            pltpu.VMEM((tslots,) + small.shape, small.dtype),
+            pltpu.SemaphoreType.DMA((tsems,)),
+            pltpu.SemaphoreType.DMA((tsems,)),
         ],
         compiler_params=pltpu.CompilerParams(
             collective_id=0, has_side_effects=True, vmem_limit_bytes=48 * 1024 * 1024
         ),
-    )(flat)
+    )(flat, small)
 
 
 logit_sharpening_divisor = 10.0
@@ -260,7 +344,8 @@
     cols_a, pre_a, hid_a = (flatten_rows(cols_a), flatten_rows(pre_a), flatten_rows(hid_a))
     cols_v, pre_v, hid_v = (flatten_rows(cols_v), flatten_rows(pre_v), flatten_rows(hid_v))
     count_part = jnp.sum(lengths - jnp.abs(labels))
-    count = jnp.sum(lax.all_gather(count_part, "clip")).astype(jnp.float32)
+    count_block = jnp.zeros((8, 128), jnp.int32).at[0, 0].set(count_part)
+    count = small_sum(count_block, ("y", "x", "h"), 1)[0, 0].astype(jnp.float32)
     matrix = jnp.einsum("cfe,cwe->cfw", emb_v, window, preferred_element_type=jnp.float32)
     lagged_inner_terms = narrow_band(matrix, offsets)
     inv_win = inverse_norm(window)
@@ -332,7 +417,8 @@
     grad_vc = conv_grad(cols_v, pre_v, grad_lip, w_lip_proj, w_lip_conv)
     parts = (grad_ac, grad_vc, grad_ap, grad_vp)
     flat = jnp.concatenate([g.reshape(-1, 128) for g in parts], axis=0)
-    total = all_sum(flat)
+    loss_block = jnp.zeros((8, 128), jnp.float32).at[0, 0].set(loss_local)
+    total, loss_total = all_sum(flat, loss_block)
     outs = []
     start = 0
     for g in parts:
@@ -340,7 +426,7 @@
         outs.append(total[start : start + rows].reshape(g.shape))
         start += rows
     grad_ac, grad_vc, grad_ap, grad_vp = outs
-    loss_sum = jnp.sum(lax.all_gather(loss_local, ("clip", "tm")))
+    loss_sum = loss_total[0, 0]
     return (loss_sum / count, grad_ac, grad_ap, grad_vc, grad_vp)
 
 

time: 335 us -> 266 us (0.79)
  blocking collectives: 92.2 us -> 0 us
  Pallas kernels: 130 us -> 155 us
    unnamed x2 -> x0, blocking collectives: 92.2 us -> none
    pallas_call x1 -> x2, Pallas kernels: 130 us -> 155 us  [the longest x1 133 us: all_sum(): pl.pallas_call(functools.partial(_kernel, rows), out_shape=(jax.ShapeDtyp...]
    unnamed x97 -> x92, local copies, waits for them, and re-layouts: 9.37 us -> 5.18 us
  transfers between devices with their start and end apart: 6 -> 6, of which waited for: 2 -> 1; matrix products, arithmetic and copies ran while one was open for 5% -> 7% of each run, Pallas kernels for 0% -> 8%
where the time goes in v2:
time: 266 us; the launch traced here: 265 us
  Pallas kernels  155 us (58%)
  local copies, waits for them, and re-layouts  41.5 us (16%)
  starting transfers between devices  24.1 us (9%)
  matrix products  21.8 us (8%)
  other arithmetic  18.3 us (7%)
  between operations  3.73 us (1%)
    pallas_call x1, Pallas kernels, all_sum(): pl.pallas_call(functools.partial(_kernel, rows), out_shape=(jax.ShapeDtyp...  133 us
    pallas_call x1, Pallas kernels, small_sum(): pl.pallas_call(functools.partial(_small_kernel, names), out_shape=jax.Sha...  22.5 us
    ppermute x2, starting transfers between devices, padded_2(): lax.ppermute(tail, axis, [(i, (i + 1) % count) for i in range(ends)])  14.7 us
    reshape x4, local copies, waits for them, and re-layouts, shards(): outs.append(total[start:start + rows].reshape(g.shape))  7.41 us
    concatenate x1, other arithmetic, shards(): flat = jnp.concatenate([g.reshape(-1, 128) for g in parts], axis=0)  5.72 us
    ppermute x2, starting transfers between devices, from_behind(): lax.ppermute(value, axis, [(source, source + steps) for source in range(i...  5.56 us
  transfers between devices with their start and end apart: 6, of which 1 were waited for; matrix products, arithmetic and copies ran while one was open for 7% of the time, Pallas kernels for 8%

profile of v2, /device:TPU:1, one launch (start us, length us, event | category | flops | bytes accessed | tf_op | source)
XLA Modules:
  0.0 265.1 jit_solution(5025774828138966974)
XLA Ops:
  0.6 0.9 pad_maximum_fusion.6
  1.5 4.9 %collective-permute-start = (bf16[2,4,1,256]{3,2,1,0:T(2,128)(2,1)S(1)}, bf16[2,4,1,256]{3,2,1,0:T(2,128)(2,1)S(1)}, u32[]{:S(2)}, u32[]{:S(2)}) collective-permute-start(bf16[2,4,1,256]{3,2,1,0:T(2,128)(2,1)S(1)} %get-tuple-element.73), channel_id=1, source_target_pairs={{0,1},{1,2},{2,3},{3,4},{4,5},{5,6},{6,7},{8,9},{9,10},{10,11},{11... | collective-permute-start | bytes 12296 | tf_op jit(solution)/shard_map/ppermute | solution.py:259
  6.5 1.9 collective-permute-start.1
  8.6 0.7 broadcast_compare_fusion.1
  9.4 0.7 compare_convert_fusion
  10.1 1.3 subtract_reduce_fusion
  11.4 1.2 scatter.6.t_ref
  12.6 22.5 %shard_map.119 = s32[8,128]{1,0:T(8,128)} custom-call(s32[8,128]{1,0:T(8,128)} %scatter.6.t_ref), custom_call_target="tpu_custom_call" | custom-call | tf_op jit(solution)/shard_map/pallas_call | solution.py:103
  35.2 1.2 slice.252
  37.1 1.5 pad_maximum_fusion.4
  38.6 0.6 fusion.33
  39.2 1.3 pad_maximum_fusion.1
  40.5 1.0 fusion.28
  41.5 0.7 convolution_convert_fusion
  42.3 0.6 copy-done.27
  42.9 9.8 %collective-permute-start.2 = (bf16[4,15,512]{2,1,0:T(8,128)(2,1)S(1)}, bf16[4,15,512]{2,1,0:T(8,128)(2,1)S(1)}, u32[]{:S(2)}, u32[]{:S(2)}) collective-permute-start(bf16[4,15,512]{2,1,0:T(8,128)(2,1)S(1)} %get-tuple-element.71), channel_id=1, source_target_pairs={{0,1},{1,2},{2,3},{3,4},{4,5},{5,6},{6,7},{8,9},{9,10},{10,11},{11... | collective-permute-start | bytes 184328 | tf_op jit(solution)/shard_map/ppermute | solution.py:259
  52.7 1.9 collective-permute-start.3
  54.7 1.0 fusion.27
  55.7 1.8 fusion.2
  57.5 1.2 pad_maximum_fusion.2
  58.7 0.5 fusion
  61.6 0.3 copy.1102
  61.9 1.9 fusion.26
  63.8 2.9 %reshape.436 = f32[4,73216]{1,0:T(4,128)S(1)} reshape(f32[4,256,286]{2,1,0:T(8,128)} %fusion.26) | data formatting | bytes 2342912 | tf_op jit(solution)/shard_map/reshape | solution.py:312
  66.9 1.5 reshape.437
  68.4 0.5 fusion.21
  69.0 1.7 multiply_reduce_fusion
  70.9 1.2 reshape.438
  72.3 1.7 reshape.439
  74.1 2.1 fusion.4
  76.2 1.8 convolution_bitcast_fusion
  78.0 2.2 fusion.11
  80.3 1.4 reshape.440
  81.8 1.1 slice.346
  82.8 3.1 %reshape.441 = f32[4,256,286]{2,1,0:T(8,128)S(1)} reshape(f32[4,73216]{1,0:T(4,128)} %slice.346) | data formatting | bytes 2342912 | tf_op jit(solution)/shard_map/reshape | solution.py:307
  86.1 2.1 fusion.1
  88.3 1.9 collective-permute-start.4
  90.2 2.1 fusion.36
  92.4 0.2 slice.347
  92.7 0.4 copy-done.17
  93.1 0.7 select_reduce_fusion
  93.7 0.6 scatter.9.t_ref
  94.4 2.4 reshape_reshape.7
  96.8 1.0 reshape.448
  97.9 3.6 %collective-permute-start.5 = (f32[4,15,512]{2,1,0:T(8,128)S(1)}, f32[4,15,512]{2,1,0:T(8,128)S(1)}, u32[]{:S(2)}, u32[]{:S(2)}) collective-permute-start(f32[4,15,512]{2,1,0:T(8,128)S(1)} %get-tuple-element.65), channel_id=1, source_target_pairs={{0,1},{1,2},{2,3},{3,4},{4,5},{5,6},{6,7},{8,9},{9,10},{10,11},{11... | collective-permute-start | bytes 368648 | tf_op jit(solution)/shard_map/ppermute | solution.py:271
  101.5 0.9 slice_add_fusion.1
  102.5 0.5 scatter-add.6
  103.0 0.5 collective-permute-done.5
  103.5 0.4 scatter-add.9
  104.0 1.4 copy-done.28
  105.5 1.7 convolution_bitcast_fusion.1
  107.2 1.2 fusion.18
  108.6 2.1 fusion.35
  110.8 1.5 reshape_reshape.6
  112.3 2.3 reshape.447
  114.6 5.7 %pad_maximum_fusion.x_ref = f32[10240,128]{1,0:T(8,128)} fusion(f32[2048,128]{1,0:T(8,128)} %reshape.448, f32[2048,128]{1,0:T(8,128)} %reshape.447, f32[3072,128]{1,0:T(8,128)S(1)} %copy-done.2, f32[3072,128]{1,0:T(8,128)S(1)} %reshape_reshape.6), kind=kLoop, calls=%fused_computation | loop fusion | flops 3932160 | bytes 10485760 | tf_op jit(solution)/shard_map/concatenate | solution.py:419
  120.3 132.7 %shard_map.120 = (f32[10240,128]{1,0:T(8,128)S(1)}, f32[8,128]{1,0:T(8,128)S(1)}) custom-call(f32[10240,128]{1,0:T(8,128)} %pad_maximum_fusion.x_ref, f32[8,128]{1,0:T(8,128)S(1)} %scatter.9.t_ref), custom_call_target="tpu_custom_call" | custom-call | tf_op jit(solution)/shard_map/pallas_call | solution.py:223
  253.0 1.1 fusion.29
  254.1 1.3 fusion.30
  255.4 0.5 slice.298
  256.6 2.6 reshape.452
  259.1 2.4 reshape.453
  261.5 1.1 reshape.451
  262.6 1.4 reshape.450
  (114 shorter events, 4.2 us)
Async XLA Ops:
  0.6 39.9 %copy-start = (bf16[3,256,512]{2,1,0:T(8,128)(2,1)S(1)}, bf16[3,256,512]{2,1,0:T(8,128)(2,1)}, u32[]{:S(2)}) copy-start(bf16[3,256,512]{2,1,0:T(8,128)(2,1)} %param.20) | copy-start | bytes 2359300
  1.5 35.5 %collective-permute-start = (bf16[2,4,1,256]{3,2,1,0:T(2,128)(2,1)S(1)}, bf16[2,4,1,256]{3,2,1,0:T(2,128)(2,1)S(1)}, u32[]{:S(2)}, u32[]{:S(2)}) collective-permute-start(bf16[2,4,1,256]{3,2,1,0:T(2,128)(2,1)S(1)} %get-tuple-element.73), channel_id=1, source_target_pairs={{0,1},{1,2},{2,3},{3,4},{4,5},{5,6},{6,7},{8,9},{9,10},{10,11},{11... | collective-permute-start | bytes 12296 | tf_op jit(solution)/shard_map/ppermute | solution.py:259
  6.5 30.6 %collective-permute-start.1 = (bf16[2,4,1,256]{3,2,1,0:T(2,128)(2,1)S(1)}, bf16[2,4,1,256]{3,2,1,0:T(2,128)(2,1)S(1)}, u32[]{:S(2)}, u32[]{:S(2)}) collective-permute-start(bf16[2,4,1,256]{3,2,1,0:T(2,128)(2,1)S(1)} %get-tuple-element.74), channel_id=1, source_target_pairs={{1,0},{2,1},{3,2},{4,3},{5,4},{6,5},{7,6},{9,8},{10,9},{11,10},{12... | collective-permute-start | bytes 12296 | tf_op jit(solution)/shard_map/ppermute | solution.py:261
  40.5 1.0 copy-start.23
  41.5 1.3 copy-start.27
  41.5 13.1 %copy-start.20 = (bf16[3,256,512]{2,1,0:T(8,128)(2,1)S(1)}, bf16[3,256,512]{2,1,0:T(8,128)(2,1)}, u32[]{:S(2)}) copy-start(bf16[3,256,512]{2,1,0:T(8,128)(2,1)} %param.22) | copy-start | bytes 2359300
  42.9 19.0 %copy-start.7 = (bf16[4,256,512]{2,1,0:T(8,128)(2,1)}, bf16[4,256,512]{2,1,0:T(8,128)(2,1)S(1)}, u32[]{:S(2)}) copy-start(bf16[4,256,512]{2,1,0:T(8,128)(2,1)S(1)} %convolution_convert_fusion) | copy-start | bytes 3145732
  42.9 15.8 %collective-permute-start.2 = (bf16[4,15,512]{2,1,0:T(8,128)(2,1)S(1)}, bf16[4,15,512]{2,1,0:T(8,128)(2,1)S(1)}, u32[]{:S(2)}, u32[]{:S(2)}) collective-permute-start(bf16[4,15,512]{2,1,0:T(8,128)(2,1)S(1)} %get-tuple-element.71), channel_id=1, source_target_pairs={{0,1},{1,2},{2,3},{3,4},{4,5},{5,6},{6,7},{8,9},{9,10},{10,11},{11... | collective-permute-start | bytes 184328 | tf_op jit(solution)/shard_map/ppermute | solution.py:259
  52.7 6.0 %collective-permute-start.3 = (bf16[4,15,512]{2,1,0:T(8,128)(2,1)S(1)}, bf16[4,15,512]{2,1,0:T(8,128)(2,1)S(1)}, u32[]{:S(2)}, u32[]{:S(2)}) collective-permute-start(bf16[4,15,512]{2,1,0:T(8,128)(2,1)S(1)} %get-tuple-element.72), channel_id=1, source_target_pairs={{1,0},{2,1},{3,2},{4,3},{5,4},{6,5},{7,6},{9,8},{10,9},{11,10},{12... | collective-permute-start | bytes 184328 | tf_op jit(solution)/shard_map/ppermute | solution.py:261
  54.6 1.0 copy-start.21
  55.7 1.8 copy-start.29
  57.5 4.4 %copy-start.25 = (bf16[4,256,512]{2,1,0:T(8,128)(2,1)S(1)}, bf16[4,256,512]{2,1,0:T(8,128)(2,1)}, u32[]{:S(2)}) copy-start(bf16[4,256,512]{2,1,0:T(8,128)(2,1)} %get-tuple-element.86) | copy-start | bytes 3145732
  58.7 3.2 %copy-start.11 = (bf16[4,15,512]{2,1,0:T(8,128)(2,1)}, bf16[4,15,512]{2,1,0:T(8,128)(2,1)S(1)}, u32[]{:S(2)}) copy-start(bf16[4,15,512]{2,1,0:T(8,128)(2,1)S(1)} %collective-permute-done.2) | copy-start | bytes 184324
  58.7 3.2 %copy-start.14 = (bf16[4,15,512]{2,1,0:T(8,128)(2,1)}, bf16[4,15,512]{2,1,0:T(8,128)(2,1)S(1)}, u32[]{:S(2)}) copy-start(bf16[4,15,512]{2,1,0:T(8,128)(2,1)S(1)} %collective-permute-done.3) | copy-start | bytes 184324
  66.7 1.7 copy-start.16
  66.9 2.1 copy-start.18
  70.9 3.1 %copy-start.8 = (bf16[4,256,512]{2,1,0:T(8,128)(2,1)S(1)}, bf16[4,256,512]{2,1,0:T(8,128)(2,1)}, u32[]{:S(2)}) copy-start(bf16[4,256,512]{2,1,0:T(8,128)(2,1)} %copy-done.7) | copy-start | bytes 3145732
  70.9 3.1 %copy-start.12 = (bf16[4,15,512]{2,1,0:T(8,128)(2,1)S(1)}, bf16[4,15,512]{2,1,0:T(8,128)(2,1)}, u32[]{:S(2)}) copy-start(bf16[4,15,512]{2,1,0:T(8,128)(2,1)} %copy-done.11) | copy-start | bytes 184324
  70.9 3.1 %copy-start.15 = (bf16[4,15,512]{2,1,0:T(8,128)(2,1)S(1)}, bf16[4,15,512]{2,1,0:T(8,128)(2,1)}, u32[]{:S(2)}) copy-start(bf16[4,15,512]{2,1,0:T(8,128)(2,1)} %copy-done.14) | copy-start | bytes 184324
  74.1 2.2 copy-start.30
  76.2 1.8 copy-start.22
  78.0 2.2 copy-start.4
  82.8 3.2 %copy-start.9 = (bf16[4,256,512]{2,1,0:T(8,128)(2,1)S(1)}, bf16[4,256,512]{2,1,0:T(8,128)(2,1)}, u32[]{:S(2)}) copy-start(bf16[4,256,512]{2,1,0:T(8,128)(2,1)} %copy-done.7) | copy-start | bytes 3145732
  82.8 3.2 %copy-start.13 = (bf16[4,15,512]{2,1,0:T(8,128)(2,1)S(1)}, bf16[4,15,512]{2,1,0:T(8,128)(2,1)}, u32[]{:S(2)}) copy-start(bf16[4,15,512]{2,1,0:T(8,128)(2,1)} %copy-done.11) | copy-start | bytes 184324
  86.1 4.1 %copy-start.6 = (bf16[4,256,768]{2,1,0:T(8,128)(2,1)S(1)}, bf16[4,256,768]{2,1,0:T(8,128)(2,1)}, u32[]{:S(2)}) copy-start(bf16[4,256,768]{2,1,0:T(8,128)(2,1)} %pad_maximum_fusion.2) | copy-start | bytes 4718596
  86.1 4.1 %copy-start.26 = (bf16[1024,512]{1,0:T(8,128)(2,1)S(1)}, bf16[1024,512]{1,0:T(8,128)(2,1)}, u32[]{:S(2)}) copy-start(bf16[1024,512]{1,0:T(8,128)(2,1)} %fusion.11) | copy-start | bytes 3145732
  88.3 4.1 %copy-start.3 = (f32[4,286,512]{2,1,0:T(8,128)}, f32[4,286,512]{2,1,0:T(8,128)S(1)}, u32[]{:S(2)}) copy-start(f32[4,286,512]{2,1,0:T(8,128)S(1)} %fusion.1) | copy-start | bytes 7028740
  88.3 13.2 %collective-permute-start.4 = (f32[4,15,512]{2,1,0:T(8,128)S(1)}, f32[4,15,512]{2,1,0:T(8,128)S(1)}, u32[]{:S(2)}, u32[]{:S(2)}) collective-permute-start(f32[4,15,512]{2,1,0:T(8,128)S(1)} %get-tuple-element.66), channel_id=1, source_target_pairs={{1,0},{2,1},{3,2},{4,3},{5,4},{6,5},{7,6},{9,8},{10,9},{11,10},{12... | collective-permute-start | bytes 368648 | tf_op jit(solution)/shard_map/ppermute | solution.py:271
  92.4 0.7 copy-start.17
  92.4 0.7 copy-start.19
  92.7 4.2 %copy-start.10 = (f32[512,512]{1,0:T(8,128)S(1)}, f32[512,512]{1,0:T(8,128)}, u32[]{:S(2)}) copy-start(f32[512,512]{1,0:T(8,128)} %convolution_bitcast_fusion) | copy-start | bytes 3145732
  97.9 5.6 %collective-permute-start.5 = (f32[4,15,512]{2,1,0:T(8,128)S(1)}, f32[4,15,512]{2,1,0:T(8,128)S(1)}, u32[]{:S(2)}, u32[]{:S(2)}) collective-permute-start(f32[4,15,512]{2,1,0:T(8,128)S(1)} %get-tuple-element.65), channel_id=1, source_target_pairs={{0,1},{1,2},{2,3},{3,4},{4,5},{5,6},{6,7},{8,9},{9,10},{10,11},{11... | collective-permute-start | bytes 368648 | tf_op jit(solution)/shard_map/ppermute | solution.py:271
  103.9 1.6 copy-start.28
  105.5 1.8 copy-start.24
  107.2 1.4 copy-start.5
  110.8 3.8 %copy-start.2 = (f32[3072,128]{1,0:T(8,128)S(1)}, f32[3072,128]{1,0:T(8,128)}, u32[]{:S(2)}) copy-start(f32[3072,128]{1,0:T(8,128)} %reshape_reshape.7) | copy-start | bytes 4718596
  261.5 2.5 copy-start.1

commit v3 on v2

--- a/solution.py
+++ b/solution.py
@@ -114,39 +114,20 @@
     )(t)
 
 
-BIG_LEVELS = ("c", "y", "x", "z")
-
-
-def _kernel(rows, x_ref, t_ref, o_ref, to_ref, work, rbuf, send_sem, recv_sem, tbuf, tsend, trecv):
-    table = _levels()
-    levels = [table[k] for k in BIG_LEVELS]
-    _barrier(levels)
-
-    base = 0
-    size = rows
-    slot = 0
-    sem = 0
-    toff = 0
-    tsem = 0
-    plan = []
-    for li, (n, me, nbr, ndir) in enumerate(levels):
-        chunk = size // n
-        piece = chunk // ndir
-        own = x_ref if li == 0 else work
-        tbuf[toff + me] = t_ref[...] if li == 0 else to_ref[...]
-
-        def pos(k, d, base=base, chunk=chunk, piece=piece):
-            return pl.multiple_of(base + k * chunk + d * piece, 8)
-
-        for s in range(n - 1):
-            copies = []
+def _rs_stage(tasks, work, rbuf, send_sem, recv_sem, slot, sem, rider=None):
+    n = tasks[0][0]
+    for s in range(n - 1):
+        copies = []
+        for tn, me, nbr, ndir, base, size, own in tasks:
+            chunk = size // tn
+            piece = chunk // ndir
             for d in range(ndir):
                 sign = 1 if d == 0 else -1
-                send_k = (me - sign * (s + 1)) % n
-                recv_k = (me - sign * (s + 2)) % n
+                send_at = pl.multiple_of(base + ((me - sign * (s + 1)) % tn) * chunk + d * piece, 8)
+                recv_at = pl.multiple_of(base + ((me - sign * (s + 2)) % tn) * chunk + d * piece, 8)
                 src = own if s == 0 else work
                 c = pltpu.make_async_remote_copy(
-                    src_ref=src.at[pl.ds(pos(send_k, d), piece)],
+                    src_ref=src.at[pl.ds(send_at, piece)],
                     dst_ref=rbuf.at[pl.ds(slot, piece)],
                     send_sem=send_sem.at[sem],
                     recv_sem=recv_sem.at[sem],
@@ -154,37 +135,31 @@
                     device_id_type=MESH_ID,
                 )
                 c.start()
-                copies.append((c, slot, recv_k, d))
+                copies.append((c, slot, recv_at, piece, own))
                 slot += piece
                 sem += 1
-            tc = _small_start(n, me, nbr, s, tbuf, toff, tsend, trecv, tsem)
-            tsem += 1
-            for c, sl, recv_k, d in copies:
-                c.wait_recv()
-                at = pl.ds(pos(recv_k, d), piece)
-                work[at] = rbuf[pl.ds(sl, piece)] + own[at]
-            for c, sl, recv_k, d in copies:
-                c.wait_send()
-            tc.wait()
-        to_ref[...] = _small_sum(n, tbuf, toff)
-        toff += n
-        plan.append((n, me, nbr, ndir, base, chunk, piece))
-        base = base + me * chunk
-        size = chunk
-
-    fin = pl.ds(pl.multiple_of(base, 8), size)
-    o_ref[fin] = work[fin]
-    for n, me, nbr, ndir, lbase, chunk, piece in reversed(plan):
-
-        def pos(k, d, base=lbase, chunk=chunk, piece=piece):
-            return pl.multiple_of(base + k * chunk + d * piece, 8)
-
-        for s in range(n - 1):
-            copies = []
+        ride = rider(s) if rider is not None else None
+        for c, sl, recv_at, piece, own in copies:
+            c.wait_recv()
+            at = pl.ds(recv_at, piece)
+            work[at] = rbuf[pl.ds(sl, piece)] + own[at]
+        for c, sl, recv_at, piece, own in copies:
+            c.wait_send()
+        if ride is not None:
+            ride.wait()
+    return slot, sem
+
+
+def _ag_stage(tasks, o_ref, send_sem, recv_sem, sem):
+    n = tasks[0][0]
+    for s in range(n - 1):
+        copies = []
+        for tn, me, nbr, ndir, base, size, own in tasks:
+            chunk = size // tn
+            piece = chunk // ndir
             for d in range(ndir):
                 sign = 1 if d == 0 else -1
-                send_k = (me - sign * s) % n
-                at = pl.ds(pos(send_k, d), piece)
+                at = pl.ds(pl.multiple_of(base + ((me - sign * s) % tn) * chunk + d * piece, 8), piece)
                 c = pltpu.make_async_remote_copy(
                     src_ref=o_ref.at[at],
                     dst_ref=o_ref.at[at],
@@ -196,30 +171,119 @@
                 c.start()
                 copies.append(c)
                 sem += 1
-            for c in copies:
-                c.wait()
+        for c in copies:
+            c.wait()
+    return sem
+
+
+def _pass_copy(buf, at, nbr, target, sems, idx):
+    c = pltpu.make_async_remote_copy(
+        src_ref=buf.at[at],
+        dst_ref=buf.at[at],
+        send_sem=sems[0].at[idx],
+        recv_sem=sems[1].at[idx],
+        device_id=nbr(target),
+        device_id_type=MESH_ID,
+    )
+    c.start()
+    return c
+
+
+def _kernel(rows, x_ref, t_ref, o_ref, to_ref, work, rbuf, zbuf, send_sem, recv_sem, tbuf, tsend, trecv):
+    table = _levels()
+    lc, ly, lx, lz = (table[k] for k in ("c", "y", "x", "z"))
+    _barrier([lc, ly, lx, lz])
+    tsems = (tsend, trecv)
+    state = {"toff": 0, "tsem": 0}
+
+    def tiny_level(level, first):
+        n, me, nbr, ndir = level
+        toff = state["toff"]
+        tbuf[toff + me] = t_ref[...] if first else to_ref[...]
+
+        def rider(s):
+            c = _pass_copy(tbuf, toff + (me - s) % n, nbr, me + 1, tsems, state["tsem"])
+            state["tsem"] += 1
+            return c
+
+        return rider
+
+    def tiny_done(n):
+        to_ref[...] = _small_sum(n, tbuf, state["toff"])
+        state["toff"] += n
+
+    slot, sem = 0, 0
+    half = rows // 2
+    quarter = rows // 4
+    nc, core, nbc, _ = lc
+    ny, yi, nby, _ = ly
+    nx, xi, nbx, _ = lx
+    nz, zi, nbz, _ = lz
+
+    rider = tiny_level(lc, True)
+    slot, sem = _rs_stage([(nc, core, nbc, 1, 0, rows, x_ref)], work, rbuf, send_sem, recv_sem, slot, sem, rider)
+    tiny_done(nc)
+    r0 = core * half
+    a1, b1 = r0, r0 + quarter
+    rider = tiny_level(ly, False)
+    slot, sem = _rs_stage(
+        [(ny, yi, nby, 2, a1, quarter, work), (nx, xi, nbx, 2, b1, quarter, work)],
+        work, rbuf, send_sem, recv_sem, slot, sem, rider,
+    )
+    tiny_done(ny)
+    c1 = quarter // 4
+    a2, b2 = a1 + yi * c1, b1 + xi * c1
+    rider = tiny_level(lx, False)
+    slot, sem = _rs_stage(
+        [(nx, xi, nbx, 1, a2, c1, work), (ny, yi, nby, 1, b2, c1, work)],
+        work, rbuf, send_sem, recv_sem, slot, sem, rider,
+    )
+    tiny_done(nx)
+    c2 = c1 // 4
+    a3, b3 = a2 + xi * c2, b2 + yi * c2
+    zbuf[zi, 0] = work[pl.ds(pl.multiple_of(a3, 8), c2)]
+    zbuf[zi, 1] = work[pl.ds(pl.multiple_of(b3, 8), c2)]
+    toff = state["toff"]
+    tbuf[toff + zi] = to_ref[...]
+    right = nz // 2
+    left = nz - 1 - right
+    for s in range(right):
+        cs = [
+            _pass_copy(zbuf, (zi - s) % nz, nbz, zi + 1, (send_sem, recv_sem), sem),
+            _pass_copy(tbuf, toff + (zi - s) % nz, nbz, zi + 1, tsems, state["tsem"]),
+        ]
+        sem += 1
+        state["tsem"] += 1
+        if s < left:
+            cs.append(_pass_copy(zbuf, (zi + s) % nz, nbz, zi - 1, (send_sem, recv_sem), sem))
+            cs.append(_pass_copy(tbuf, toff + (zi + s) % nz, nbz, zi - 1, tsems, state["tsem"]))
+            sem += 1
+            state["tsem"] += 1
+        for c in cs:
+            c.wait()
+    for colour, at in ((0, a3), (1, b3)):
+        acc = zbuf[0, colour]
+        for k in range(1, nz):
+            acc = acc + zbuf[k, colour]
+        o_ref[pl.ds(pl.multiple_of(at, 8), c2)] = acc
+    tiny_done(nz)
+    sem = _ag_stage([(nx, xi, nbx, 1, a2, c1, None), (ny, yi, nby, 1, b2, c1, None)], o_ref, send_sem, recv_sem, sem)
+    sem = _ag_stage([(ny, yi, nby, 2, a1, quarter, None), (nx, xi, nbx, 2, b1, quarter, None)], o_ref, send_sem, recv_sem, sem)
+    sem = _ag_stage([(nc, core, nbc, 1, 0, rows, None)], o_ref, send_sem, recv_sem, sem)
 
 
 def _counts(rows):
-    slot = 0
-    sem = 0
-    tslots = 0
-    tsems = 0
-    size = rows
-    for n, ndir in ((2, 1), (4, 2), (4, 2), (8, 1)):
-        chunk = size // n
-        piece = chunk // ndir
-        slot += piece * ndir * (n - 1)
-        sem += 2 * ndir * (n - 1)
-        tslots += n
-        tsems += n - 1
-        size = chunk
-    return slot, sem, tslots, tsems
+    half, quarter = rows // 2, rows // 4
+    c1 = quarter // 4
+    slots = half + 3 * 2 * quarter // 4 + 3 * 2 * c1 // 4
+    sems = 1 + 3 * 4 + 3 * 2 + 7 + 3 * 2 + 3 * 4 + 1
+    return slots, sems, 2 + 4 + 4 + 8, 1 + 3 + 3 + 7
 
 
 def all_sum(flat, small):
     rows = flat.shape[0]
     slots, sems, tslots, tsems = _counts(rows)
+    c2 = rows // 64
     return pl.pallas_call(
         functools.partial(_kernel, rows),
         out_shape=(
@@ -231,6 +295,7 @@
         scratch_shapes=[
             pltpu.VMEM(flat.shape, flat.dtype),
             pltpu.VMEM((slots, flat.shape[1]), flat.dtype),
+            pltpu.VMEM((8, 2, c2, flat.shape[1]), flat.dtype),
             pltpu.SemaphoreType.DMA((sems,)),
             pltpu.SemaphoreType.DMA((sems,)),
             pltpu.VMEM((tslots,) + small.shape, small.dtype),
@@ -416,13 +481,14 @@
     grad_ac = conv_grad(cols_a, pre_a, grad_audio, w_audio_proj, w_audio_conv)
     grad_vc = conv_grad(cols_v, pre_v, grad_lip, w_lip_proj, w_lip_conv)
     parts = (grad_ac, grad_vc, grad_ap, grad_vp)
-    flat = jnp.concatenate([g.reshape(-1, 128) for g in parts], axis=0)
+    lanes = grad_ap.shape[1]
+    flat = jnp.concatenate([g.reshape(-1, lanes) for g in parts], axis=0)
     loss_block = jnp.zeros((8, 128), jnp.float32).at[0, 0].set(loss_local)
     total, loss_total = all_sum(flat, loss_block)
     outs = []
     start = 0
     for g in parts:
-        rows = g.size // 128
+        rows = g.size // lanes
         outs.append(total[start : start + rows].reshape(g.shape))
         start += rows
     grad_ac, grad_vc, grad_ap, grad_vp = outs

time: 266 us -> 221 us (0.83)
  Pallas kernels: 155 us -> 122 us
  local copies, waits for them, and re-layouts: 41.5 us -> 30.8 us
    pallas_call x1, Pallas kernels: 133 us -> 99.2 us  [all_sum(): pl.pallas_call(functools.partial(_kernel, rows), out_shape=(jax.ShapeDtyp...]
    reshape x6 -> x0, local copies, waits for them, and re-layouts: 10.7 us -> none  [the longest x4 7.41 us: shards(): outs.append(total[start:start + rows].reshape(g.shape))]
    another operation x2 -> x0, local copies, waits for them, and re-layouts: 3.97 us -> none  [shards(): flat = jnp.concatenate([g.reshape(-1, 128) for g in parts], axis=0)]
    concatenate x1, other arithmetic: 5.72 us -> 2.69 us  [shards(): flat = jnp.concatenate([g.reshape(-1, lanes) for g in parts], axis=0)]
    unnamed x92 -> x84, local copies, waits for them, and re-layouts: 5.18 us -> 6.11 us
  transfers between devices with their start and end apart: 6 -> 6, of which waited for: 1 -> 1; matrix products, arithmetic and copies ran while one was open for 7% -> 6% of each run, Pallas kernels for 8% -> 10%
where the time goes in v3:
time: 221 us; the launch traced here: 220 us
  Pallas kernels  122 us (55%)
  local copies, waits for them, and re-layouts  30.8 us (14%)
  starting transfers between devices  24.2 us (11%)
  matrix products  20.7 us (9%)
  other arithmetic  17.6 us (8%)
  between operations  3.64 us (2%)
    pallas_call x1, Pallas kernels, all_sum(): pl.pallas_call(functools.partial(_kernel, rows), out_shape=(jax.ShapeDtyp...  99.2 us
    pallas_call x1, Pallas kernels, small_sum(): pl.pallas_call(functools.partial(_small_kernel, names), out_shape=jax.Sha...  22.5 us
    ppermute x2, starting transfers between devices, padded_2(): lax.ppermute(tail, axis, [(i, (i + 1) % count) for i in range(ends)])  14.7 us
    unnamed x84, local copies, waits for them, and re-layouts  6.11 us
    ppermute x2, starting transfers between devices, from_behind(): lax.ppermute(value, axis, [(source, source + steps) for source in range(i...  5.57 us
    reshape x2, local copies, waits for them, and re-layouts, spread_band(): return flat_band.reshape(clip_num, row_num, wide_len)  4.77 us
  transfers between devices with their start and end apart: 6, of which 1 were waited for; matrix products, arithmetic and copies ran while one was open for 6% of the time, Pallas kernels for 10%

profile of v3, /device:TPU:1, one launch (start us, length us, event | category | flops | bytes accessed | tf_op | source)
XLA Modules:
  0.0 220.1 jit_solution(7255579968755248926)
XLA Ops:
  0.6 0.9 pad_maximum_fusion.6
  1.5 4.9 %collective-permute-start = (bf16[2,4,1,256]{3,2,1,0:T(2,128)(2,1)S(1)}, bf16[2,4,1,256]{3,2,1,0:T(2,128)(2,1)S(1)}, u32[]{:S(2)}, u32[]{:S(2)}) collective-permute-start(bf16[2,4,1,256]{3,2,1,0:T(2,128)(2,1)S(1)} %get-tuple-element.73), channel_id=1, source_target_pairs={{0,1},{1,2},{2,3},{3,4},{4,5},{5,6},{6,7},{8,9},{9,10},{10,11},{11... | collective-permute-start | bytes 12296 | tf_op jit(solution)/shard_map/ppermute | solution.py:324
  6.5 1.9 collective-permute-start.1
  8.6 0.7 broadcast_compare_fusion.1
  9.4 0.7 compare_convert_fusion
  10.1 1.3 subtract_reduce_fusion
  11.4 1.2 scatter.6.t_ref
  12.6 22.5 %shard_map.119 = s32[8,128]{1,0:T(8,128)} custom-call(s32[8,128]{1,0:T(8,128)} %scatter.6.t_ref), custom_call_target="tpu_custom_call" | custom-call | tf_op jit(solution)/shard_map/pallas_call | solution.py:103
  35.1 1.2 slice.252
  37.0 1.5 pad_maximum_fusion.4
  38.6 0.6 fusion.33
  39.2 1.3 pad_maximum_fusion.1
  40.5 1.0 fusion.28
  41.6 0.7 convolution_convert_fusion
  42.3 0.6 copy-done.23
  42.9 9.8 %collective-permute-start.2 = (bf16[4,15,512]{2,1,0:T(8,128)(2,1)S(1)}, bf16[4,15,512]{2,1,0:T(8,128)(2,1)S(1)}, u32[]{:S(2)}, u32[]{:S(2)}) collective-permute-start(bf16[4,15,512]{2,1,0:T(8,128)(2,1)S(1)} %get-tuple-element.71), channel_id=1, source_target_pairs={{0,1},{1,2},{2,3},{3,4},{4,5},{5,6},{6,7},{8,9},{9,10},{10,11},{11... | collective-permute-start | bytes 184328 | tf_op jit(solution)/shard_map/ppermute | solution.py:324
  52.7 1.9 collective-permute-start.3
  54.7 1.0 fusion.27
  55.7 1.8 fusion.2
  57.5 1.2 pad_maximum_fusion.2
  58.8 0.5 fusion
  61.6 0.3 copy.1102
  61.9 2.3 %fusion.26 = f32[4,256,286]{2,1,0:T(8,128)S(1)} fusion(bf16[4,256,512]{2,1,0:T(8,128)(2,1)} %get-tuple-element.86, bf16[4,15,512]{2,1,0:T(8,128)(2,1)S(1)} %collective-permute-done.3, bf16[4,256,512]{2,1,0:T(8,128)(2,1)} %copy-done.4, bf16[4,15,512]{2,1,0:T(8,128)(2,1)S(1)} %collective-permute-done.2), kind=kOutput, calls=%fused_computation.138 | convolution fusion | flops 303407104 | bytes 3391488 | tf_op jit(solution)/shard_map/cfe,cwe->cfw/dot_general | solution.py:414
  64.1 2.5 %reshape.424 = f32[4,73216]{1,0:T(4,128)} reshape(f32[4,256,286]{2,1,0:T(8,128)S(1)} %fusion.26) | data formatting | bytes 2342912 | tf_op jit(solution)/shard_map/reshape | solution.py:377
  66.7 1.5 pad.27
  68.2 2.6 %reshape.425 = f32[4,256,287]{2,1,0:T(8,128)} reshape(f32[4,73472]{1,0:T(4,128)S(1)} %pad.27) | data formatting | bytes 2351104 | tf_op jit(solution)/shard_map/reshape | solution.py:378
  70.8 1.6 fusion.21
  72.5 2.7 %multiply_reduce_fusion = (f32[4,256]{1,0:T(4,128)}, f32[4,256]{1,0:T(4,128)S(1)}, f32[4,256,31]{2,1,0:T(8,128)S(1)}, bf16[4,256,31]{2,1,0:T(8,128)(2,1)S(1)}) fusion(f32[4,256,31]{2,1,0:T(8,128)S(1)} %get-tuple-element.60, f32[4,31]{1,0:T(4,128)S(1)} %compare_convert_fusion, f32[4,256,31]{2,1,0:T(8,128)S(1)} %copy.1102, f32[4,256,287]{2,1,0:T(8,128)} %reshape.425, ...), kind=kLoop, calls=%fused_computation.42 | loop fusion | flops 505856 | bytes 633088 | tf_op jit(solution)/shard_map/reduce_sum | solution.py:437
  75.3 1.2 reshape.426
  76.5 0.2 slice.345
  76.7 1.7 reshape.427
  78.4 2.6 %fusion.4 = bf16[4,256,512]{2,1,0:T(8,128)(2,1)S(1)} fusion(bf16[4,256,512]{2,1,0:T(8,128)(2,1)} %get-tuple-element.86, bf16[4,256,286]{2,1,0:T(8,128)(2,1)S(1)} %reshape.427, f32[4,256]{1,0:T(4,128)S(1)} %fusion.23, bf16[4,15,512]{2,1,0:T(8,128)(2,1)S(1)} %collective-permute-done.3, bf16[4,256,512]{2,1,0:T(8,128)(2,1)} %copy-done.4, ...), kind=kOutput, calls=%fused_computation.9 | convolution fusion | flops 305504256 | bytes 3858432 | tf_op jit(solution)/shard_map/cfw,cwe->cfe/dot_general | solution.py:456
  81.1 1.8 convolution_bitcast_fusion
  82.9 2.1 fusion.11
  85.1 1.4 reshape.428
  86.6 1.1 slice.346
  87.7 3.1 %reshape.429 = f32[4,256,286]{2,1,0:T(8,128)S(1)} reshape(f32[4,73216]{1,0:T(4,128)} %slice.346) | data formatting | bytes 2342912 | tf_op jit(solution)/shard_map/reshape | solution.py:372
  90.8 0.7 reduce_sum.76
  91.4 0.7 fusion.22
  92.2 2.4 %fusion.1 = f32[4,286,512]{2,1,0:T(8,128)S(1)} fusion(f32[4,286]{1,0:T(4,128)S(1)} %fusion.22, bf16[4,15,512]{2,1,0:T(8,128)(2,1)S(1)} %copy-done.11, bf16[4,256,512]{2,1,0:T(8,128)(2,1)S(1)} %copy-done.5, bf16[4,15,512]{2,1,0:T(8,128)(2,1)S(1)} %copy-done.9, bf16[4,256,286]{2,1,0:T(8,128)(2,1)} %copy-done.7, bf16[4,256,512]{2,1,0:T(8,128)(2,1)} %get-tuple-element.86), kind=kOutput, calls=%fused_computation.6 | convolution fusion | flops 304578560 | bytes 5153248 | tf_op jit(solution)/shard_map/cfw,cfe->cwe/dot_general | solution.py:468
  94.6 1.9 collective-permute-start.4
  96.5 2.1 fusion.36
  98.7 0.2 slice.347
  99.0 0.4 copy-done.12
  99.4 0.7 select_reduce_fusion
  100.1 0.6 scatter.9.t_ref
  100.7 3.6 %collective-permute-start.5 = (f32[4,15,512]{2,1,0:T(8,128)S(1)}, f32[4,15,512]{2,1,0:T(8,128)S(1)}, u32[]{:S(2)}, u32[]{:S(2)}) collective-permute-start(f32[4,15,512]{2,1,0:T(8,128)S(1)} %get-tuple-element.65), channel_id=1, source_target_pairs={{0,1},{1,2},{2,3},{3,4},{4,5},{5,6},{6,7},{8,9},{9,10},{10,11},{11... | collective-permute-start | bytes 368648 | tf_op jit(solution)/shard_map/ppermute | solution.py:336
  104.4 0.5 scatter-add.6
  104.9 1.4 collective-permute-done.5
  106.3 0.4 scatter-add.9
  106.7 0.1 convert_element_type.61
  106.9 1.4 copy-done.24
  108.3 0.8 convolution_bitcast_fusion.1
  109.1 0.3 copy-done.21
  109.3 1.2 fusion.18
  110.5 0.2 copy-done.2
  110.8 1.0 fusion.35
  111.8 0.4 copy-done.1
  112.2 0.3 copy-done.6
  112.5 2.7 %pad_maximum_fusion.x_ref = f32[2560,512]{1,0:T(8,128)} fusion(f32[512,512]{1,0:T(8,128)S(1)} %copy-done.6, f32[512,512]{1,0:T(8,128)S(1)} %convolution_bitcast_fusion.1, f32[768,512]{1,0:T(8,128)S(1)} %copy-done.1, f32[768,512]{1,0:T(8,128)S(1)} %fusion.35), kind=kLoop, calls=%fused_computation | loop fusion | flops 3932160 | bytes 10485760 | tf_op jit(solution)/shard_map/concatenate | solution.py:485
  115.1 99.2 %shard_map.120 = (f32[2560,512]{1,0:T(8,128)S(1)}, f32[8,128]{1,0:T(8,128)S(1)}) custom-call(f32[2560,512]{1,0:T(8,128)} %pad_maximum_fusion.x_ref, f32[8,128]{1,0:T(8,128)S(1)} %scatter.9.t_ref), custom_call_target="tpu_custom_call" | custom-call | tf_op jit(solution)/shard_map/pallas_call | solution.py:287
  214.3 1.5 fusion.29
  215.8 2.0 fusion.30
  217.8 0.5 slice.298
  (98 shorter events, 3.3 us)
Async XLA Ops:
  0.6 39.9 %copy-start = (bf16[3,256,512]{2,1,0:T(8,128)(2,1)S(1)}, bf16[3,256,512]{2,1,0:T(8,128)(2,1)}, u32[]{:S(2)}) copy-start(bf16[3,256,512]{2,1,0:T(8,128)(2,1)} %param.20) | copy-start | bytes 2359300
  1.5 35.5 %collective-permute-start = (bf16[2,4,1,256]{3,2,1,0:T(2,128)(2,1)S(1)}, bf16[2,4,1,256]{3,2,1,0:T(2,128)(2,1)S(1)}, u32[]{:S(2)}, u32[]{:S(2)}) collective-permute-start(bf16[2,4,1,256]{3,2,1,0:T(2,128)(2,1)S(1)} %get-tuple-element.73), channel_id=1, source_target_pairs={{0,1},{1,2},{2,3},{3,4},{4,5},{5,6},{6,7},{8,9},{9,10},{10,11},{11... | collective-permute-start | bytes 12296 | tf_op jit(solution)/shard_map/ppermute | solution.py:324
  6.5 30.6 %collective-permute-start.1 = (bf16[2,4,1,256]{3,2,1,0:T(2,128)(2,1)S(1)}, bf16[2,4,1,256]{3,2,1,0:T(2,128)(2,1)S(1)}, u32[]{:S(2)}, u32[]{:S(2)}) collective-permute-start(bf16[2,4,1,256]{3,2,1,0:T(2,128)(2,1)S(1)} %get-tuple-element.74), channel_id=1, source_target_pairs={{1,0},{2,1},{3,2},{4,3},{5,4},{6,5},{7,6},{9,8},{10,9},{11,10},{12... | collective-permute-start | bytes 12296 | tf_op jit(solution)/shard_map/ppermute | solution.py:326
  40.5 1.0 copy-start.20
  41.5 1.3 copy-start.23
  41.5 13.1 %copy-start.17 = (bf16[3,256,512]{2,1,0:T(8,128)(2,1)S(1)}, bf16[3,256,512]{2,1,0:T(8,128)(2,1)}, u32[]{:S(2)}) copy-start(bf16[3,256,512]{2,1,0:T(8,128)(2,1)} %param.22) | copy-start | bytes 2359300
  42.9 15.9 %copy-start.4 = (bf16[4,256,512]{2,1,0:T(8,128)(2,1)}, bf16[4,256,512]{2,1,0:T(8,128)(2,1)S(1)}, u32[]{:S(2)}) copy-start(bf16[4,256,512]{2,1,0:T(8,128)(2,1)S(1)} %convolution_convert_fusion) | copy-start | bytes 3145732
  42.9 15.8 %collective-permute-start.2 = (bf16[4,15,512]{2,1,0:T(8,128)(2,1)S(1)}, bf16[4,15,512]{2,1,0:T(8,128)(2,1)S(1)}, u32[]{:S(2)}, u32[]{:S(2)}) collective-permute-start(bf16[4,15,512]{2,1,0:T(8,128)(2,1)S(1)} %get-tuple-element.71), channel_id=1, source_target_pairs={{0,1},{1,2},{2,3},{3,4},{4,5},{5,6},{6,7},{8,9},{9,10},{10,11},{11... | collective-permute-start | bytes 184328 | tf_op jit(solution)/shard_map/ppermute | solution.py:324
  52.7 6.0 %collective-permute-start.3 = (bf16[4,15,512]{2,1,0:T(8,128)(2,1)S(1)}, bf16[4,15,512]{2,1,0:T(8,128)(2,1)S(1)}, u32[]{:S(2)}, u32[]{:S(2)}) collective-permute-start(bf16[4,15,512]{2,1,0:T(8,128)(2,1)S(1)} %get-tuple-element.72), channel_id=1, source_target_pairs={{1,0},{2,1},{3,2},{4,3},{5,4},{6,5},{7,6},{9,8},{10,9},{11,10},{12... | collective-permute-start | bytes 184328 | tf_op jit(solution)/shard_map/ppermute | solution.py:326
  54.7 1.0 copy-start.18
  55.7 1.8 copy-start.25
  58.7 19.7 %copy-start.8 = (bf16[4,15,512]{2,1,0:T(8,128)(2,1)}, bf16[4,15,512]{2,1,0:T(8,128)(2,1)S(1)}, u32[]{:S(2)}) copy-start(bf16[4,15,512]{2,1,0:T(8,128)(2,1)S(1)} %collective-permute-done.2) | copy-start | bytes 184324
  58.7 19.7 %copy-start.10 = (bf16[4,15,512]{2,1,0:T(8,128)(2,1)}, bf16[4,15,512]{2,1,0:T(8,128)(2,1)S(1)}, u32[]{:S(2)}) copy-start(bf16[4,15,512]{2,1,0:T(8,128)(2,1)S(1)} %collective-permute-done.3) | copy-start | bytes 184324
  66.7 4.1 %copy-start.13 = (s32[4]{0:T(128)S(1)}, s32[4]{0:T(128)}, u32[]{:S(2)}) copy-start(s32[4]{0:T(128)} %param.18) | copy-start | bytes 52
  68.2 4.2 %copy-start.15 = (s32[4]{0:T(128)S(1)}, s32[4]{0:T(128)}, u32[]{:S(2)}) copy-start(s32[4]{0:T(128)} %param.19) | copy-start | bytes 52
  78.4 2.7 %copy-start.7 = (bf16[4,256,286]{2,1,0:T(8,128)(2,1)}, bf16[4,256,286]{2,1,0:T(8,128)(2,1)S(1)}, u32[]{:S(2)}) copy-start(bf16[4,256,286]{2,1,0:T(8,128)(2,1)S(1)} %reshape.427) | copy-start | bytes 1757188
  78.4 2.7 %copy-start.26 = (f32[4,256,512]{2,1,0:T(8,128)S(1)}, f32[4,256,512]{2,1,0:T(8,128)}, u32[]{:S(2)}) copy-start(f32[4,256,512]{2,1,0:T(8,128)} %copy-done.25) | copy-start | bytes 6291460
  81.1 1.8 copy-start.19
  87.7 4.5 %copy-start.5 = (bf16[4,256,512]{2,1,0:T(8,128)(2,1)S(1)}, bf16[4,256,512]{2,1,0:T(8,128)(2,1)}, u32[]{:S(2)}) copy-start(bf16[4,256,512]{2,1,0:T(8,128)(2,1)} %copy-done.4) | copy-start | bytes 3145732
  87.7 4.5 %copy-start.9 = (bf16[4,15,512]{2,1,0:T(8,128)(2,1)S(1)}, bf16[4,15,512]{2,1,0:T(8,128)(2,1)}, u32[]{:S(2)}) copy-start(bf16[4,15,512]{2,1,0:T(8,128)(2,1)} %copy-done.8) | copy-start | bytes 184324
  87.7 4.5 %copy-start.11 = (bf16[4,15,512]{2,1,0:T(8,128)(2,1)S(1)}, bf16[4,15,512]{2,1,0:T(8,128)(2,1)}, u32[]{:S(2)}) copy-start(bf16[4,15,512]{2,1,0:T(8,128)(2,1)} %copy-done.10) | copy-start | bytes 184324
  92.2 4.4 %copy-start.3 = (bf16[4,256,768]{2,1,0:T(8,128)(2,1)S(1)}, bf16[4,256,768]{2,1,0:T(8,128)(2,1)}, u32[]{:S(2)}) copy-start(bf16[4,256,768]{2,1,0:T(8,128)(2,1)} %pad_maximum_fusion.2) | copy-start | bytes 4718596
  92.2 4.4 %copy-start.22 = (bf16[1024,512]{1,0:T(8,128)(2,1)S(1)}, bf16[1024,512]{1,0:T(8,128)(2,1)}, u32[]{:S(2)}) copy-start(bf16[1024,512]{1,0:T(8,128)(2,1)} %fusion.11) | copy-start | bytes 3145732
  94.6 9.8 %collective-permute-start.4 = (f32[4,15,512]{2,1,0:T(8,128)S(1)}, f32[4,15,512]{2,1,0:T(8,128)S(1)}, u32[]{:S(2)}, u32[]{:S(2)}) collective-permute-start(f32[4,15,512]{2,1,0:T(8,128)S(1)} %get-tuple-element.66), channel_id=1, source_target_pairs={{1,0},{2,1},{3,2},{4,3},{5,4},{6,5},{7,6},{9,8},{10,9},{11,10},{12... | collective-permute-start | bytes 368648 | tf_op jit(solution)/shard_map/ppermute | solution.py:336
  98.7 0.7 copy-start.12
  98.7 0.7 copy-start.14
  98.7 0.7 copy-start.16
  100.7 5.6 %collective-permute-start.5 = (f32[4,15,512]{2,1,0:T(8,128)S(1)}, f32[4,15,512]{2,1,0:T(8,128)S(1)}, u32[]{:S(2)}, u32[]{:S(2)}) collective-permute-start(f32[4,15,512]{2,1,0:T(8,128)S(1)} %get-tuple-element.65), channel_id=1, source_target_pairs={{0,1},{1,2},{2,3},{3,4},{4,5},{5,6},{6,7},{8,9},{9,10},{10,11},{11... | collective-permute-start | bytes 368648 | tf_op jit(solution)/shard_map/ppermute | solution.py:336
  106.7 1.6 copy-start.24
  108.3 1.0 copy-start.21
  109.3 1.4 copy-start.2
  110.8 1.4 copy-start.1
  110.8 1.7 copy-start.6

commit v4 on v3

--- a/solution.py
+++ b/solution.py
@@ -83,15 +83,30 @@
 def _small_kernel(names, t_ref, to_ref, tbuf, tsend, trecv):
     table = _levels()
     levels = [table[k] for k in names]
-    _barrier(levels)
+    barrier = pltpu.get_barrier_semaphore()
+    peers = [nbr(me + j) for n, me, nbr, ndir in levels for j in range(1, n)]
+    for p in peers:
+        pl.semaphore_signal(barrier, inc=1, device_id=p, device_id_type=MESH_ID)
+    pl.semaphore_wait(barrier, len(peers))
     toff = 0
     tsem = 0
     for li, (n, me, nbr, ndir) in enumerate(levels):
         tbuf[toff + me] = t_ref[...] if li == 0 else to_ref[...]
-        for s in range(n - 1):
-            c = _small_start(n, me, nbr, s, tbuf, toff, tsend, trecv, tsem)
+        copies = []
+        for j in range(1, n):
+            c = pltpu.make_async_remote_copy(
+                src_ref=tbuf.at[toff + me],
+                dst_ref=tbuf.at[toff + me],
+                send_sem=tsend.at[tsem],
+                recv_sem=trecv.at[tsem],
+                device_id=nbr(me + j),
+                device_id_type=MESH_ID,
+            )
+            c.start()
+            copies.append(c)
+            tsem += 1
+        for c in copies:
             c.wait()
-            tsem += 1
         to_ref[...] = _small_sum(n, tbuf, toff)
         toff += n
 

time: 221 us -> 212 us (0.959)
  Pallas kernels: 122 us -> 116 us
  starting transfers between devices: 24.2 us -> 20.7 us
    pallas_call x1, Pallas kernels: 22.5 us -> 17.4 us  [small_sum(): pl.pallas_call(functools.partial(_small_kernel, names), out_shape=jax.Sha...]
    ppermute x2, starting transfers between devices: 14.7 us -> 11.3 us  [padded_2(): lax.ppermute(tail, axis, [(i, (i + 1) % count) for i in range(ends)])]
  transfers between devices with their start and end apart: 6 -> 6, of which waited for: 1 -> 1; matrix products, arithmetic and copies ran while one was open for 6% -> 6% of each run, Pallas kernels for 10% -> 8%
where the time goes in v4:
time: 212 us; the launch traced here: 211 us
  Pallas kernels  116 us (55%)
  local copies, waits for them, and re-layouts  30.9 us (15%)
  starting transfers between devices  20.7 us (10%)
  matrix products  20.7 us (10%)
  other arithmetic  17.6 us (8%)
  between operations  3.64 us (2%)
    pallas_call x1, Pallas kernels, all_sum(): pl.pallas_call(functools.partial(_kernel, rows), out_shape=(jax.ShapeDtyp...  98.9 us
    pallas_call x1, Pallas kernels, small_sum(): pl.pallas_call(functools.partial(_small_kernel, names), out_shape=jax.Sha...  17.4 us
    ppermute x2, starting transfers between devices, padded_2(): lax.ppermute(tail, axis, [(i, (i + 1) % count) for i in range(ends)])  11.3 us
    unnamed x84, local copies, waits for them, and re-layouts  6.12 us
    ppermute x2, starting transfers between devices, from_behind(): lax.ppermute(value, axis, [(source, source + steps) for source in range(i...  5.57 us
    reshape x2, local copies, waits for them, and re-layouts, spread_band(): return flat_band.reshape(clip_num, row_num, wide_len)  4.77 us
  transfers between devices with their start and end apart: 6, of which 1 were waited for; matrix products, arithmetic and copies ran while one was open for 6% of the time, Pallas kernels for 8%

profile of v4, /device:TPU:1, one launch (start us, length us, event | category | flops | bytes accessed | tf_op | source)
XLA Modules:
  0.0 211.2 jit_solution(13010288647742427103)
XLA Ops:
  0.6 0.9 pad_maximum_fusion.6
  1.5 4.9 %collective-permute-start = (bf16[2,4,1,256]{3,2,1,0:T(2,128)(2,1)S(1)}, bf16[2,4,1,256]{3,2,1,0:T(2,128)(2,1)S(1)}, u32[]{:S(2)}, u32[]{:S(2)}) collective-permute-start(bf16[2,4,1,256]{3,2,1,0:T(2,128)(2,1)S(1)} %get-tuple-element.73), channel_id=1, source_target_pairs={{0,1},{1,2},{2,3},{3,4},{4,5},{5,6},{6,7},{8,9},{9,10},{10,11},{11... | collective-permute-start | bytes 12296 | tf_op jit(solution)/shard_map/ppermute | solution.py:339
  6.5 1.9 collective-permute-start.1
  8.6 0.7 broadcast_compare_fusion.1
  9.4 0.7 compare_convert_fusion
  10.1 1.3 subtract_reduce_fusion
  11.4 1.2 scatter.6.t_ref
  12.6 17.4 %shard_map.119 = s32[8,128]{1,0:T(8,128)} custom-call(s32[8,128]{1,0:T(8,128)} %scatter.6.t_ref), custom_call_target="tpu_custom_call" | custom-call | tf_op jit(solution)/shard_map/pallas_call | solution.py:118
  30.0 1.2 slice.252
  31.9 1.5 pad_maximum_fusion.4
  33.5 0.6 fusion.33
  34.1 1.3 pad_maximum_fusion.1
  35.3 1.0 fusion.28
  36.4 0.7 convolution_convert_fusion
  37.1 0.6 copy-done.23
  37.7 6.3 %collective-permute-start.2 = (bf16[4,15,512]{2,1,0:T(8,128)(2,1)S(1)}, bf16[4,15,512]{2,1,0:T(8,128)(2,1)S(1)}, u32[]{:S(2)}, u32[]{:S(2)}) collective-permute-start(bf16[4,15,512]{2,1,0:T(8,128)(2,1)S(1)} %get-tuple-element.71), channel_id=1, source_target_pairs={{0,1},{1,2},{2,3},{3,4},{4,5},{5,6},{6,7},{8,9},{9,10},{10,11},{11... | collective-permute-start | bytes 184328 | tf_op jit(solution)/shard_map/ppermute | solution.py:339
  44.1 1.9 collective-permute-start.3
  46.0 1.0 fusion.27
  47.1 1.8 fusion.2
  48.8 1.2 pad_maximum_fusion.2
  50.1 0.5 fusion
  53.0 0.3 copy.1102
  53.2 2.3 %fusion.26 = f32[4,256,286]{2,1,0:T(8,128)S(1)} fusion(bf16[4,256,512]{2,1,0:T(8,128)(2,1)} %get-tuple-element.86, bf16[4,15,512]{2,1,0:T(8,128)(2,1)S(1)} %collective-permute-done.3, bf16[4,256,512]{2,1,0:T(8,128)(2,1)} %copy-done.4, bf16[4,15,512]{2,1,0:T(8,128)(2,1)S(1)} %collective-permute-done.2), kind=kOutput, calls=%fused_computation.138 | convolution fusion | flops 303407104 | bytes 3391488 | tf_op jit(solution)/shard_map/cfe,cwe->cfw/dot_general | solution.py:429
  55.5 2.5 %reshape.424 = f32[4,73216]{1,0:T(4,128)} reshape(f32[4,256,286]{2,1,0:T(8,128)S(1)} %fusion.26) | data formatting | bytes 2342912 | tf_op jit(solution)/shard_map/reshape | solution.py:392
  58.1 1.5 pad.27
  59.5 2.6 %reshape.425 = f32[4,256,287]{2,1,0:T(8,128)} reshape(f32[4,73472]{1,0:T(4,128)S(1)} %pad.27) | data formatting | bytes 2351104 | tf_op jit(solution)/shard_map/reshape | solution.py:393
  62.2 1.6 fusion.21
  63.8 2.7 %multiply_reduce_fusion = (f32[4,256]{1,0:T(4,128)}, f32[4,256]{1,0:T(4,128)S(1)}, f32[4,256,31]{2,1,0:T(8,128)S(1)}, bf16[4,256,31]{2,1,0:T(8,128)(2,1)S(1)}) fusion(f32[4,256,31]{2,1,0:T(8,128)S(1)} %get-tuple-element.60, f32[4,31]{1,0:T(4,128)S(1)} %compare_convert_fusion, f32[4,256,31]{2,1,0:T(8,128)S(1)} %copy.1102, f32[4,256,287]{2,1,0:T(8,128)} %reshape.425, ...), kind=kLoop, calls=%fused_computation.42 | loop fusion | flops 505856 | bytes 633088 | tf_op jit(solution)/shard_map/reduce_sum | solution.py:452
  66.7 1.2 reshape.426
  67.8 0.2 slice.345
  68.1 1.7 reshape.427
  69.8 2.6 %fusion.4 = bf16[4,256,512]{2,1,0:T(8,128)(2,1)S(1)} fusion(bf16[4,256,512]{2,1,0:T(8,128)(2,1)} %get-tuple-element.86, bf16[4,256,286]{2,1,0:T(8,128)(2,1)S(1)} %reshape.427, f32[4,256]{1,0:T(4,128)S(1)} %fusion.23, bf16[4,15,512]{2,1,0:T(8,128)(2,1)S(1)} %collective-permute-done.3, bf16[4,256,512]{2,1,0:T(8,128)(2,1)} %copy-done.4, ...), kind=kOutput, calls=%fused_computation.9 | convolution fusion | flops 305504256 | bytes 3858432 | tf_op jit(solution)/shard_map/cfw,cwe->cfe/dot_general | solution.py:471
  72.5 1.8 convolution_bitcast_fusion
  74.2 2.1 %fusion.11 = bf16[1024,512]{1,0:T(8,128)(2,1)} fusion(f32[4,256,512]{2,1,0:T(8,128)S(1)} %copy-done.26, bf16[1024,512]{1,0:T(8,128)(2,1)S(1)} %bitcast.223, bf16[512,512]{1,0:T(8,128)(2,1)S(1)} %copy-done.19), kind=kOutput, calls=%fused_computation.18 | convolution fusion | flops 541589504 | bytes 4718592 | tf_op jit(solution)/shard_map/rf,ef->re/dot_general | solution.py:405
  76.5 1.4 reshape.428
  77.9 1.1 slice.346
  79.0 3.1 %reshape.429 = f32[4,256,286]{2,1,0:T(8,128)S(1)} reshape(f32[4,73216]{1,0:T(4,128)} %slice.346) | data formatting | bytes 2342912 | tf_op jit(solution)/shard_map/reshape | solution.py:387
  82.1 0.7 reduce_sum.76
  82.8 0.7 fusion.22
  83.6 2.4 %fusion.1 = f32[4,286,512]{2,1,0:T(8,128)S(1)} fusion(f32[4,286]{1,0:T(4,128)S(1)} %fusion.22, bf16[4,15,512]{2,1,0:T(8,128)(2,1)S(1)} %copy-done.11, bf16[4,256,512]{2,1,0:T(8,128)(2,1)S(1)} %copy-done.5, bf16[4,15,512]{2,1,0:T(8,128)(2,1)S(1)} %copy-done.9, bf16[4,256,286]{2,1,0:T(8,128)(2,1)} %copy-done.7, bf16[4,256,512]{2,1,0:T(8,128)(2,1)} %get-tuple-element.86), kind=kOutput, calls=%fused_computation.6 | convolution fusion | flops 304578560 | bytes 5153248 | tf_op jit(solution)/shard_map/cfw,cfe->cwe/dot_general | solution.py:483
  86.0 1.9 collective-permute-start.4
  87.9 2.1 %fusion.36 = f32[768,512]{1,0:T(8,128)} fusion(bf16[1024,768]{1,0:T(8,128)(2,1)S(1)} %bitcast.218, bf16[1024,512]{1,0:T(8,128)(2,1)S(1)} %copy-done.22), kind=kOutput, calls=%fused_computation.148 | convolution fusion | flops 805306368 | bytes 4194304 | tf_op jit(solution)/shard_map/rk,re->ke/dot_general | solution.py:407
  90.1 0.2 slice.347
  90.3 0.4 copy-done.12
  90.8 0.7 select_reduce_fusion
  91.4 0.6 scatter.9.t_ref
  92.1 3.6 %collective-permute-start.5 = (f32[4,15,512]{2,1,0:T(8,128)S(1)}, f32[4,15,512]{2,1,0:T(8,128)S(1)}, u32[]{:S(2)}, u32[]{:S(2)}) collective-permute-start(f32[4,15,512]{2,1,0:T(8,128)S(1)} %get-tuple-element.65), channel_id=1, source_target_pairs={{0,1},{1,2},{2,3},{3,4},{4,5},{5,6},{6,7},{8,9},{9,10},{10,11},{11... | collective-permute-start | bytes 368648 | tf_op jit(solution)/shard_map/ppermute | solution.py:351
  95.8 0.5 scatter-add.6
  96.3 1.4 collective-permute-done.5
  97.7 0.4 scatter-add.9
  98.1 0.1 convert_element_type.61
  98.2 1.4 copy-done.24
  99.7 0.8 convolution_bitcast_fusion.1
  100.4 0.3 copy-done.21
  100.7 1.2 fusion.18
  101.9 0.2 copy-done.2
  102.1 1.0 fusion.35
  103.1 0.4 copy-done.1
  103.5 0.3 copy-done.6
  103.8 2.7 %pad_maximum_fusion.x_ref = f32[2560,512]{1,0:T(8,128)} fusion(f32[512,512]{1,0:T(8,128)S(1)} %copy-done.6, f32[512,512]{1,0:T(8,128)S(1)} %convolution_bitcast_fusion.1, f32[768,512]{1,0:T(8,128)S(1)} %copy-done.1, f32[768,512]{1,0:T(8,128)S(1)} %fusion.35), kind=kLoop, calls=%fused_computation | loop fusion | flops 3932160 | bytes 10485760 | tf_op jit(solution)/shard_map/concatenate | solution.py:500
  106.5 98.9 %shard_map.120 = (f32[2560,512]{1,0:T(8,128)S(1)}, f32[8,128]{1,0:T(8,128)S(1)}) custom-call(f32[2560,512]{1,0:T(8,128)} %pad_maximum_fusion.x_ref, f32[8,128]{1,0:T(8,128)S(1)} %scatter.9.t_ref), custom_call_target="tpu_custom_call" | custom-call | tf_op jit(solution)/shard_map/pallas_call | solution.py:302
  205.4 1.5 fusion.29
  206.9 2.0 fusion.30
  208.9 0.5 slice.298
  (98 shorter events, 3.3 us)
Async XLA Ops:
  0.6 34.7 %copy-start = (bf16[3,256,512]{2,1,0:T(8,128)(2,1)S(1)}, bf16[3,256,512]{2,1,0:T(8,128)(2,1)}, u32[]{:S(2)}) copy-start(bf16[3,256,512]{2,1,0:T(8,128)(2,1)} %param.20) | copy-start | bytes 2359300
  1.5 30.4 %collective-permute-start = (bf16[2,4,1,256]{3,2,1,0:T(2,128)(2,1)S(1)}, bf16[2,4,1,256]{3,2,1,0:T(2,128)(2,1)S(1)}, u32[]{:S(2)}, u32[]{:S(2)}) collective-permute-start(bf16[2,4,1,256]{3,2,1,0:T(2,128)(2,1)S(1)} %get-tuple-element.73), channel_id=1, source_target_pairs={{0,1},{1,2},{2,3},{3,4},{4,5},{5,6},{6,7},{8,9},{9,10},{10,11},{11... | collective-permute-start | bytes 12296 | tf_op jit(solution)/shard_map/ppermute | solution.py:339
  6.5 25.4 %collective-permute-start.1 = (bf16[2,4,1,256]{3,2,1,0:T(2,128)(2,1)S(1)}, bf16[2,4,1,256]{3,2,1,0:T(2,128)(2,1)S(1)}, u32[]{:S(2)}, u32[]{:S(2)}) collective-permute-start(bf16[2,4,1,256]{3,2,1,0:T(2,128)(2,1)S(1)} %get-tuple-element.74), channel_id=1, source_target_pairs={{1,0},{2,1},{3,2},{4,3},{5,4},{6,5},{7,6},{9,8},{10,9},{11,10},{12... | collective-permute-start | bytes 12296 | tf_op jit(solution)/shard_map/ppermute | solution.py:341
  35.3 1.0 copy-start.20
  36.4 1.3 copy-start.23
  36.4 9.6 %copy-start.17 = (bf16[3,256,512]{2,1,0:T(8,128)(2,1)S(1)}, bf16[3,256,512]{2,1,0:T(8,128)(2,1)}, u32[]{:S(2)}) copy-start(bf16[3,256,512]{2,1,0:T(8,128)(2,1)} %param.22) | copy-start | bytes 2359300
  37.7 12.4 %copy-start.4 = (bf16[4,256,512]{2,1,0:T(8,128)(2,1)}, bf16[4,256,512]{2,1,0:T(8,128)(2,1)S(1)}, u32[]{:S(2)}) copy-start(bf16[4,256,512]{2,1,0:T(8,128)(2,1)S(1)} %convolution_convert_fusion) | copy-start | bytes 3145732
  37.7 12.3 %collective-permute-start.2 = (bf16[4,15,512]{2,1,0:T(8,128)(2,1)S(1)}, bf16[4,15,512]{2,1,0:T(8,128)(2,1)S(1)}, u32[]{:S(2)}, u32[]{:S(2)}) collective-permute-start(bf16[4,15,512]{2,1,0:T(8,128)(2,1)S(1)} %get-tuple-element.71), channel_id=1, source_target_pairs={{0,1},{1,2},{2,3},{3,4},{4,5},{5,6},{6,7},{8,9},{9,10},{10,11},{11... | collective-permute-start | bytes 184328 | tf_op jit(solution)/shard_map/ppermute | solution.py:339
  44.1 6.0 %collective-permute-start.3 = (bf16[4,15,512]{2,1,0:T(8,128)(2,1)S(1)}, bf16[4,15,512]{2,1,0:T(8,128)(2,1)S(1)}, u32[]{:S(2)}, u32[]{:S(2)}) collective-permute-start(bf16[4,15,512]{2,1,0:T(8,128)(2,1)S(1)} %get-tuple-element.72), channel_id=1, source_target_pairs={{1,0},{2,1},{3,2},{4,3},{5,4},{6,5},{7,6},{9,8},{10,9},{11,10},{12... | collective-permute-start | bytes 184328 | tf_op jit(solution)/shard_map/ppermute | solution.py:341
  46.0 1.0 copy-start.18
  47.1 1.8 copy-start.25
  50.1 19.7 %copy-start.8 = (bf16[4,15,512]{2,1,0:T(8,128)(2,1)}, bf16[4,15,512]{2,1,0:T(8,128)(2,1)S(1)}, u32[]{:S(2)}) copy-start(bf16[4,15,512]{2,1,0:T(8,128)(2,1)S(1)} %collective-permute-done.2) | copy-start | bytes 184324
  50.1 19.7 %copy-start.10 = (bf16[4,15,512]{2,1,0:T(8,128)(2,1)}, bf16[4,15,512]{2,1,0:T(8,128)(2,1)S(1)}, u32[]{:S(2)}) copy-start(bf16[4,15,512]{2,1,0:T(8,128)(2,1)S(1)} %collective-permute-done.3) | copy-start | bytes 184324
  58.0 4.1 %copy-start.13 = (s32[4]{0:T(128)S(1)}, s32[4]{0:T(128)}, u32[]{:S(2)}) copy-start(s32[4]{0:T(128)} %param.18) | copy-start | bytes 52
  59.5 4.2 %copy-start.15 = (s32[4]{0:T(128)S(1)}, s32[4]{0:T(128)}, u32[]{:S(2)}) copy-start(s32[4]{0:T(128)} %param.19) | copy-start | bytes 52
  69.8 2.7 %copy-start.7 = (bf16[4,256,286]{2,1,0:T(8,128)(2,1)}, bf16[4,256,286]{2,1,0:T(8,128)(2,1)S(1)}, u32[]{:S(2)}) copy-start(bf16[4,256,286]{2,1,0:T(8,128)(2,1)S(1)} %reshape.427) | copy-start | bytes 1757188
  69.8 2.7 %copy-start.26 = (f32[4,256,512]{2,1,0:T(8,128)S(1)}, f32[4,256,512]{2,1,0:T(8,128)}, u32[]{:S(2)}) copy-start(f32[4,256,512]{2,1,0:T(8,128)} %copy-done.25) | copy-start | bytes 6291460
  72.5 1.8 copy-start.19
  79.0 4.5 %copy-start.5 = (bf16[4,256,512]{2,1,0:T(8,128)(2,1)S(1)}, bf16[4,256,512]{2,1,0:T(8,128)(2,1)}, u32[]{:S(2)}) copy-start(bf16[4,256,512]{2,1,0:T(8,128)(2,1)} %copy-done.4) | copy-start | bytes 3145732
  79.0 4.5 %copy-start.9 = (bf16[4,15,512]{2,1,0:T(8,128)(2,1)S(1)}, bf16[4,15,512]{2,1,0:T(8,128)(2,1)}, u32[]{:S(2)}) copy-start(bf16[4,15,512]{2,1,0:T(8,128)(2,1)} %copy-done.8) | copy-start | bytes 184324
  79.0 4.5 %copy-start.11 = (bf16[4,15,512]{2,1,0:T(8,128)(2,1)S(1)}, bf16[4,15,512]{2,1,0:T(8,128)(2,1)}, u32[]{:S(2)}) copy-start(bf16[4,15,512]{2,1,0:T(8,128)(2,1)} %copy-done.10) | copy-start | bytes 184324
  83.5 4.4 %copy-start.3 = (bf16[4,256,768]{2,1,0:T(8,128)(2,1)S(1)}, bf16[4,256,768]{2,1,0:T(8,128)(2,1)}, u32[]{:S(2)}) copy-start(bf16[4,256,768]{2,1,0:T(8,128)(2,1)} %pad_maximum_fusion.2) | copy-start | bytes 4718596
  83.5 4.4 %copy-start.22 = (bf16[1024,512]{1,0:T(8,128)(2,1)S(1)}, bf16[1024,512]{1,0:T(8,128)(2,1)}, u32[]{:S(2)}) copy-start(bf16[1024,512]{1,0:T(8,128)(2,1)} %fusion.11) | copy-start | bytes 3145732
  86.0 9.8 %collective-permute-start.4 = (f32[4,15,512]{2,1,0:T(8,128)S(1)}, f32[4,15,512]{2,1,0:T(8,128)S(1)}, u32[]{:S(2)}, u32[]{:S(2)}) collective-permute-start(f32[4,15,512]{2,1,0:T(8,128)S(1)} %get-tuple-element.66), channel_id=1, source_target_pairs={{1,0},{2,1},{3,2},{4,3},{5,4},{6,5},{7,6},{9,8},{10,9},{11,10},{12... | collective-permute-start | bytes 368648 | tf_op jit(solution)/shard_map/ppermute | solution.py:351
  90.1 0.7 copy-start.12
  90.1 0.7 copy-start.14
  90.1 0.7 copy-start.16
  92.1 5.6 %collective-permute-start.5 = (f32[4,15,512]{2,1,0:T(8,128)S(1)}, f32[4,15,512]{2,1,0:T(8,128)S(1)}, u32[]{:S(2)}, u32[]{:S(2)}) collective-permute-start(f32[4,15,512]{2,1,0:T(8,128)S(1)} %get-tuple-element.65), channel_id=1, source_target_pairs={{0,1},{1,2},{2,3},{3,4},{4,5},{5,6},{6,7},{8,9},{9,10},{10,11},{11... | collective-permute-start | bytes 368648 | tf_op jit(solution)/shard_map/ppermute | solution.py:351
  98.1 1.6 copy-start.24
  99.7 1.0 copy-start.21
  100.7 1.4 copy-start.2
  102.1 1.4 copy-start.1
  102.1 1.7 copy-start.6

commit v5 on v4

--- a/solution.py
+++ b/solution.py
@@ -323,6 +323,80 @@
     )(flat, small)
 
 
+def _corr_fwd_kernel(ev_ref, win_ref, inv_ref, dots_ref, strip_ref):
+    wide = win_ref.shape[0]
+    lanes = dots_ref.shape[1]
+    m = lax.dot_general(
+        ev_ref[...], win_ref[...], (((1,), (1,)), ((), ())), preferred_element_type=jnp.float32
+    )
+    dots_ref[...] = pltpu.roll(m, 0, 1, stride=1, stride_axis=0)[:, wide - lanes :]
+    inv = jnp.broadcast_to(inv_ref[...], m.shape)
+    strip_ref[...] = pltpu.roll(inv, 0, 1, stride=1, stride_axis=0)[:, wide - lanes :]
+
+
+def corr_fwd(emb_v, win_pad, inv_pad):
+    clips, frames, width = emb_v.shape
+    wide = win_pad.shape[1]
+    lanes = 128
+    return pl.pallas_call(
+        _corr_fwd_kernel,
+        grid=(clips,),
+        in_specs=[
+            pl.BlockSpec((None, frames, width), lambda c: (c, 0, 0)),
+            pl.BlockSpec((None, wide, width), lambda c: (c, 0, 0)),
+            pl.BlockSpec((None, 1, wide), lambda c: (c, 0, 0)),
+        ],
+        out_specs=[
+            pl.BlockSpec((None, frames, lanes), lambda c: (c, 0, 0)),
+            pl.BlockSpec((None, frames, lanes), lambda c: (c, 0, 0)),
+        ],
+        out_shape=[
+            jax.ShapeDtypeStruct((clips, frames, lanes), jnp.float32),
+            jax.ShapeDtypeStruct((clips, frames, lanes), jnp.float32),
+        ],
+    )(emb_v, win_pad, inv_pad)
+
+
+def _corr_bwd_kernel(gd_ref, at_ref, ev_ref, win_ref, lip_ref, wsum_ref, ginv_ref):
+    frames, lanes = gd_ref.shape
+    wide = win_ref.shape[0]
+    pad = jnp.zeros((frames, wide - lanes), jnp.float32)
+    g = jnp.concatenate([gd_ref[...].astype(jnp.float32), pad], axis=1)
+    band = pltpu.roll(g, 0, 1, stride=1, stride_axis=0)
+    lip_ref[...] = jnp.dot(band.astype(jnp.bfloat16), win_ref[...], preferred_element_type=jnp.float32)
+    band_t = band.T.astype(jnp.bfloat16)
+    wsum_ref[...] = jnp.dot(band_t, ev_ref[...], preferred_element_type=jnp.float32)
+    a = jnp.concatenate([at_ref[...], pad], axis=1)
+    spread = pltpu.roll(a, 0, 1, stride=1, stride_axis=0)
+    ginv_ref[...] = jnp.sum(spread, axis=0, keepdims=True)
+
+
+def corr_bwd(gd_pad, at_pad, emb_v, win_pad):
+    clips, frames, width = emb_v.shape
+    wide = win_pad.shape[1]
+    lanes = gd_pad.shape[2]
+    return pl.pallas_call(
+        _corr_bwd_kernel,
+        grid=(clips,),
+        in_specs=[
+            pl.BlockSpec((None, frames, lanes), lambda c: (c, 0, 0)),
+            pl.BlockSpec((None, frames, lanes), lambda c: (c, 0, 0)),
+            pl.BlockSpec((None, frames, width), lambda c: (c, 0, 0)),
+            pl.BlockSpec((None, wide, width), lambda c: (c, 0, 0)),
+        ],
+        out_specs=[
+            pl.BlockSpec((None, frames, width), lambda c: (c, 0, 0)),
+            pl.BlockSpec((None, wide, width), lambda c: (c, 0, 0)),
+            pl.BlockSpec((None, 1, wide), lambda c: (c, 0, 0)),
+        ],
+        out_shape=[
+            jax.ShapeDtypeStruct((clips, frames, width), jnp.float32),
+            jax.ShapeDtypeStruct((clips, wide, width), jnp.float32),
+            jax.ShapeDtypeStruct((clips, 1, wide), jnp.float32),
+        ],
+    )(gd_pad, at_pad, emb_v, win_pad)
+
+
 logit_sharpening_divisor = 10.0
 loss_scale = 1024.0
 epsilon = 1e-06
@@ -426,13 +500,14 @@
     count_part = jnp.sum(lengths - jnp.abs(labels))
     count_block = jnp.zeros((8, 128), jnp.int32).at[0, 0].set(count_part)
     count = small_sum(count_block, ("y", "x", "h"), 1)[0, 0].astype(jnp.float32)
-    matrix = jnp.einsum("cfe,cwe->cfw", emb_v, window, preferred_element_type=jnp.float32)
-    lagged_inner_terms = narrow_band(matrix, offsets)
     inv_win = inverse_norm(window)
     reciprocal_visual_length = inverse_norm(emb_v)
-    reciprocal_lag_strip = jnp.stack(
-        [inv_win[:, offset : offset + frame_num] for offset in range(offsets)], axis=2
-    )
+    wide_pad = -(-wide_len // 128) * 128
+    win_pad = jnp.pad(window, ((0, 0), (0, wide_pad - wide_len), (0, 0)))
+    inv_pad = jnp.pad(inv_win, ((0, 0), (0, wide_pad - wide_len)))[:, None, :]
+    dots_rev, strip_rev = corr_fwd(emb_v, win_pad[:, ::-1], inv_pad[:, :, ::-1])
+    lagged_inner_terms = dots_rev[:, :, ::-1][:, :, :offsets]
+    reciprocal_lag_strip = strip_rev[:, :, ::-1][:, :, :offsets]
     frame_ids = first_frame + jnp.arange(frame_num, dtype=jnp.int32)
     shifts = jnp.arange(offsets, dtype=jnp.int32) - SPAN
     positions = frame_ids[:, None] + shifts[None, :]
@@ -461,14 +536,12 @@
         logit_derivative * reciprocal_visual_length[:, :, None] * reciprocal_lag_strip
     ).astype(jnp.bfloat16)
     grad_inv_v = jnp.sum(logit_derivative * lagged_inner_terms * reciprocal_lag_strip, axis=2)
-    grad_inv_win = jnp.sum(
-        spread_band(
-            logit_derivative * lagged_inner_terms * reciprocal_visual_length[:, :, None], wide_len
-        ),
-        axis=1,
-    )
-    band_full = spread_band(grad_dots, wide_len)
-    lip_sum = jnp.einsum("cfw,cwe->cfe", band_full, window, preferred_element_type=jnp.float32)
+    audio_term = logit_derivative * lagged_inner_terms * reciprocal_visual_length[:, :, None]
+    band_pad = ((0, 0), (0, 0), (0, 128 - offsets))
+    lip_sum, win_sum_pad, ginv_pad = corr_bwd(
+        jnp.pad(grad_dots, band_pad), jnp.pad(audio_term, band_pad), emb_v, win_pad
+    )
+    grad_inv_win = ginv_pad[:, 0, :wide_len]
     lip_vals = emb_v.astype(jnp.float32)
     grad_lip = (
         lip_sum
@@ -480,7 +553,7 @@
         )[:, :, None]
         * lip_vals
     ).astype(jnp.bfloat16)
-    win_sum = jnp.einsum("cfw,cfe->cwe", band_full, emb_v, preferred_element_type=jnp.float32)
+    win_sum = win_sum_pad[:, :wide_len]
     win_sum = win_sum - (inv_win * inv_win * inv_win * grad_inv_win)[:, :, None] * window.astype(
         jnp.float32
     )

time: 212 us -> 223 us (1.052)
  Pallas kernels: 116 us -> 126 us
  matrix products: 20.7 us -> 12.4 us
  local copies, waits for them, and re-layouts: 30.9 us -> 35.5 us
  other arithmetic: 17.6 us -> 21.8 us
    rev x0 -> x2, local copies, waits for them, and re-layouts: none -> 16 us  [shards(): dots_rev, strip_rev = corr_fwd(emb_v, win_pad[:, ::-1], inv_pad[:, :, ::-1])]
    reshape x6 -> x0, local copies, waits for them, and re-layouts: 12.5 us -> none  [the longest x2 4.77 us: spread_band(): return flat_band.reshape(clip_num, row_num, wide_len)]
    pallas_call x0 -> x2, Pallas kernels: none -> 9.8 us  [the longest x1 5.45 us: corr_bwd(): pl.pallas_call(_corr_bwd_kernel, grid=(clips,), in_specs=[pl.BlockSpec((N...]
    dot_general x3 -> x0, matrix products: 7.27 us -> none  [the longest x1 2.65 us: shards(): jnp.einsum('cfw,cwe->cfe', band_full, window, preferred_element_type=jnp....]
    slice x2 -> x4, local copies, waits for them, and re-layouts: 1.29 us -> 3.94 us  [the longest x2 1.98 us: shards(): reciprocal_lag_strip = strip_rev[:, :, ::-1][:, :, :offsets]]
    unnamed x84 -> x40, local copies, waits for them, and re-layouts: 6.12 us -> 4.92 us
  transfers between devices with their start and end apart: 6 -> 6, of which waited for: 1 -> 1; matrix products, arithmetic and copies ran while one was open for 6% -> 8% of each run, Pallas kernels for 8% -> 8%
where the time goes in v5:
time: 223 us; the launch traced here: 222 us
  Pallas kernels  126 us (57%)
  local copies, waits for them, and re-layouts  35.5 us (16%)
  other arithmetic  21.8 us (10%)
  starting transfers between devices  20.9 us (9%)
  matrix products  12.4 us (6%)
  between operations  3.51 us (2%)
    pallas_call x1, Pallas kernels, all_sum(): pl.pallas_call(functools.partial(_kernel, rows), out_shape=(jax.ShapeDtyp...  98.9 us
    pallas_call x1, Pallas kernels, small_sum(): pl.pallas_call(functools.partial(_small_kernel, names), out_shape=jax.Sha...  17.3 us
    rev x2, local copies, waits for them, and re-layouts, shards(): dots_rev, strip_rev = corr_fwd(emb_v, win_pad[:, ::-1], inv_pad[:, :, ::-1])  16 us
    ppermute x2, starting transfers between devices, padded_2(): lax.ppermute(tail, axis, [(i, (i + 1) % count) for i in range(ends)])  11.3 us
    ppermute x2, starting transfers between devices, from_behind(): lax.ppermute(value, axis, [(source, source + steps) for source in range(i...  5.75 us
    pallas_call x1, Pallas kernels, corr_bwd(): pl.pallas_call(_corr_bwd_kernel, grid=(clips,), in_specs=[pl.BlockSpec((N...  5.45 us
    unnamed x40, local copies, waits for them, and re-layouts  4.92 us
  transfers between devices with their start and end apart: 6, of which 1 were waited for; matrix products, arithmetic and copies ran while one was open for 8% of the time, Pallas kernels for 8%

profile of v5, /device:TPU:1, one launch (start us, length us, event | category | flops | bytes accessed | tf_op | source)
XLA Modules:
  0.0 221.6 jit_solution(10970274171736111118)
XLA Ops:
  0.6 0.9 pad_maximum_fusion.6
  1.5 4.9 %collective-permute-start = (bf16[2,4,1,256]{3,2,1,0:T(2,128)(2,1)S(1)}, bf16[2,4,1,256]{3,2,1,0:T(2,128)(2,1)S(1)}, u32[]{:S(2)}, u32[]{:S(2)}) collective-permute-start(bf16[2,4,1,256]{3,2,1,0:T(2,128)(2,1)S(1)} %get-tuple-element.86), channel_id=1, source_target_pairs={{0,1},{1,2},{2,3},{3,4},{4,5},{5,6},{6,7},{8,9},{9,10},{10,11},{11... | collective-permute-start | bytes 12296 | tf_op jit(solution)/shard_map/ppermute | solution.py:413
  6.5 1.9 collective-permute-start.1
  8.4 0.7 broadcast_compare_fusion
  9.1 0.8 broadcast_add_fusion
  9.9 1.2 broadcast_compare_fusion.1
  11.1 1.3 compare_convert_fusion
  12.4 1.3 subtract_reduce_fusion
  13.8 1.2 scatter.6.t_ref
  15.0 17.3 %shard_map.119 = s32[8,128]{1,0:T(8,128)} custom-call(s32[8,128]{1,0:T(8,128)} %scatter.6.t_ref), custom_call_target="tpu_custom_call" | custom-call | tf_op jit(solution)/shard_map/pallas_call | solution.py:118
  32.4 1.2 slice.168
  34.2 1.5 pad_maximum_fusion.4
  35.8 0.6 fusion.34
  36.4 1.2 pad_maximum_fusion.1
  37.7 1.0 fusion.28
  38.7 0.7 convolution_convert_fusion
  39.4 0.6 copy-done.16
  40.1 6.3 %collective-permute-start.2 = (bf16[4,15,512]{2,1,0:T(8,128)(2,1)S(1)}, bf16[4,15,512]{2,1,0:T(8,128)(2,1)S(1)}, u32[]{:S(2)}, u32[]{:S(2)}) collective-permute-start(bf16[4,15,512]{2,1,0:T(8,128)(2,1)S(1)} %get-tuple-element.84), channel_id=1, source_target_pairs={{0,1},{1,2},{2,3},{3,4},{4,5},{5,6},{6,7},{8,9},{9,10},{10,11},{11... | collective-permute-start | bytes 184328 | tf_op jit(solution)/shard_map/ppermute | solution.py:413
  46.4 1.9 collective-permute-start.3
  48.4 1.0 fusion.27
  49.4 1.8 fusion.2
  51.2 1.3 pad_maximum_fusion.2
  52.4 0.5 fusion
  53.0 0.3 reverse.5
  53.3 0.6 copy.13.inv_ref
  54.0 15.4 %rev.8.win_ref = bf16[4,384,512]{2,1,0:T(8,128)(2,1)} reverse(bf16[4,384,512]{2,1,0:T(8,128)(2,1)S(1)} %pad.31.win_ref), dimensions={1} | reverse | bytes 3145728 | tf_op jit(solution)/shard_map/rev | solution.py:508
  69.4 4.4 %shard_map.120 = (f32[4,256,128]{2,1,0:T(8,128)}, f32[4,256,128]{2,1,0:T(8,128)}) custom-call(bf16[4,256,512]{2,1,0:T(8,128)(2,1)} %get-tuple-element.98.ev_ref, bf16[4,384,512]{2,1,0:T(8,128)(2,1)} %rev.8.win_ref, f32[4,1,384]{2,1,0:T(1,128)} %copy.13.inv_ref), custom_call_target="tpu_custom_call" | custom-call | tf_op jit(solution)/shard_map/pallas_call | solution.py:341
  73.8 1.2 slice.175
  75.0 0.7 slice.176
  75.8 1.3 slice.177
  77.0 0.7 slice.178
  77.7 1.6 multiply_reduce_fusion
  79.4 1.4 select_reduce_fusion
  80.8 1.9 multiply_reduce_fusion.1
  82.7 0.8 pad.33.gd_ref
  83.6 0.8 pad.34.at_ref
  84.5 5.4 %shard_map.121 = (f32[4,256,512]{2,1,0:T(8,128)}, f32[4,384,512]{2,1,0:T(8,128)}, f32[4,1,384]{2,1,0:T(1,128)}) custom-call(bf16[4,256,128]{2,1,0:T(8,128)(2,1)} %pad.33.gd_ref, f32[4,256,128]{2,1,0:T(8,128)} %pad.34.at_ref, bf16[4,256,512]{2,1,0:T(8,128)(2,1)} %get-tuple-element.98.ev_ref, bf16[4,384,512]{2,1,0:T(8,128)(2,1)} %copy-done.1), custom_call_target="tpu_custom_call" | custom-call | tf_op jit(solution)/shard_map/pallas_call | solution.py:378
  89.9 0.7 fusion.23
  90.6 2.1 fusion.1
  92.8 1.9 collective-permute-start.4
  94.7 0.3 fusion.4
  95.0 1.3 copy-done.19
  96.3 1.7 convolution_bitcast_fusion
  98.1 1.2 fusion.11
  99.2 0.2 copy-done.6
  99.5 2.1 fusion.37
  101.6 0.3 slice.201
  101.9 0.6 scatter.9.t_ref
  102.5 3.8 %collective-permute-start.5 = (f32[4,15,512]{2,1,0:T(8,128)S(1)}, f32[4,15,512]{2,1,0:T(8,128)S(1)}, u32[]{:S(2)}, u32[]{:S(2)}) collective-permute-start(f32[4,15,512]{2,1,0:T(8,128)S(1)} %get-tuple-element.79), channel_id=1, source_target_pairs={{0,1},{1,2},{2,3},{3,4},{4,5},{5,6},{6,7},{8,9},{9,10},{10,11},{11... | collective-permute-start | bytes 368648 | tf_op jit(solution)/shard_map/ppermute | solution.py:425
  106.4 0.3 scatter-add.6
  106.6 1.4 collective-permute-done.5
  108.1 0.4 scatter-add.9
  108.6 1.4 copy-done.17
  110.1 0.8 convolution_bitcast_fusion.1
  110.8 0.3 copy-done.15
  111.1 1.2 fusion.18
  112.5 1.0 fusion.36
  113.5 0.4 copy-done.4
  113.9 0.3 copy-done.7
  114.2 2.7 %pad_maximum_fusion.x_ref = f32[2560,512]{1,0:T(8,128)} fusion(f32[512,512]{1,0:T(8,128)S(1)} %copy-done.7, f32[512,512]{1,0:T(8,128)S(1)} %convolution_bitcast_fusion.1, f32[768,512]{1,0:T(8,128)S(1)} %copy-done.4, f32[768,512]{1,0:T(8,128)S(1)} %fusion.36), kind=kLoop, calls=%fused_computation | loop fusion | flops 3932160 | bytes 10485760 | tf_op jit(solution)/shard_map/concatenate | solution.py:573
  116.9 98.9 %shard_map.122 = (f32[2560,512]{1,0:T(8,128)S(1)}, f32[8,128]{1,0:T(8,128)S(1)}) custom-call(f32[2560,512]{1,0:T(8,128)} %pad_maximum_fusion.x_ref, f32[8,128]{1,0:T(8,128)S(1)} %scatter.9.t_ref), custom_call_target="tpu_custom_call" | custom-call | tf_op jit(solution)/shard_map/pallas_call | solution.py:302
  215.8 1.5 fusion.30
  217.3 2.0 fusion.31
  219.3 0.5 slice.186
  (52 shorter events, 1.1 us)
Async XLA Ops:
  0.6 37.0 %copy-start = (bf16[3,256,512]{2,1,0:T(8,128)(2,1)S(1)}, bf16[3,256,512]{2,1,0:T(8,128)(2,1)}, u32[]{:S(2)}) copy-start(bf16[3,256,512]{2,1,0:T(8,128)(2,1)} %param.20) | copy-start | bytes 2359300
  1.5 32.7 %collective-permute-start = (bf16[2,4,1,256]{3,2,1,0:T(2,128)(2,1)S(1)}, bf16[2,4,1,256]{3,2,1,0:T(2,128)(2,1)S(1)}, u32[]{:S(2)}, u32[]{:S(2)}) collective-permute-start(bf16[2,4,1,256]{3,2,1,0:T(2,128)(2,1)S(1)} %get-tuple-element.86), channel_id=1, source_target_pairs={{0,1},{1,2},{2,3},{3,4},{4,5},{5,6},{6,7},{8,9},{9,10},{10,11},{11... | collective-permute-start | bytes 12296 | tf_op jit(solution)/shard_map/ppermute | solution.py:413
  6.5 27.8 %collective-permute-start.1 = (bf16[2,4,1,256]{3,2,1,0:T(2,128)(2,1)S(1)}, bf16[2,4,1,256]{3,2,1,0:T(2,128)(2,1)S(1)}, u32[]{:S(2)}, u32[]{:S(2)}) collective-permute-start(bf16[2,4,1,256]{3,2,1,0:T(2,128)(2,1)S(1)} %get-tuple-element.87), channel_id=1, source_target_pairs={{1,0},{2,1},{3,2},{4,3},{5,4},{6,5},{7,6},{9,8},{10,9},{11,10},{12... | collective-permute-start | bytes 12296 | tf_op jit(solution)/shard_map/ppermute | solution.py:415
  8.4 1.5 copy-start.8
  37.7 1.0 copy-start.14
  38.7 1.4 copy-start.16
  38.7 9.6 %copy-start.11 = (bf16[3,256,512]{2,1,0:T(8,128)(2,1)S(1)}, bf16[3,256,512]{2,1,0:T(8,128)(2,1)}, u32[]{:S(2)}) copy-start(bf16[3,256,512]{2,1,0:T(8,128)(2,1)} %param.22) | copy-start | bytes 2359300
  40.1 12.4 %collective-permute-start.2 = (bf16[4,15,512]{2,1,0:T(8,128)(2,1)S(1)}, bf16[4,15,512]{2,1,0:T(8,128)(2,1)S(1)}, u32[]{:S(2)}, u32[]{:S(2)}) collective-permute-start(bf16[4,15,512]{2,1,0:T(8,128)(2,1)S(1)} %get-tuple-element.84), channel_id=1, source_target_pairs={{0,1},{1,2},{2,3},{3,4},{4,5},{5,6},{6,7},{8,9},{9,10},{10,11},{11... | collective-permute-start | bytes 184328 | tf_op jit(solution)/shard_map/ppermute | solution.py:413
  46.4 6.0 %collective-permute-start.3 = (bf16[4,15,512]{2,1,0:T(8,128)(2,1)S(1)}, bf16[4,15,512]{2,1,0:T(8,128)(2,1)S(1)}, u32[]{:S(2)}, u32[]{:S(2)}) collective-permute-start(bf16[4,15,512]{2,1,0:T(8,128)(2,1)S(1)} %get-tuple-element.85), channel_id=1, source_target_pairs={{1,0},{2,1},{3,2},{4,3},{5,4},{6,5},{7,6},{9,8},{10,9},{11,10},{12... | collective-permute-start | bytes 184328 | tf_op jit(solution)/shard_map/ppermute | solution.py:415
  48.4 1.0 copy-start.12
  49.4 1.8 copy-start.18
  51.2 1.8 copy-start.9
  54.0 19.8 %copy-start.1 = (bf16[4,384,512]{2,1,0:T(8,128)(2,1)}, bf16[4,384,512]{2,1,0:T(8,128)(2,1)S(1)}, u32[]{:S(2)}) copy-start(bf16[4,384,512]{2,1,0:T(8,128)(2,1)S(1)} %pad.31.win_ref) | copy-start | bytes 4718596
  77.7 4.9 %copy-start.10 = (f32[4,256]{1,0:T(4,128)S(1)}, f32[4,256]{1,0:T(4,128)}, u32[]{:S(2)}) copy-start(f32[4,256]{1,0:T(4,128)} %copy-done.9) | copy-start | bytes 12292
  90.6 4.1 %copy-start.2 = (bf16[4,256,512]{2,1,0:T(8,128)(2,1)S(1)}, bf16[4,256,512]{2,1,0:T(8,128)(2,1)}, u32[]{:S(2)}) copy-start(bf16[4,256,512]{2,1,0:T(8,128)(2,1)} %get-tuple-element.98.ev_ref) | copy-start | bytes 3145732
  90.6 4.1 %copy-start.3 = (f32[4,256,512]{2,1,0:T(8,128)S(1)}, f32[4,256,512]{2,1,0:T(8,128)}, u32[]{:S(2)}) copy-start(f32[4,256,512]{2,1,0:T(8,128)} %get-tuple-element.64) | copy-start | bytes 6291460
  92.8 13.6 %collective-permute-start.4 = (f32[4,15,512]{2,1,0:T(8,128)S(1)}, f32[4,15,512]{2,1,0:T(8,128)S(1)}, u32[]{:S(2)}, u32[]{:S(2)}) collective-permute-start(f32[4,15,512]{2,1,0:T(8,128)S(1)} %get-tuple-element.80), channel_id=1, source_target_pairs={{1,0},{2,1},{3,2},{4,3},{5,4},{6,5},{7,6},{9,8},{10,9},{11,10},{12... | collective-permute-start | bytes 368648 | tf_op jit(solution)/shard_map/ppermute | solution.py:425
  94.7 1.6 copy-start.19
  96.3 1.8 copy-start.13
  98.1 1.4 copy-start.6
  102.5 5.6 %collective-permute-start.5 = (f32[4,15,512]{2,1,0:T(8,128)S(1)}, f32[4,15,512]{2,1,0:T(8,128)S(1)}, u32[]{:S(2)}, u32[]{:S(2)}) collective-permute-start(f32[4,15,512]{2,1,0:T(8,128)S(1)} %get-tuple-element.79), channel_id=1, source_target_pairs={{0,1},{1,2},{2,3},{3,4},{4,5},{5,6},{6,7},{8,9},{9,10},{10,11},{11... | collective-permute-start | bytes 368648 | tf_op jit(solution)/shard_map/ppermute | solution.py:425
  108.5 1.6 copy-start.17
  110.1 1.0 copy-start.15
  111.1 1.4 copy-start.5
  112.5 1.4 copy-start.4
  112.5 1.7 copy-start.7

commit v6 on v5

--- a/solution.py
+++ b/solution.py
@@ -326,8 +326,12 @@
 def _corr_fwd_kernel(ev_ref, win_ref, inv_ref, dots_ref, strip_ref):
     wide = win_ref.shape[0]
     lanes = dots_ref.shape[1]
+    rows = lax.broadcasted_iota(jnp.int32, (wide, wide), 0)
+    cols = lax.broadcasted_iota(jnp.int32, (wide, wide), 1)
+    flip = (rows + cols == wide - 1).astype(jnp.bfloat16)
+    win_rev = jnp.dot(flip, win_ref[...], preferred_element_type=jnp.float32).astype(jnp.bfloat16)
     m = lax.dot_general(
-        ev_ref[...], win_ref[...], (((1,), (1,)), ((), ())), preferred_element_type=jnp.float32
+        ev_ref[...], win_rev, (((1,), (1,)), ((), ())), preferred_element_type=jnp.float32
     )
     dots_ref[...] = pltpu.roll(m, 0, 1, stride=1, stride_axis=0)[:, wide - lanes :]
     inv = jnp.broadcast_to(inv_ref[...], m.shape)
@@ -505,7 +509,7 @@
     wide_pad = -(-wide_len // 128) * 128
     win_pad = jnp.pad(window, ((0, 0), (0, wide_pad - wide_len), (0, 0)))
     inv_pad = jnp.pad(inv_win, ((0, 0), (0, wide_pad - wide_len)))[:, None, :]
-    dots_rev, strip_rev = corr_fwd(emb_v, win_pad[:, ::-1], inv_pad[:, :, ::-1])
+    dots_rev, strip_rev = corr_fwd(emb_v, win_pad, inv_pad[:, :, ::-1])
     lagged_inner_terms = dots_rev[:, :, ::-1][:, :, :offsets]
     reciprocal_lag_strip = strip_rev[:, :, ::-1][:, :, :offsets]
     frame_ids = first_frame + jnp.arange(frame_num, dtype=jnp.int32)

time: 223 us -> 209 us (0.937)
  local copies, waits for them, and re-layouts: 35.5 us -> 21.2 us
    rev x2 -> x1, local copies, waits for them, and re-layouts: 16 us -> 0.61 us  [shards(): dots_rev, strip_rev = corr_fwd(emb_v, win_pad, inv_pad[:, :, ::-1])]
    unnamed x40 -> x38, local copies, waits for them, and re-layouts: 4.92 us -> 4.91 us
  transfers between devices with their start and end apart: 6 -> 6, of which waited for: 1 -> 1; matrix products, arithmetic and copies ran while one was open for 8% -> 9% of each run, Pallas kernels for 8% -> 8%
where the time goes in v6:
time: 209 us; the launch traced here: 208 us
  Pallas kernels  127 us (61%)
  other arithmetic  21.7 us (10%)
  local copies, waits for them, and re-layouts  21.2 us (10%)
  starting transfers between devices  20.8 us (10%)
  matrix products  12.4 us (6%)
  between operations  3.5 us (2%)
    pallas_call x1, Pallas kernels, all_sum(): pl.pallas_call(functools.partial(_kernel, rows), out_shape=(jax.ShapeDtyp...  98.9 us
    pallas_call x1, Pallas kernels, small_sum(): pl.pallas_call(functools.partial(_small_kernel, names), out_shape=jax.Sha...  17.4 us
    ppermute x2, starting transfers between devices, padded_2(): lax.ppermute(tail, axis, [(i, (i + 1) % count) for i in range(ends)])  11.3 us
    ppermute x2, starting transfers between devices, from_behind(): lax.ppermute(value, axis, [(source, source + steps) for source in range(i...  5.74 us
    pallas_call x1, Pallas kernels, corr_bwd(): pl.pallas_call(_corr_bwd_kernel, grid=(clips,), in_specs=[pl.BlockSpec((N...  5.44 us
    pallas_call x1, Pallas kernels, corr_fwd(): pl.pallas_call(_corr_fwd_kernel, grid=(clips,), in_specs=[pl.BlockSpec((N...  5.12 us
    unnamed x38, local copies, waits for them, and re-layouts  4.91 us
  transfers between devices with their start and end apart: 6, of which 1 were waited for; matrix products, arithmetic and copies ran while one was open for 9% of the time, Pallas kernels for 8%

profile of v6, /device:TPU:1, one launch (start us, length us, event | category | flops | bytes accessed | tf_op | source)
XLA Modules:
  0.0 208.0 jit_solution(14196986968059729960)
XLA Ops:
  0.6 0.9 pad_maximum_fusion.6
  1.5 4.9 %collective-permute-start = (bf16[2,4,1,256]{3,2,1,0:T(2,128)(2,1)S(1)}, bf16[2,4,1,256]{3,2,1,0:T(2,128)(2,1)S(1)}, u32[]{:S(2)}, u32[]{:S(2)}) collective-permute-start(bf16[2,4,1,256]{3,2,1,0:T(2,128)(2,1)S(1)} %get-tuple-element.86), channel_id=1, source_target_pairs={{0,1},{1,2},{2,3},{3,4},{4,5},{5,6},{6,7},{8,9},{9,10},{10,11},{11... | collective-permute-start | bytes 12296 | tf_op jit(solution)/shard_map/ppermute | solution.py:417
  6.5 1.9 collective-permute-start.1
  8.4 0.7 broadcast_compare_fusion
  9.1 0.8 broadcast_add_fusion
  9.9 1.3 broadcast_compare_fusion.1
  11.2 1.3 compare_convert_fusion
  12.5 1.3 subtract_reduce_fusion
  13.8 1.2 scatter.6.t_ref
  15.0 17.4 %shard_map.119 = s32[8,128]{1,0:T(8,128)} custom-call(s32[8,128]{1,0:T(8,128)} %scatter.6.t_ref), custom_call_target="tpu_custom_call" | custom-call | tf_op jit(solution)/shard_map/pallas_call | solution.py:118
  32.4 1.2 slice.168
  34.3 1.5 pad_maximum_fusion.4
  35.9 0.6 fusion.34
  36.5 1.2 pad_maximum_fusion.1
  37.7 1.0 fusion.28
  38.7 0.7 convolution_convert_fusion
  39.5 0.6 copy-done.15
  40.1 6.3 %collective-permute-start.2 = (bf16[4,15,512]{2,1,0:T(8,128)(2,1)S(1)}, bf16[4,15,512]{2,1,0:T(8,128)(2,1)S(1)}, u32[]{:S(2)}, u32[]{:S(2)}) collective-permute-start(bf16[4,15,512]{2,1,0:T(8,128)(2,1)S(1)} %get-tuple-element.84), channel_id=1, source_target_pairs={{0,1},{1,2},{2,3},{3,4},{4,5},{5,6},{6,7},{8,9},{9,10},{10,11},{11... | collective-permute-start | bytes 184328 | tf_op jit(solution)/shard_map/ppermute | solution.py:417
  46.4 1.9 collective-permute-start.3
  48.4 1.0 fusion.27
  49.4 1.8 fusion.2
  51.2 1.2 pad_maximum_fusion.2
  52.5 0.5 fusion
  53.0 0.3 reverse.5
  53.3 0.6 copy.13.inv_ref
  53.9 1.3 pad.31.win_ref
  55.2 5.1 %shard_map.120 = (f32[4,256,128]{2,1,0:T(8,128)}, f32[4,256,128]{2,1,0:T(8,128)}) custom-call(bf16[4,256,512]{2,1,0:T(8,128)(2,1)} %get-tuple-element.98.ev_ref, bf16[4,384,512]{2,1,0:T(8,128)(2,1)} %pad.31.win_ref, f32[4,1,384]{2,1,0:T(1,128)} %copy.13.inv_ref), custom_call_target="tpu_custom_call" | custom-call | tf_op jit(solution)/shard_map/pallas_call | solution.py:345
  60.3 1.2 slice.175
  61.5 0.7 slice.176
  62.3 1.3 slice.177
  63.5 0.7 slice.178
  64.3 1.6 multiply_reduce_fusion
  65.9 1.3 select_reduce_fusion
  67.2 1.9 multiply_reduce_fusion.1
  69.1 0.8 pad.33.gd_ref
  70.1 0.8 pad.34.at_ref
  70.9 5.4 %shard_map.121 = (f32[4,256,512]{2,1,0:T(8,128)}, f32[4,384,512]{2,1,0:T(8,128)}, f32[4,1,384]{2,1,0:T(1,128)}) custom-call(bf16[4,256,128]{2,1,0:T(8,128)(2,1)} %pad.33.gd_ref, f32[4,256,128]{2,1,0:T(8,128)} %pad.34.at_ref, bf16[4,256,512]{2,1,0:T(8,128)(2,1)} %get-tuple-element.98.ev_ref, bf16[4,384,512]{2,1,0:T(8,128)(2,1)} %pad.31.win_ref), custom_call_target="tpu_custom_call" | custom-call | tf_op jit(solution)/shard_map/pallas_call | solution.py:382
  76.3 0.7 fusion.23
  77.1 2.1 %fusion.1 = f32[4,286,512]{2,1,0:T(8,128)S(1)} fusion(bf16[4,286,512]{2,1,0:T(8,128)(2,1)S(1)} %get-tuple-element.74, f32[4,384,512]{2,1,0:T(8,128)} %get-tuple-element.62, f32[4,286]{1,0:T(4,128)S(1)} %fusion.23), kind=kLoop, calls=%fused_computation.6 | loop fusion | flops 1757184 | bytes 5861856 | tf_op jit(solution)/shard_map/sub | solution.py:561
  79.2 1.9 collective-permute-start.4
  81.2 0.3 fusion.4
  81.5 1.3 copy-done.18
  82.7 1.7 convolution_bitcast_fusion
  84.5 1.2 fusion.11
  85.7 0.2 copy-done.5
  85.9 2.1 %fusion.37 = f32[768,512]{1,0:T(8,128)} fusion(bf16[1024,768]{1,0:T(8,128)(2,1)S(1)} %bitcast.94, bf16[1024,512]{1,0:T(8,128)(2,1)S(1)} %fusion.11), kind=kOutput, calls=%fused_computation.85 | convolution fusion | flops 805306368 | bytes 4194304 | tf_op jit(solution)/shard_map/rk,re->ke/dot_general | solution.py:485
  88.1 0.3 slice.201
  88.3 0.6 scatter.9.t_ref
  88.9 3.8 %collective-permute-start.5 = (f32[4,15,512]{2,1,0:T(8,128)S(1)}, f32[4,15,512]{2,1,0:T(8,128)S(1)}, u32[]{:S(2)}, u32[]{:S(2)}) collective-permute-start(f32[4,15,512]{2,1,0:T(8,128)S(1)} %get-tuple-element.79), channel_id=1, source_target_pairs={{0,1},{1,2},{2,3},{3,4},{4,5},{5,6},{6,7},{8,9},{9,10},{10,11},{11... | collective-permute-start | bytes 368648 | tf_op jit(solution)/shard_map/ppermute | solution.py:429
  92.8 0.3 scatter-add.6
  93.0 1.4 collective-permute-done.5
  94.5 0.4 scatter-add.9
  95.0 1.4 copy-done.16
  96.5 0.8 convolution_bitcast_fusion.1
  97.2 0.3 copy-done.14
  97.5 1.2 fusion.18
  98.9 1.0 fusion.36
  99.9 0.4 copy-done.3
  100.3 0.3 copy-done.6
  100.6 2.7 %pad_maximum_fusion.x_ref = f32[2560,512]{1,0:T(8,128)} fusion(f32[512,512]{1,0:T(8,128)S(1)} %copy-done.6, f32[512,512]{1,0:T(8,128)S(1)} %convolution_bitcast_fusion.1, f32[768,512]{1,0:T(8,128)S(1)} %copy-done.3, f32[768,512]{1,0:T(8,128)S(1)} %fusion.36), kind=kLoop, calls=%fused_computation | loop fusion | flops 3932160 | bytes 10485760 | tf_op jit(solution)/shard_map/concatenate | solution.py:577
  103.3 98.9 %shard_map.122 = (f32[2560,512]{1,0:T(8,128)S(1)}, f32[8,128]{1,0:T(8,128)S(1)}) custom-call(f32[2560,512]{1,0:T(8,128)} %pad_maximum_fusion.x_ref, f32[8,128]{1,0:T(8,128)S(1)} %scatter.9.t_ref), custom_call_target="tpu_custom_call" | custom-call | tf_op jit(solution)/shard_map/pallas_call | solution.py:302
  202.2 1.5 fusion.30
  203.7 2.0 fusion.31
  205.7 0.5 slice.186
  (49 shorter events, 1.0 us)
Async XLA Ops:
  0.6 37.1 %copy-start = (bf16[3,256,512]{2,1,0:T(8,128)(2,1)S(1)}, bf16[3,256,512]{2,1,0:T(8,128)(2,1)}, u32[]{:S(2)}) copy-start(bf16[3,256,512]{2,1,0:T(8,128)(2,1)} %param.20) | copy-start | bytes 2359300
  1.5 32.8 %collective-permute-start = (bf16[2,4,1,256]{3,2,1,0:T(2,128)(2,1)S(1)}, bf16[2,4,1,256]{3,2,1,0:T(2,128)(2,1)S(1)}, u32[]{:S(2)}, u32[]{:S(2)}) collective-permute-start(bf16[2,4,1,256]{3,2,1,0:T(2,128)(2,1)S(1)} %get-tuple-element.86), channel_id=1, source_target_pairs={{0,1},{1,2},{2,3},{3,4},{4,5},{5,6},{6,7},{8,9},{9,10},{10,11},{11... | collective-permute-start | bytes 12296 | tf_op jit(solution)/shard_map/ppermute | solution.py:417
  6.5 27.8 %collective-permute-start.1 = (bf16[2,4,1,256]{3,2,1,0:T(2,128)(2,1)S(1)}, bf16[2,4,1,256]{3,2,1,0:T(2,128)(2,1)S(1)}, u32[]{:S(2)}, u32[]{:S(2)}) collective-permute-start(bf16[2,4,1,256]{3,2,1,0:T(2,128)(2,1)S(1)} %get-tuple-element.87), channel_id=1, source_target_pairs={{1,0},{2,1},{3,2},{4,3},{5,4},{6,5},{7,6},{9,8},{10,9},{11,10},{12... | collective-permute-start | bytes 12296 | tf_op jit(solution)/shard_map/ppermute | solution.py:419
  8.4 1.5 copy-start.7
  37.7 1.0 copy-start.13
  38.7 1.4 copy-start.15
  38.7 9.6 %copy-start.10 = (bf16[3,256,512]{2,1,0:T(8,128)(2,1)S(1)}, bf16[3,256,512]{2,1,0:T(8,128)(2,1)}, u32[]{:S(2)}) copy-start(bf16[3,256,512]{2,1,0:T(8,128)(2,1)} %param.22) | copy-start | bytes 2359300
  40.1 12.3 %collective-permute-start.2 = (bf16[4,15,512]{2,1,0:T(8,128)(2,1)S(1)}, bf16[4,15,512]{2,1,0:T(8,128)(2,1)S(1)}, u32[]{:S(2)}, u32[]{:S(2)}) collective-permute-start(bf16[4,15,512]{2,1,0:T(8,128)(2,1)S(1)} %get-tuple-element.84), channel_id=1, source_target_pairs={{0,1},{1,2},{2,3},{3,4},{4,5},{5,6},{6,7},{8,9},{9,10},{10,11},{11... | collective-permute-start | bytes 184328 | tf_op jit(solution)/shard_map/ppermute | solution.py:417
  46.4 6.0 %collective-permute-start.3 = (bf16[4,15,512]{2,1,0:T(8,128)(2,1)S(1)}, bf16[4,15,512]{2,1,0:T(8,128)(2,1)S(1)}, u32[]{:S(2)}, u32[]{:S(2)}) collective-permute-start(bf16[4,15,512]{2,1,0:T(8,128)(2,1)S(1)} %get-tuple-element.85), channel_id=1, source_target_pairs={{1,0},{2,1},{3,2},{4,3},{5,4},{6,5},{7,6},{9,8},{10,9},{11,10},{12... | collective-permute-start | bytes 184328 | tf_op jit(solution)/shard_map/ppermute | solution.py:419
  48.4 1.0 copy-start.11
  49.4 1.8 copy-start.17
  51.2 1.8 copy-start.8
  64.2 4.8 %copy-start.9 = (f32[4,256]{1,0:T(4,128)S(1)}, f32[4,256]{1,0:T(4,128)}, u32[]{:S(2)}) copy-start(f32[4,256]{1,0:T(4,128)} %copy-done.8) | copy-start | bytes 12292
  77.0 4.1 %copy-start.1 = (bf16[4,256,512]{2,1,0:T(8,128)(2,1)S(1)}, bf16[4,256,512]{2,1,0:T(8,128)(2,1)}, u32[]{:S(2)}) copy-start(bf16[4,256,512]{2,1,0:T(8,128)(2,1)} %get-tuple-element.98.ev_ref) | copy-start | bytes 3145732
  77.0 4.1 %copy-start.2 = (f32[4,256,512]{2,1,0:T(8,128)S(1)}, f32[4,256,512]{2,1,0:T(8,128)}, u32[]{:S(2)}) copy-start(f32[4,256,512]{2,1,0:T(8,128)} %get-tuple-element.64) | copy-start | bytes 6291460
  79.2 13.5 %collective-permute-start.4 = (f32[4,15,512]{2,1,0:T(8,128)S(1)}, f32[4,15,512]{2,1,0:T(8,128)S(1)}, u32[]{:S(2)}, u32[]{:S(2)}) collective-permute-start(f32[4,15,512]{2,1,0:T(8,128)S(1)} %get-tuple-element.80), channel_id=1, source_target_pairs={{1,0},{2,1},{3,2},{4,3},{5,4},{6,5},{7,6},{9,8},{10,9},{11,10},{12... | collective-permute-start | bytes 368648 | tf_op jit(solution)/shard_map/ppermute | solution.py:429
  81.2 1.6 copy-start.18
  82.7 1.8 copy-start.12
  84.5 1.4 copy-start.5
  88.9 5.6 %collective-permute-start.5 = (f32[4,15,512]{2,1,0:T(8,128)S(1)}, f32[4,15,512]{2,1,0:T(8,128)S(1)}, u32[]{:S(2)}, u32[]{:S(2)}) collective-permute-start(f32[4,15,512]{2,1,0:T(8,128)S(1)} %get-tuple-element.79), channel_id=1, source_target_pairs={{0,1},{1,2},{2,3},{3,4},{4,5},{5,6},{6,7},{8,9},{9,10},{10,11},{11... | collective-permute-start | bytes 368648 | tf_op jit(solution)/shard_map/ppermute | solution.py:429
  94.9 1.6 copy-start.16
  96.5 1.0 copy-start.14
  97.5 1.4 copy-start.4
  98.9 1.4 copy-start.3
  98.9 1.7 copy-start.6

commit v7 on v6

--- a/solution.py
+++ b/solution.py
@@ -204,7 +204,7 @@
     return c
 
 
-def _kernel(rows, x_ref, t_ref, o_ref, to_ref, work, rbuf, zbuf, send_sem, recv_sem, tbuf, tsend, trecv):
+def _kernel(rows, x_ref, t_ref, o_ref, to_ref, work, rbuf, zbuf, send_sem, recv_sem, tbuf, tsend, trecv, half_ref, hsend, hrecv):
     table = _levels()
     lc, ly, lx, lz = (table[k] for k in ("c", "y", "x", "z"))
     _barrier([lc, ly, lx, lz])
@@ -283,15 +283,19 @@
         o_ref[pl.ds(pl.multiple_of(at, 8), c2)] = acc
     tiny_done(nz)
     sem = _ag_stage([(nx, xi, nbx, 1, a2, c1, None), (ny, yi, nby, 1, b2, c1, None)], o_ref, send_sem, recv_sem, sem)
-    sem = _ag_stage([(ny, yi, nby, 2, a1, quarter, None), (nx, xi, nbx, 2, b1, quarter, None)], o_ref, send_sem, recv_sem, sem)
-    sem = _ag_stage([(nc, core, nbc, 1, 0, rows, None)], o_ref, send_sem, recv_sem, sem)
+    for at in (a2, b2):
+        region = pl.ds(pl.multiple_of(at, 16), c1)
+        half_ref[region] = o_ref[region].astype(half_ref.dtype)
+    sem = _ag_stage([(ny, yi, nby, 2, a1, quarter, None), (nx, xi, nbx, 2, b1, quarter, None)], half_ref, hsend, hrecv, 0)
+    _ag_stage([(nc, core, nbc, 1, 0, rows, None)], half_ref, hsend, hrecv, sem)
+    o_ref[...] = half_ref[...].astype(o_ref.dtype)
 
 
 def _counts(rows):
     half, quarter = rows // 2, rows // 4
     c1 = quarter // 4
     slots = half + 3 * 2 * quarter // 4 + 3 * 2 * c1 // 4
-    sems = 1 + 3 * 4 + 3 * 2 + 7 + 3 * 2 + 3 * 4 + 1
+    sems = 1 + 3 * 4 + 3 * 2 + 7 + 3 * 2
     return slots, sems, 2 + 4 + 4 + 8, 1 + 3 + 3 + 7
 
 
@@ -316,6 +320,9 @@
             pltpu.VMEM((tslots,) + small.shape, small.dtype),
             pltpu.SemaphoreType.DMA((tsems,)),
             pltpu.SemaphoreType.DMA((tsems,)),
+            pltpu.VMEM(flat.shape, jnp.bfloat16),
+            pltpu.SemaphoreType.DMA((13,)),
+            pltpu.SemaphoreType.DMA((13,)),
         ],
         compiler_params=pltpu.CompilerParams(
             collective_id=0, has_side_effects=True, vmem_limit_bytes=48 * 1024 * 1024

time: 209 us -> 202 us (0.967)
  Pallas kernels: 127 us -> 120 us
    pallas_call x1, Pallas kernels: 98.9 us -> 92.3 us  [all_sum(): pl.pallas_call(functools.partial(_kernel, rows), out_shape=(jax.ShapeDtyp...]
  transfers between devices with their start and end apart: 6 -> 6, of which waited for: 1 -> 1; matrix products, arithmetic and copies ran while one was open for 9% -> 9% of each run, Pallas kernels for 8% -> 9%
where the time goes in v7:
time: 202 us; the launch traced here: 201 us
  Pallas kernels  120 us (59%)
  other arithmetic  21.7 us (11%)
  local copies, waits for them, and re-layouts  21.2 us (10%)
  starting transfers between devices  20.8 us (10%)
  matrix products  12.4 us (6%)
  between operations  3.5 us (2%)
    pallas_call x1, Pallas kernels, all_sum(): pl.pallas_call(functools.partial(_kernel, rows), out_shape=(jax.ShapeDtyp...  92.3 us
    pallas_call x1, Pallas kernels, small_sum(): pl.pallas_call(functools.partial(_small_kernel, names), out_shape=jax.Sha...  17.4 us
    ppermute x2, starting transfers between devices, padded_2(): lax.ppermute(tail, axis, [(i, (i + 1) % count) for i in range(ends)])  11.3 us
    ppermute x2, starting transfers between devices, from_behind(): lax.ppermute(value, axis, [(source, source + steps) for source in range(i...  5.74 us
    pallas_call x1, Pallas kernels, corr_bwd(): pl.pallas_call(_corr_bwd_kernel, grid=(clips,), in_specs=[pl.BlockSpec((N...  5.44 us
    pallas_call x1, Pallas kernels, corr_fwd(): pl.pallas_call(_corr_fwd_kernel, grid=(clips,), in_specs=[pl.BlockSpec((N...  5.12 us
    unnamed x38, local copies, waits for them, and re-layouts  4.91 us
  transfers between devices with their start and end apart: 6, of which 1 were waited for; matrix products, arithmetic and copies ran while one was open for 9% of the time, Pallas kernels for 9%

profile of v7, /device:TPU:1, one launch (start us, length us, event | category | flops | bytes accessed | tf_op | source)
XLA Modules:
  0.0 201.4 jit_solution(2517766382531136926)
XLA Ops:
  0.6 0.9 pad_maximum_fusion.6
  1.5 4.9 %collective-permute-start = (bf16[2,4,1,256]{3,2,1,0:T(2,128)(2,1)S(1)}, bf16[2,4,1,256]{3,2,1,0:T(2,128)(2,1)S(1)}, u32[]{:S(2)}, u32[]{:S(2)}) collective-permute-start(bf16[2,4,1,256]{3,2,1,0:T(2,128)(2,1)S(1)} %get-tuple-element.86), channel_id=1, source_target_pairs={{0,1},{1,2},{2,3},{3,4},{4,5},{5,6},{6,7},{8,9},{9,10},{10,11},{11... | collective-permute-start | bytes 12296 | tf_op jit(solution)/shard_map/ppermute | solution.py:424
  6.5 1.9 collective-permute-start.1
  8.4 0.7 broadcast_compare_fusion
  9.1 0.8 broadcast_add_fusion
  9.9 1.3 broadcast_compare_fusion.1
  11.2 1.3 compare_convert_fusion
  12.5 1.3 subtract_reduce_fusion
  13.8 1.2 scatter.6.t_ref
  15.0 17.4 %shard_map.119 = s32[8,128]{1,0:T(8,128)} custom-call(s32[8,128]{1,0:T(8,128)} %scatter.6.t_ref), custom_call_target="tpu_custom_call" | custom-call | tf_op jit(solution)/shard_map/pallas_call | solution.py:118
  32.4 1.2 slice.168
  34.3 1.5 pad_maximum_fusion.4
  35.9 0.6 fusion.34
  36.5 1.2 pad_maximum_fusion.1
  37.7 1.0 fusion.28
  38.7 0.7 convolution_convert_fusion
  39.5 0.6 copy-done.15
  40.1 6.3 %collective-permute-start.2 = (bf16[4,15,512]{2,1,0:T(8,128)(2,1)S(1)}, bf16[4,15,512]{2,1,0:T(8,128)(2,1)S(1)}, u32[]{:S(2)}, u32[]{:S(2)}) collective-permute-start(bf16[4,15,512]{2,1,0:T(8,128)(2,1)S(1)} %get-tuple-element.84), channel_id=1, source_target_pairs={{0,1},{1,2},{2,3},{3,4},{4,5},{5,6},{6,7},{8,9},{9,10},{10,11},{11... | collective-permute-start | bytes 184328 | tf_op jit(solution)/shard_map/ppermute | solution.py:424
  46.4 1.9 collective-permute-start.3
  48.4 1.0 fusion.27
  49.4 1.8 fusion.2
  51.2 1.2 pad_maximum_fusion.2
  52.5 0.5 fusion
  53.0 0.3 reverse.5
  53.3 0.6 copy.13.inv_ref
  53.9 1.3 pad.31.win_ref
  55.2 5.1 %shard_map.120 = (f32[4,256,128]{2,1,0:T(8,128)}, f32[4,256,128]{2,1,0:T(8,128)}) custom-call(bf16[4,256,512]{2,1,0:T(8,128)(2,1)} %get-tuple-element.98.ev_ref, bf16[4,384,512]{2,1,0:T(8,128)(2,1)} %pad.31.win_ref, f32[4,1,384]{2,1,0:T(1,128)} %copy.13.inv_ref), custom_call_target="tpu_custom_call" | custom-call | tf_op jit(solution)/shard_map/pallas_call | solution.py:352
  60.3 1.2 slice.175
  61.5 0.7 slice.176
  62.3 1.3 slice.177
  63.5 0.7 slice.178
  64.3 1.6 multiply_reduce_fusion
  65.9 1.3 select_reduce_fusion
  67.2 1.9 multiply_reduce_fusion.1
  69.1 0.8 pad.33.gd_ref
  70.1 0.8 pad.34.at_ref
  70.9 5.4 %shard_map.121 = (f32[4,256,512]{2,1,0:T(8,128)}, f32[4,384,512]{2,1,0:T(8,128)}, f32[4,1,384]{2,1,0:T(1,128)}) custom-call(bf16[4,256,128]{2,1,0:T(8,128)(2,1)} %pad.33.gd_ref, f32[4,256,128]{2,1,0:T(8,128)} %pad.34.at_ref, bf16[4,256,512]{2,1,0:T(8,128)(2,1)} %get-tuple-element.98.ev_ref, bf16[4,384,512]{2,1,0:T(8,128)(2,1)} %pad.31.win_ref), custom_call_target="tpu_custom_call" | custom-call | tf_op jit(solution)/shard_map/pallas_call | solution.py:389
  76.3 0.7 fusion.23
  77.1 2.1 %fusion.1 = f32[4,286,512]{2,1,0:T(8,128)S(1)} fusion(bf16[4,286,512]{2,1,0:T(8,128)(2,1)S(1)} %get-tuple-element.74, f32[4,384,512]{2,1,0:T(8,128)} %get-tuple-element.62, f32[4,286]{1,0:T(4,128)S(1)} %fusion.23), kind=kLoop, calls=%fused_computation.6 | loop fusion | flops 1757184 | bytes 5861856 | tf_op jit(solution)/shard_map/sub | solution.py:568
  79.2 1.9 collective-permute-start.4
  81.2 0.3 fusion.4
  81.5 1.3 copy-done.18
  82.7 1.7 convolution_bitcast_fusion
  84.5 1.2 fusion.11
  85.7 0.2 copy-done.5
  85.9 2.1 %fusion.37 = f32[768,512]{1,0:T(8,128)} fusion(bf16[1024,768]{1,0:T(8,128)(2,1)S(1)} %bitcast.94, bf16[1024,512]{1,0:T(8,128)(2,1)S(1)} %fusion.11), kind=kOutput, calls=%fused_computation.85 | convolution fusion | flops 805306368 | bytes 4194304 | tf_op jit(solution)/shard_map/rk,re->ke/dot_general | solution.py:492
  88.1 0.3 slice.201
  88.3 0.6 scatter.9.t_ref
  88.9 3.8 %collective-permute-start.5 = (f32[4,15,512]{2,1,0:T(8,128)S(1)}, f32[4,15,512]{2,1,0:T(8,128)S(1)}, u32[]{:S(2)}, u32[]{:S(2)}) collective-permute-start(f32[4,15,512]{2,1,0:T(8,128)S(1)} %get-tuple-element.79), channel_id=1, source_target_pairs={{0,1},{1,2},{2,3},{3,4},{4,5},{5,6},{6,7},{8,9},{9,10},{10,11},{11... | collective-permute-start | bytes 368648 | tf_op jit(solution)/shard_map/ppermute | solution.py:436
  92.8 0.3 scatter-add.6
  93.0 1.4 collective-permute-done.5
  94.5 0.4 scatter-add.9
  95.0 1.4 copy-done.16
  96.5 0.8 convolution_bitcast_fusion.1
  97.2 0.3 copy-done.14
  97.5 1.2 fusion.18
  98.9 1.0 fusion.36
  99.9 0.4 copy-done.3
  100.3 0.3 copy-done.6
  100.6 2.7 %pad_maximum_fusion.x_ref = f32[2560,512]{1,0:T(8,128)} fusion(f32[512,512]{1,0:T(8,128)S(1)} %copy-done.6, f32[512,512]{1,0:T(8,128)S(1)} %convolution_bitcast_fusion.1, f32[768,512]{1,0:T(8,128)S(1)} %copy-done.3, f32[768,512]{1,0:T(8,128)S(1)} %fusion.36), kind=kLoop, calls=%fused_computation | loop fusion | flops 3932160 | bytes 10485760 | tf_op jit(solution)/shard_map/concatenate | solution.py:584
  103.3 92.3 %shard_map.122 = (f32[2560,512]{1,0:T(8,128)S(1)}, f32[8,128]{1,0:T(8,128)S(1)}) custom-call(f32[2560,512]{1,0:T(8,128)} %pad_maximum_fusion.x_ref, f32[8,128]{1,0:T(8,128)S(1)} %scatter.9.t_ref), custom_call_target="tpu_custom_call" | custom-call | tf_op jit(solution)/shard_map/pallas_call | solution.py:306
  195.6 1.5 fusion.30
  197.1 2.0 fusion.31
  199.1 0.5 slice.186
  (49 shorter events, 1.0 us)
Async XLA Ops:
  0.6 37.1 %copy-start = (bf16[3,256,512]{2,1,0:T(8,128)(2,1)S(1)}, bf16[3,256,512]{2,1,0:T(8,128)(2,1)}, u32[]{:S(2)}) copy-start(bf16[3,256,512]{2,1,0:T(8,128)(2,1)} %param.20) | copy-start | bytes 2359300
  1.5 32.8 %collective-permute-start = (bf16[2,4,1,256]{3,2,1,0:T(2,128)(2,1)S(1)}, bf16[2,4,1,256]{3,2,1,0:T(2,128)(2,1)S(1)}, u32[]{:S(2)}, u32[]{:S(2)}) collective-permute-start(bf16[2,4,1,256]{3,2,1,0:T(2,128)(2,1)S(1)} %get-tuple-element.86), channel_id=1, source_target_pairs={{0,1},{1,2},{2,3},{3,4},{4,5},{5,6},{6,7},{8,9},{9,10},{10,11},{11... | collective-permute-start | bytes 12296 | tf_op jit(solution)/shard_map/ppermute | solution.py:424
  6.5 27.8 %collective-permute-start.1 = (bf16[2,4,1,256]{3,2,1,0:T(2,128)(2,1)S(1)}, bf16[2,4,1,256]{3,2,1,0:T(2,128)(2,1)S(1)}, u32[]{:S(2)}, u32[]{:S(2)}) collective-permute-start(bf16[2,4,1,256]{3,2,1,0:T(2,128)(2,1)S(1)} %get-tuple-element.87), channel_id=1, source_target_pairs={{1,0},{2,1},{3,2},{4,3},{5,4},{6,5},{7,6},{9,8},{10,9},{11,10},{12... | collective-permute-start | bytes 12296 | tf_op jit(solution)/shard_map/ppermute | solution.py:426
  8.4 1.5 copy-start.7
  37.7 1.0 copy-start.13
  38.7 1.4 copy-start.15
  38.7 9.6 %copy-start.10 = (bf16[3,256,512]{2,1,0:T(8,128)(2,1)S(1)}, bf16[3,256,512]{2,1,0:T(8,128)(2,1)}, u32[]{:S(2)}) copy-start(bf16[3,256,512]{2,1,0:T(8,128)(2,1)} %param.22) | copy-start | bytes 2359300
  40.1 12.3 %collective-permute-start.2 = (bf16[4,15,512]{2,1,0:T(8,128)(2,1)S(1)}, bf16[4,15,512]{2,1,0:T(8,128)(2,1)S(1)}, u32[]{:S(2)}, u32[]{:S(2)}) collective-permute-start(bf16[4,15,512]{2,1,0:T(8,128)(2,1)S(1)} %get-tuple-element.84), channel_id=1, source_target_pairs={{0,1},{1,2},{2,3},{3,4},{4,5},{5,6},{6,7},{8,9},{9,10},{10,11},{11... | collective-permute-start | bytes 184328 | tf_op jit(solution)/shard_map/ppermute | solution.py:424
  46.4 6.0 %collective-permute-start.3 = (bf16[4,15,512]{2,1,0:T(8,128)(2,1)S(1)}, bf16[4,15,512]{2,1,0:T(8,128)(2,1)S(1)}, u32[]{:S(2)}, u32[]{:S(2)}) collective-permute-start(bf16[4,15,512]{2,1,0:T(8,128)(2,1)S(1)} %get-tuple-element.85), channel_id=1, source_target_pairs={{1,0},{2,1},{3,2},{4,3},{5,4},{6,5},{7,6},{9,8},{10,9},{11,10},{12... | collective-permute-start | bytes 184328 | tf_op jit(solution)/shard_map/ppermute | solution.py:426
  48.4 1.0 copy-start.11
  49.4 1.8 copy-start.17
  51.2 1.8 copy-start.8
  64.2 4.8 %copy-start.9 = (f32[4,256]{1,0:T(4,128)S(1)}, f32[4,256]{1,0:T(4,128)}, u32[]{:S(2)}) copy-start(f32[4,256]{1,0:T(4,128)} %copy-done.8) | copy-start | bytes 12292
  77.0 4.1 %copy-start.1 = (bf16[4,256,512]{2,1,0:T(8,128)(2,1)S(1)}, bf16[4,256,512]{2,1,0:T(8,128)(2,1)}, u32[]{:S(2)}) copy-start(bf16[4,256,512]{2,1,0:T(8,128)(2,1)} %get-tuple-element.98.ev_ref) | copy-start | bytes 3145732
  77.0 4.1 %copy-start.2 = (f32[4,256,512]{2,1,0:T(8,128)S(1)}, f32[4,256,512]{2,1,0:T(8,128)}, u32[]{:S(2)}) copy-start(f32[4,256,512]{2,1,0:T(8,128)} %get-tuple-element.64) | copy-start | bytes 6291460
  79.2 13.5 %collective-permute-start.4 = (f32[4,15,512]{2,1,0:T(8,128)S(1)}, f32[4,15,512]{2,1,0:T(8,128)S(1)}, u32[]{:S(2)}, u32[]{:S(2)}) collective-permute-start(f32[4,15,512]{2,1,0:T(8,128)S(1)} %get-tuple-element.80), channel_id=1, source_target_pairs={{1,0},{2,1},{3,2},{4,3},{5,4},{6,5},{7,6},{9,8},{10,9},{11,10},{12... | collective-permute-start | bytes 368648 | tf_op jit(solution)/shard_map/ppermute | solution.py:436
  81.2 1.6 copy-start.18
  82.7 1.8 copy-start.12
  84.5 1.4 copy-start.5
  88.9 5.6 %collective-permute-start.5 = (f32[4,15,512]{2,1,0:T(8,128)S(1)}, f32[4,15,512]{2,1,0:T(8,128)S(1)}, u32[]{:S(2)}, u32[]{:S(2)}) collective-permute-start(f32[4,15,512]{2,1,0:T(8,128)S(1)} %get-tuple-element.79), channel_id=1, source_target_pairs={{0,1},{1,2},{2,3},{3,4},{4,5},{5,6},{6,7},{8,9},{9,10},{10,11},{11... | collective-permute-start | bytes 368648 | tf_op jit(solution)/shard_map/ppermute | solution.py:436
  94.9 1.6 copy-start.16
  96.5 1.0 copy-start.14
  97.5 1.4 copy-start.4
  98.9 1.4 copy-start.3
  98.9 1.7 copy-start.6

commit v8 on v7

--- a/solution.py
+++ b/solution.py
@@ -204,7 +204,16 @@
     return c
 
 
-def _kernel(rows, x_ref, t_ref, o_ref, to_ref, work, rbuf, zbuf, send_sem, recv_sem, tbuf, tsend, trecv, half_ref, hsend, hrecv):
+def _kernel(sizes, *refs):
+    parts = len(sizes)
+    ins, t_ref = refs[:parts], refs[parts]
+    outs, to_ref = refs[parts + 1 : 2 * parts + 1], refs[2 * parts + 1]
+    work, rbuf, zbuf, send_sem, recv_sem, tbuf, tsend, trecv, half_ref, hsend, hrecv, o_ref = refs[2 * parts + 2 :]
+    rows = sum(sizes)
+    start = 0
+    for size, in_ref in zip(sizes, ins):
+        work[start : start + size] = in_ref[...]
+        start += size
     table = _levels()
     lc, ly, lx, lz = (table[k] for k in ("c", "y", "x", "z"))
     _barrier([lc, ly, lx, lz])
@@ -236,7 +245,7 @@
     nz, zi, nbz, _ = lz
 
     rider = tiny_level(lc, True)
-    slot, sem = _rs_stage([(nc, core, nbc, 1, 0, rows, x_ref)], work, rbuf, send_sem, recv_sem, slot, sem, rider)
+    slot, sem = _rs_stage([(nc, core, nbc, 1, 0, rows, work)], work, rbuf, send_sem, recv_sem, slot, sem, rider)
     tiny_done(nc)
     r0 = core * half
     a1, b1 = r0, r0 + quarter
@@ -288,7 +297,10 @@
         half_ref[region] = o_ref[region].astype(half_ref.dtype)
     sem = _ag_stage([(ny, yi, nby, 2, a1, quarter, None), (nx, xi, nbx, 2, b1, quarter, None)], half_ref, hsend, hrecv, 0)
     _ag_stage([(nc, core, nbc, 1, 0, rows, None)], half_ref, hsend, hrecv, sem)
-    o_ref[...] = half_ref[...].astype(o_ref.dtype)
+    start = 0
+    for size, out_ref in zip(sizes, outs):
+        out_ref[...] = half_ref[start : start + size].astype(out_ref.dtype)
+        start += size
 
 
 def _counts(rows):
@@ -299,35 +311,37 @@
     return slots, sems, 2 + 4 + 4 + 8, 1 + 3 + 3 + 7
 
 
-def all_sum(flat, small):
-    rows = flat.shape[0]
+def all_sum(parts, small):
+    sizes = tuple(p.shape[0] for p in parts)
+    lanes = parts[0].shape[1]
+    rows = sum(sizes)
     slots, sems, tslots, tsems = _counts(rows)
     c2 = rows // 64
+    vmem = pl.BlockSpec(memory_space=pltpu.VMEM)
     return pl.pallas_call(
-        functools.partial(_kernel, rows),
-        out_shape=(
-            jax.ShapeDtypeStruct(flat.shape, flat.dtype),
-            jax.ShapeDtypeStruct(small.shape, small.dtype),
-        ),
-        in_specs=[pl.BlockSpec(memory_space=pltpu.VMEM)] * 2,
-        out_specs=(pl.BlockSpec(memory_space=pltpu.VMEM),) * 2,
+        functools.partial(_kernel, sizes),
+        out_shape=tuple(jax.ShapeDtypeStruct(p.shape, p.dtype) for p in parts)
+        + (jax.ShapeDtypeStruct(small.shape, small.dtype),),
+        in_specs=[vmem] * (len(parts) + 1),
+        out_specs=(vmem,) * (len(parts) + 1),
         scratch_shapes=[
-            pltpu.VMEM(flat.shape, flat.dtype),
-            pltpu.VMEM((slots, flat.shape[1]), flat.dtype),
-            pltpu.VMEM((8, 2, c2, flat.shape[1]), flat.dtype),
+            pltpu.VMEM((rows, lanes), jnp.float32),
+            pltpu.VMEM((slots, lanes), jnp.float32),
+            pltpu.VMEM((8, 2, c2, lanes), jnp.float32),
             pltpu.SemaphoreType.DMA((sems,)),
             pltpu.SemaphoreType.DMA((sems,)),
             pltpu.VMEM((tslots,) + small.shape, small.dtype),
             pltpu.SemaphoreType.DMA((tsems,)),
             pltpu.SemaphoreType.DMA((tsems,)),
-            pltpu.VMEM(flat.shape, jnp.bfloat16),
+            pltpu.VMEM((rows, lanes), jnp.bfloat16),
             pltpu.SemaphoreType.DMA((13,)),
             pltpu.SemaphoreType.DMA((13,)),
+            pltpu.VMEM((rows, lanes), jnp.float32),
         ],
         compiler_params=pltpu.CompilerParams(
             collective_id=0, has_side_effects=True, vmem_limit_bytes=48 * 1024 * 1024
         ),
-    )(flat, small)
+    )(*parts, small)
 
 
 def _corr_fwd_kernel(ev_ref, win_ref, inv_ref, dots_ref, strip_ref):
@@ -581,16 +595,9 @@
     grad_vc = conv_grad(cols_v, pre_v, grad_lip, w_lip_proj, w_lip_conv)
     parts = (grad_ac, grad_vc, grad_ap, grad_vp)
     lanes = grad_ap.shape[1]
-    flat = jnp.concatenate([g.reshape(-1, lanes) for g in parts], axis=0)
     loss_block = jnp.zeros((8, 128), jnp.float32).at[0, 0].set(loss_local)
-    total, loss_total = all_sum(flat, loss_block)
-    outs = []
-    start = 0
-    for g in parts:
-        rows = g.size // lanes
-        outs.append(total[start : start + rows].reshape(g.shape))
-        start += rows
-    grad_ac, grad_vc, grad_ap, grad_vp = outs
+    *sums, loss_total = all_sum([g.reshape(-1, lanes) for g in parts], loss_block)
+    grad_ac, grad_vc, grad_ap, grad_vp = (t.reshape(g.shape) for t, g in zip(sums, parts))
     loss_sum = loss_total[0, 0]
     return (loss_sum / count, grad_ac, grad_ap, grad_vc, grad_vp)
 

time: 202 us -> 202 us (level)
  local copies, waits for them, and re-layouts: 21.2 us -> 24.2 us
    slice x2 -> x0, local copies, waits for them, and re-layouts: 3.45 us -> none  [shards(): outs.append(total[start:start + rows].reshape(g.shape))]
    concatenate x1 -> x0, other arithmetic: 2.68 us -> none  [shards(): flat = jnp.concatenate([g.reshape(-1, lanes) for g in parts], axis=0)]
    unnamed x38 -> x42, local copies, waits for them, and re-layouts: 4.91 us -> 7.33 us
  transfers between devices with their start and end apart: 6 -> 6, of which waited for: 1 -> 0; matrix products, arithmetic and copies ran while one was open for 9% -> 10% of each run, Pallas kernels for 9% -> 9%
where the time goes in v8:
time: 202 us; the launch traced here: 201 us
  Pallas kernels  119 us (59%)
  local copies, waits for them, and re-layouts  24.2 us (12%)
  other arithmetic  21 us (10%)
  starting transfers between devices  21 us (10%)
  matrix products  12.6 us (6%)
  between operations  3.48 us (2%)
    pallas_call x1, Pallas kernels, all_sum(): pl.pallas_call(functools.partial(_kernel, sizes), out_shape=tuple((jax.Sh...  91.1 us
    pallas_call x1, Pallas kernels, small_sum(): pl.pallas_call(functools.partial(_small_kernel, names), out_shape=jax.Sha...  17.4 us
    ppermute x2, starting transfers between devices, padded_2(): lax.ppermute(tail, axis, [(i, (i + 1) % count) for i in range(ends)])  11.4 us
    unnamed x42, local copies, waits for them, and re-layouts  7.33 us
    ppermute x2, starting transfers between devices, from_behind(): lax.ppermute(value, axis, [(source, source + steps) for source in range(i...  5.75 us
    pallas_call x1, Pallas kernels, corr_bwd(): pl.pallas_call(_corr_bwd_kernel, grid=(clips,), in_specs=[pl.BlockSpec((N...  5.44 us
    pallas_call x1, Pallas kernels, corr_fwd(): pl.pallas_call(_corr_fwd_kernel, grid=(clips,), in_specs=[pl.BlockSpec((N...  5.13 us
    dot_general x2, matrix products, conv_grad(): jnp.einsum('rk,re->ke', columns, grad_before, preferred_element_type=jnp....  4.3 us
  transfers between devices with their start and end apart: 6, of which 0 were waited for; matrix products, arithmetic and copies ran while one was open for 10% of the time, Pallas kernels for 9%

profile of v8, /device:TPU:1, one launch (start us, length us, event | category | flops | bytes accessed | tf_op | source)
XLA Modules:
  0.0 201.3 jit_solution(4317818207138037757)
XLA Ops:
  0.6 0.9 pad_maximum_fusion.5
  1.5 4.9 %collective-permute-start = (bf16[2,4,1,256]{3,2,1,0:T(2,128)(2,1)S(1)}, bf16[2,4,1,256]{3,2,1,0:T(2,128)(2,1)S(1)}, u32[]{:S(2)}, u32[]{:S(2)}) collective-permute-start(bf16[2,4,1,256]{3,2,1,0:T(2,128)(2,1)S(1)} %get-tuple-element.88), channel_id=1, source_target_pairs={{0,1},{1,2},{2,3},{3,4},{4,5},{5,6},{6,7},{8,9},{9,10},{10,11},{11... | collective-permute-start | bytes 12296 | tf_op jit(solution)/shard_map/ppermute | solution.py:438
  6.5 1.9 collective-permute-start.1
  8.4 0.8 broadcast_add_fusion
  9.2 0.7 broadcast_compare_fusion
  9.9 1.2 broadcast_compare_fusion.1
  11.1 1.3 compare_convert_fusion
  12.5 1.3 subtract_reduce_fusion
  13.8 1.2 scatter.6.t_ref
  15.0 17.4 %shard_map.119 = s32[8,128]{1,0:T(8,128)} custom-call(s32[8,128]{1,0:T(8,128)} %scatter.6.t_ref), custom_call_target="tpu_custom_call" | custom-call | tf_op jit(solution)/shard_map/pallas_call | solution.py:118
  32.4 1.2 slice.156
  34.3 1.5 pad_maximum_fusion.3
  35.8 0.6 fusion.32
  36.5 1.0 fusion.28
  37.5 0.7 convolution_convert_fusion
  38.2 0.6 copy-done.15
  38.9 6.5 %collective-permute-start.2 = (bf16[4,15,512]{2,1,0:T(8,128)(2,1)S(1)}, bf16[4,15,512]{2,1,0:T(8,128)(2,1)S(1)}, u32[]{:S(2)}, u32[]{:S(2)}) collective-permute-start(bf16[4,15,512]{2,1,0:T(8,128)(2,1)S(1)} %get-tuple-element.86), channel_id=1, source_target_pairs={{0,1},{1,2},{2,3},{3,4},{4,5},{5,6},{6,7},{8,9},{9,10},{10,11},{11... | collective-permute-start | bytes 184328 | tf_op jit(solution)/shard_map/ppermute | solution.py:438
  45.3 1.9 collective-permute-start.3
  47.3 1.2 pad_maximum_fusion.1
  48.5 1.0 fusion.27
  49.6 1.8 fusion.2
  51.3 1.2 pad_maximum_fusion
  52.6 0.5 fusion
  53.1 0.3 reverse.5
  53.4 0.6 copy.13.inv_ref
  54.0 1.3 pad.31.win_ref
  55.3 5.1 %shard_map.120 = (f32[4,256,128]{2,1,0:T(8,128)}, f32[4,256,128]{2,1,0:T(8,128)}) custom-call(bf16[4,256,512]{2,1,0:T(8,128)(2,1)} %get-tuple-element.100.ev_ref, bf16[4,384,512]{2,1,0:T(8,128)(2,1)} %pad.31.win_ref, f32[4,1,384]{2,1,0:T(1,128)} %copy.13.inv_ref), custom_call_target="tpu_custom_call" | custom-call | tf_op jit(solution)/shard_map/pallas_call | solution.py:366
  60.4 1.2 slice.163
  61.7 0.7 slice.164
  62.4 1.3 slice.165
  63.7 0.7 slice.166
  64.4 1.6 multiply_reduce_fusion
  66.0 1.4 select_reduce_fusion
  67.4 1.9 multiply_reduce_fusion.1
  69.5 0.8 pad.34.at_ref
  70.3 0.8 pad.33.gd_ref
  71.0 5.4 %shard_map.121 = (f32[4,256,512]{2,1,0:T(8,128)}, f32[4,384,512]{2,1,0:T(8,128)}, f32[4,1,384]{2,1,0:T(1,128)}) custom-call(bf16[4,256,128]{2,1,0:T(8,128)(2,1)} %pad.33.gd_ref, f32[4,256,128]{2,1,0:T(8,128)} %pad.34.at_ref, bf16[4,256,512]{2,1,0:T(8,128)(2,1)} %get-tuple-element.100.ev_ref, bf16[4,384,512]{2,1,0:T(8,128)(2,1)} %pad.31.win_ref), custom_call_target="tpu_custom_call" | custom-call | tf_op jit(solution)/shard_map/pallas_call | solution.py:403
  76.5 2.0 %fusion.4 = bf16[4,256,512]{2,1,0:T(8,128)(2,1)S(1)} fusion(f32[4,256,512]{2,1,0:T(8,128)} %get-tuple-element.67, bf16[4,256,512]{2,1,0:T(8,128)(2,1)S(1)} %copy-done.1, f32[4,256]{1,0:T(4,128)S(1)} %fusion.24), kind=kLoop, calls=%fused_computation.8 | loop fusion | flops 2097152 | bytes 4198400 | tf_op jit(solution)/shard_map/convert_element_type | solution.py:580
  78.7 0.8 convolution_bitcast_fusion.refs_3_
  79.5 1.1 copy-done.2
  80.6 0.3 fusion.1
  81.0 1.9 collective-permute-start.4
  82.9 3.8 %collective-permute-start.5 = (f32[4,15,512]{2,1,0:T(8,128)S(1)}, f32[4,15,512]{2,1,0:T(8,128)S(1)}, u32[]{:S(2)}, u32[]{:S(2)}) collective-permute-start(f32[4,15,512]{2,1,0:T(8,128)S(1)} %get-tuple-element.81), channel_id=1, source_target_pairs={{0,1},{1,2},{2,3},{3,4},{4,5},{5,6},{6,7},{8,9},{9,10},{10,11},{11... | collective-permute-start | bytes 368648 | tf_op jit(solution)/shard_map/ppermute | solution.py:450
  86.8 1.2 fusion.11
  87.9 0.2 copy-done.4
  88.2 2.1 %fusion.35.refs_1_ = f32[768,512]{1,0:T(8,128)} fusion(bf16[1024,768]{1,0:T(8,128)(2,1)S(1)} %bitcast.95, bf16[1024,512]{1,0:T(8,128)(2,1)S(1)} %fusion.11), kind=kOutput, calls=%fused_computation.82 | convolution fusion | flops 805306368 | bytes 4194304 | tf_op jit(solution)/shard_map/rk,re->ke/dot_general | solution.py:506
  90.3 1.6 slice.185
  91.9 0.6 scatter.9.refs_4_
  92.6 1.6 scatter-add.6
  94.2 0.9 slice_add_fusion
  95.1 1.7 scatter-add.9
  96.8 1.9 convert_element_type.63
  98.7 0.3 copy-done.16
  99.0 0.8 convolution_bitcast_fusion.1.refs_2_
  99.8 0.2 copy-done.14
  100.1 1.2 fusion.18
  101.3 0.2 copy-done.3
  101.5 2.1 %fusion.34.refs_0_ = f32[768,512]{1,0:T(8,128)} fusion(bf16[1024,768]{1,0:T(8,128)(2,1)S(1)} %bitcast.94, bf16[1024,512]{1,0:T(8,128)(2,1)S(1)} %fusion.18), kind=kOutput, calls=%fused_computation.81 | convolution fusion | flops 805306368 | bytes 4194304 | tf_op jit(solution)/shard_map/rk,re->ke/dot_general | solution.py:506
  103.6 91.1 %shard_map.122 = (f32[768,512]{1,0:T(8,128)S(1)}, f32[768,512]{1,0:T(8,128)}, f32[512,512]{1,0:T(8,128)S(1)}, f32[512,512]{1,0:T(8,128)S(1)}, f32[8,128]{1,0:T(8,128)S(1)}) custom-call(f32[768,512]{1,0:T(8,128)} %fusion.34.refs_0_, f32[768,512]{1,0:T(8,128)} %fusion.35.refs_1_, f32[512,512]{1,0:T(8,128)S(1)} %convolution_bitcast_fusion.1.refs_2_, ...), custom_call_target="tpu_custom_call" | custom-call | tf_op jit(solution)/shard_map/pallas_call | solution.py:321
  194.7 0.5 slice.174
  195.9 1.1 copy.26
  197.1 1.0 copy.27
  198.0 1.1 copy.28
  199.2 1.0 copy.29
  (50 shorter events, 0.8 us)
Async XLA Ops:
  0.6 35.8 %copy-start = (bf16[3,256,512]{2,1,0:T(8,128)(2,1)S(1)}, bf16[3,256,512]{2,1,0:T(8,128)(2,1)}, u32[]{:S(2)}) copy-start(bf16[3,256,512]{2,1,0:T(8,128)(2,1)} %param.20) | copy-start | bytes 2359300
  1.5 32.8 %collective-permute-start = (bf16[2,4,1,256]{3,2,1,0:T(2,128)(2,1)S(1)}, bf16[2,4,1,256]{3,2,1,0:T(2,128)(2,1)S(1)}, u32[]{:S(2)}, u32[]{:S(2)}) collective-permute-start(bf16[2,4,1,256]{3,2,1,0:T(2,128)(2,1)S(1)} %get-tuple-element.88), channel_id=1, source_target_pairs={{0,1},{1,2},{2,3},{3,4},{4,5},{5,6},{6,7},{8,9},{9,10},{10,11},{11... | collective-permute-start | bytes 12296 | tf_op jit(solution)/shard_map/ppermute | solution.py:438
  6.5 27.8 %collective-permute-start.1 = (bf16[2,4,1,256]{3,2,1,0:T(2,128)(2,1)S(1)}, bf16[2,4,1,256]{3,2,1,0:T(2,128)(2,1)S(1)}, u32[]{:S(2)}, u32[]{:S(2)}) collective-permute-start(bf16[2,4,1,256]{3,2,1,0:T(2,128)(2,1)S(1)} %get-tuple-element.89), channel_id=1, source_target_pairs={{1,0},{2,1},{3,2},{4,3},{5,4},{6,5},{7,6},{9,8},{10,9},{11,10},{12... | collective-permute-start | bytes 12296 | tf_op jit(solution)/shard_map/ppermute | solution.py:440
  8.4 1.5 copy-start.6
  36.4 1.0 copy-start.13
  37.5 1.4 copy-start.15
  38.9 9.7 %copy-start.10 = (bf16[3,256,512]{2,1,0:T(8,128)(2,1)S(1)}, bf16[3,256,512]{2,1,0:T(8,128)(2,1)}, u32[]{:S(2)}) copy-start(bf16[3,256,512]{2,1,0:T(8,128)(2,1)} %param.22) | copy-start | bytes 2359300
  38.9 13.7 %collective-permute-start.2 = (bf16[4,15,512]{2,1,0:T(8,128)(2,1)S(1)}, bf16[4,15,512]{2,1,0:T(8,128)(2,1)S(1)}, u32[]{:S(2)}, u32[]{:S(2)}) collective-permute-start(bf16[4,15,512]{2,1,0:T(8,128)(2,1)S(1)} %get-tuple-element.86), channel_id=1, source_target_pairs={{0,1},{1,2},{2,3},{3,4},{4,5},{5,6},{6,7},{8,9},{9,10},{10,11},{11... | collective-permute-start | bytes 184328 | tf_op jit(solution)/shard_map/ppermute | solution.py:438
  45.3 7.2 %collective-permute-start.3 = (bf16[4,15,512]{2,1,0:T(8,128)(2,1)S(1)}, bf16[4,15,512]{2,1,0:T(8,128)(2,1)S(1)}, u32[]{:S(2)}, u32[]{:S(2)}) collective-permute-start(bf16[4,15,512]{2,1,0:T(8,128)(2,1)S(1)} %get-tuple-element.87), channel_id=1, source_target_pairs={{1,0},{2,1},{3,2},{4,3},{5,4},{6,5},{7,6},{9,8},{10,9},{11,10},{12... | collective-permute-start | bytes 184328 | tf_op jit(solution)/shard_map/ppermute | solution.py:440
  48.5 1.0 copy-start.11
  49.6 1.8 copy-start.17
  51.3 1.8 copy-start.7
  64.4 4.9 %copy-start.8 = (f32[4,256]{1,0:T(4,128)S(1)}, f32[4,256]{1,0:T(4,128)}, u32[]{:S(2)}) copy-start(f32[4,256]{1,0:T(4,128)} %copy-done.7) | copy-start | bytes 12292
  70.3 6.2 %copy-start.1 = (bf16[4,256,512]{2,1,0:T(8,128)(2,1)S(1)}, bf16[4,256,512]{2,1,0:T(8,128)(2,1)}, u32[]{:S(2)}) copy-start(bf16[4,256,512]{2,1,0:T(8,128)(2,1)} %get-tuple-element.100.ev_ref) | copy-start | bytes 3145732
  76.5 2.2 %copy-start.18 = (f32[4,256,512]{2,1,0:T(8,128)S(1)}, f32[4,256,512]{2,1,0:T(8,128)}, u32[]{:S(2)}) copy-start(f32[4,256,512]{2,1,0:T(8,128)} %copy-done.17) | copy-start | bytes 6291460
  78.7 0.8 copy-start.9
  78.7 1.9 copy-start.2
  80.6 6.1 %copy-start.12 = (bf16[512,512]{1,0:T(8,128)(2,1)S(1)}, bf16[512,512]{1,0:T(8,128)(2,1)}, u32[]{:S(2)}) copy-start(bf16[512,512]{1,0:T(8,128)(2,1)} %param.23) | copy-start | bytes 1572868
  81.0 11.6 %collective-permute-start.4 = (f32[4,15,512]{2,1,0:T(8,128)S(1)}, f32[4,15,512]{2,1,0:T(8,128)S(1)}, u32[]{:S(2)}, u32[]{:S(2)}) collective-permute-start(f32[4,15,512]{2,1,0:T(8,128)S(1)} %get-tuple-element.82), channel_id=1, source_target_pairs={{1,0},{2,1},{3,2},{4,3},{5,4},{6,5},{7,6},{9,8},{10,9},{11,10},{12... | collective-permute-start | bytes 368648 | tf_op jit(solution)/shard_map/ppermute | solution.py:450
  82.9 11.3 %collective-permute-start.5 = (f32[4,15,512]{2,1,0:T(8,128)S(1)}, f32[4,15,512]{2,1,0:T(8,128)S(1)}, u32[]{:S(2)}, u32[]{:S(2)}) collective-permute-start(f32[4,15,512]{2,1,0:T(8,128)S(1)} %get-tuple-element.81), channel_id=1, source_target_pairs={{0,1},{1,2},{2,3},{3,4},{4,5},{5,6},{6,7},{8,9},{9,10},{10,11},{11... | collective-permute-start | bytes 368648 | tf_op jit(solution)/shard_map/ppermute | solution.py:450
  86.8 1.4 copy-start.4
  96.8 2.2 %copy-start.16 = (f32[4,256,512]{2,1,0:T(8,128)S(1)}, f32[4,256,512]{2,1,0:T(8,128)}, u32[]{:S(2)}) copy-start(f32[4,256,512]{2,1,0:T(8,128)} %copy-done.15) | copy-start | bytes 6291460
  99.0 1.0 copy-start.14
  100.1 1.4 copy-start.3
  195.9 2.1 %copy-start.5 = (f32[768,512]{1,0:T(8,128)S(1)}, f32[768,512]{1,0:T(8,128)}, u32[]{:S(2)}) copy-start(f32[768,512]{1,0:T(8,128)} %get-tuple-element.71) | copy-start | bytes 4718596

commit v9 on v8

--- a/solution.py
+++ b/solution.py
@@ -38,12 +38,16 @@
     def at_h(v):
         return ((v % 2) * 16 + x * 4 + y, ti)
 
+    def at_k(v):
+        return (v % 32, ti)
+
     return {
         "c": (2, core, at_c, 1),
         "y": (4, y, at_y, 2),
         "x": (4, x, at_x, 2),
         "z": (8, z, at_z, 1),
         "h": (2, zh, at_h, 1),
+        "k": (32, ci, at_k, 1),
     }
 
 
@@ -112,7 +116,7 @@
 
 
 def small_sum(t, names, cid):
-    table_n = {"c": 2, "y": 4, "x": 4, "z": 8, "h": 2}
+    table_n = {"c": 2, "y": 4, "x": 4, "z": 8, "h": 2, "k": 32}
     slots = sum(table_n[k] for k in names)
     sems = sum(table_n[k] - 1 for k in names)
     return pl.pallas_call(
@@ -524,7 +528,7 @@
     cols_v, pre_v, hid_v = (flatten_rows(cols_v), flatten_rows(pre_v), flatten_rows(hid_v))
     count_part = jnp.sum(lengths - jnp.abs(labels))
     count_block = jnp.zeros((8, 128), jnp.int32).at[0, 0].set(count_part)
-    count = small_sum(count_block, ("y", "x", "h"), 1)[0, 0].astype(jnp.float32)
+    count = small_sum(count_block, ("k",), 1)[0, 0].astype(jnp.float32)
     inv_win = inverse_norm(window)
     reciprocal_visual_length = inverse_norm(emb_v)
     wide_pad = -(-wide_len // 128) * 128

time: 202 us -> 201 us (level)
  transfers between devices with their start and end apart: 6 -> 6, of which waited for: 0 -> 0; matrix products, arithmetic and copies ran while one was open for 10% -> 10% of each run, Pallas kernels for 9% -> 8%
where the time goes in v9:
time: 201 us; the launch traced here: 200 us
  Pallas kernels  119 us (59%)
  local copies, waits for them, and re-layouts  24.2 us (12%)
  other arithmetic  21 us (10%)
  starting transfers between devices  19.6 us (10%)
  matrix products  12.6 us (6%)
  between operations  3.48 us (2%)
    pallas_call x1, Pallas kernels, all_sum(): pl.pallas_call(functools.partial(_kernel, sizes), out_shape=tuple((jax.Sh...  92.8 us
    pallas_call x1, Pallas kernels, small_sum(): pl.pallas_call(functools.partial(_small_kernel, names), out_shape=jax.Sha...  16 us
    ppermute x2, starting transfers between devices, padded_2(): lax.ppermute(tail, axis, [(i, (i + 1) % count) for i in range(ends)])  9.97 us
    unnamed x42, local copies, waits for them, and re-layouts  7.33 us
    ppermute x2, starting transfers between devices, from_behind(): lax.ppermute(value, axis, [(source, source + steps) for source in range(i...  5.75 us
    pallas_call x1, Pallas kernels, corr_bwd(): pl.pallas_call(_corr_bwd_kernel, grid=(clips,), in_specs=[pl.BlockSpec((N...  5.44 us
    pallas_call x1, Pallas kernels, corr_fwd(): pl.pallas_call(_corr_fwd_kernel, grid=(clips,), in_specs=[pl.BlockSpec((N...  5.13 us
    dot_general x2, matrix products, conv_grad(): jnp.einsum('rk,re->ke', columns, grad_before, preferred_element_type=jnp....  4.3 us
  transfers between devices with their start and end apart: 6, of which 0 were waited for; matrix products, arithmetic and copies ran while one was open for 10% of the time, Pallas kernels for 8%

profile of v9, /device:TPU:1, one launch (start us, length us, event | category | flops | bytes accessed | tf_op | source)
XLA Modules:
  0.0 200.2 jit_solution(10825330742972827676)
XLA Ops:
  0.6 0.9 pad_maximum_fusion.5
  1.5 4.9 %collective-permute-start = (bf16[2,4,1,256]{3,2,1,0:T(2,128)(2,1)S(1)}, bf16[2,4,1,256]{3,2,1,0:T(2,128)(2,1)S(1)}, u32[]{:S(2)}, u32[]{:S(2)}) collective-permute-start(bf16[2,4,1,256]{3,2,1,0:T(2,128)(2,1)S(1)} %get-tuple-element.88), channel_id=1, source_target_pairs={{0,1},{1,2},{2,3},{3,4},{4,5},{5,6},{6,7},{8,9},{9,10},{10,11},{11... | collective-permute-start | bytes 12296 | tf_op jit(solution)/shard_map/ppermute | solution.py:442
  6.5 1.9 collective-permute-start.1
  8.4 0.8 broadcast_add_fusion
  9.2 0.7 broadcast_compare_fusion
  9.9 1.2 broadcast_compare_fusion.1
  11.1 1.3 compare_convert_fusion
  12.5 1.3 subtract_reduce_fusion
  13.8 1.2 scatter.6.t_ref
  15.0 16.0 %shard_map.119 = s32[8,128]{1,0:T(8,128)} custom-call(s32[8,128]{1,0:T(8,128)} %scatter.6.t_ref), custom_call_target="tpu_custom_call" | custom-call | tf_op jit(solution)/shard_map/pallas_call | solution.py:122
  31.0 1.2 slice.156
  32.9 1.5 pad_maximum_fusion.3
  34.5 0.6 fusion.32
  35.1 1.0 fusion.28
  36.1 0.7 convolution_convert_fusion
  36.9 0.6 copy-done.15
  37.5 5.0 %collective-permute-start.2 = (bf16[4,15,512]{2,1,0:T(8,128)(2,1)S(1)}, bf16[4,15,512]{2,1,0:T(8,128)(2,1)S(1)}, u32[]{:S(2)}, u32[]{:S(2)}) collective-permute-start(bf16[4,15,512]{2,1,0:T(8,128)(2,1)S(1)} %get-tuple-element.86), channel_id=1, source_target_pairs={{0,1},{1,2},{2,3},{3,4},{4,5},{5,6},{6,7},{8,9},{9,10},{10,11},{11... | collective-permute-start | bytes 184328 | tf_op jit(solution)/shard_map/ppermute | solution.py:442
  42.6 1.9 collective-permute-start.3
  44.5 1.2 pad_maximum_fusion.1
  45.7 1.0 fusion.27
  46.8 1.8 fusion.2
  48.5 1.2 pad_maximum_fusion
  49.8 0.5 fusion
  50.3 0.3 reverse.5
  50.6 0.6 copy.13.inv_ref
  51.2 1.3 pad.31.win_ref
  52.5 5.1 %shard_map.120 = (f32[4,256,128]{2,1,0:T(8,128)}, f32[4,256,128]{2,1,0:T(8,128)}) custom-call(bf16[4,256,512]{2,1,0:T(8,128)(2,1)} %get-tuple-element.100.ev_ref, bf16[4,384,512]{2,1,0:T(8,128)(2,1)} %pad.31.win_ref, f32[4,1,384]{2,1,0:T(1,128)} %copy.13.inv_ref), custom_call_target="tpu_custom_call" | custom-call | tf_op jit(solution)/shard_map/pallas_call | solution.py:370
  57.6 1.2 slice.163
  58.9 0.7 slice.164
  59.6 1.3 slice.165
  60.9 0.7 slice.166
  61.6 1.6 multiply_reduce_fusion
  63.2 1.4 select_reduce_fusion
  64.6 1.9 multiply_reduce_fusion.1
  66.7 0.8 pad.34.at_ref
  67.5 0.8 pad.33.gd_ref
  68.3 5.4 %shard_map.121 = (f32[4,256,512]{2,1,0:T(8,128)}, f32[4,384,512]{2,1,0:T(8,128)}, f32[4,1,384]{2,1,0:T(1,128)}) custom-call(bf16[4,256,128]{2,1,0:T(8,128)(2,1)} %pad.33.gd_ref, f32[4,256,128]{2,1,0:T(8,128)} %pad.34.at_ref, bf16[4,256,512]{2,1,0:T(8,128)(2,1)} %get-tuple-element.100.ev_ref, bf16[4,384,512]{2,1,0:T(8,128)(2,1)} %pad.31.win_ref), custom_call_target="tpu_custom_call" | custom-call | tf_op jit(solution)/shard_map/pallas_call | solution.py:407
  73.7 2.0 %fusion.4 = bf16[4,256,512]{2,1,0:T(8,128)(2,1)S(1)} fusion(f32[4,256,512]{2,1,0:T(8,128)} %get-tuple-element.67, bf16[4,256,512]{2,1,0:T(8,128)(2,1)S(1)} %copy-done.1, f32[4,256]{1,0:T(4,128)S(1)} %fusion.24), kind=kLoop, calls=%fused_computation.8 | loop fusion | flops 2097152 | bytes 4198400 | tf_op jit(solution)/shard_map/convert_element_type | solution.py:584
  75.9 0.8 convolution_bitcast_fusion.refs_3_
  76.7 1.1 copy-done.2
  77.8 0.3 fusion.1
  78.2 1.9 collective-permute-start.4
  80.1 3.8 %collective-permute-start.5 = (f32[4,15,512]{2,1,0:T(8,128)S(1)}, f32[4,15,512]{2,1,0:T(8,128)S(1)}, u32[]{:S(2)}, u32[]{:S(2)}) collective-permute-start(f32[4,15,512]{2,1,0:T(8,128)S(1)} %get-tuple-element.81), channel_id=1, source_target_pairs={{0,1},{1,2},{2,3},{3,4},{4,5},{5,6},{6,7},{8,9},{9,10},{10,11},{11... | collective-permute-start | bytes 368648 | tf_op jit(solution)/shard_map/ppermute | solution.py:454
  84.0 1.2 fusion.11
  85.2 0.2 copy-done.4
  85.4 2.1 %fusion.35.refs_1_ = f32[768,512]{1,0:T(8,128)} fusion(bf16[1024,768]{1,0:T(8,128)(2,1)S(1)} %bitcast.95, bf16[1024,512]{1,0:T(8,128)(2,1)S(1)} %fusion.11), kind=kOutput, calls=%fused_computation.82 | convolution fusion | flops 805306368 | bytes 4194304 | tf_op jit(solution)/shard_map/rk,re->ke/dot_general | solution.py:510
  87.5 1.6 slice.185
  89.1 0.6 scatter.9.refs_4_
  89.8 1.6 scatter-add.6
  91.4 0.9 slice_add_fusion
  92.3 1.7 scatter-add.9
  94.0 1.9 convert_element_type.63
  95.9 0.3 copy-done.16
  96.2 0.8 convolution_bitcast_fusion.1.refs_2_
  97.0 0.2 copy-done.14
  97.3 1.2 fusion.18
  98.5 0.2 copy-done.3
  98.7 2.1 %fusion.34.refs_0_ = f32[768,512]{1,0:T(8,128)} fusion(bf16[1024,768]{1,0:T(8,128)(2,1)S(1)} %bitcast.94, bf16[1024,512]{1,0:T(8,128)(2,1)S(1)} %fusion.18), kind=kOutput, calls=%fused_computation.81 | convolution fusion | flops 805306368 | bytes 4194304 | tf_op jit(solution)/shard_map/rk,re->ke/dot_general | solution.py:510
  100.8 92.8 %shard_map.122 = (f32[768,512]{1,0:T(8,128)S(1)}, f32[768,512]{1,0:T(8,128)}, f32[512,512]{1,0:T(8,128)S(1)}, f32[512,512]{1,0:T(8,128)S(1)}, f32[8,128]{1,0:T(8,128)S(1)}) custom-call(f32[768,512]{1,0:T(8,128)} %fusion.34.refs_0_, f32[768,512]{1,0:T(8,128)} %fusion.35.refs_1_, f32[512,512]{1,0:T(8,128)S(1)} %convolution_bitcast_fusion.1.refs_2_, ...), custom_call_target="tpu_custom_call" | custom-call | tf_op jit(solution)/shard_map/pallas_call | solution.py:325
  193.7 0.5 slice.174
  194.9 1.1 copy.26
  196.0 1.0 copy.27
  197.0 1.1 copy.28
  198.1 1.0 copy.29
  (50 shorter events, 0.8 us)
Async XLA Ops:
  0.6 34.4 %copy-start = (bf16[3,256,512]{2,1,0:T(8,128)(2,1)S(1)}, bf16[3,256,512]{2,1,0:T(8,128)(2,1)}, u32[]{:S(2)}) copy-start(bf16[3,256,512]{2,1,0:T(8,128)(2,1)} %param.20) | copy-start | bytes 2359300
  1.5 31.4 %collective-permute-start = (bf16[2,4,1,256]{3,2,1,0:T(2,128)(2,1)S(1)}, bf16[2,4,1,256]{3,2,1,0:T(2,128)(2,1)S(1)}, u32[]{:S(2)}, u32[]{:S(2)}) collective-permute-start(bf16[2,4,1,256]{3,2,1,0:T(2,128)(2,1)S(1)} %get-tuple-element.88), channel_id=1, source_target_pairs={{0,1},{1,2},{2,3},{3,4},{4,5},{5,6},{6,7},{8,9},{9,10},{10,11},{11... | collective-permute-start | bytes 12296 | tf_op jit(solution)/shard_map/ppermute | solution.py:442
  6.5 26.4 %collective-permute-start.1 = (bf16[2,4,1,256]{3,2,1,0:T(2,128)(2,1)S(1)}, bf16[2,4,1,256]{3,2,1,0:T(2,128)(2,1)S(1)}, u32[]{:S(2)}, u32[]{:S(2)}) collective-permute-start(bf16[2,4,1,256]{3,2,1,0:T(2,128)(2,1)S(1)} %get-tuple-element.89), channel_id=1, source_target_pairs={{1,0},{2,1},{3,2},{4,3},{5,4},{6,5},{7,6},{9,8},{10,9},{11,10},{12... | collective-permute-start | bytes 12296 | tf_op jit(solution)/shard_map/ppermute | solution.py:444
  8.4 1.5 copy-start.6
  35.1 1.0 copy-start.13
  36.1 1.4 copy-start.15
  37.5 8.2 %copy-start.10 = (bf16[3,256,512]{2,1,0:T(8,128)(2,1)S(1)}, bf16[3,256,512]{2,1,0:T(8,128)(2,1)}, u32[]{:S(2)}) copy-start(bf16[3,256,512]{2,1,0:T(8,128)(2,1)} %param.22) | copy-start | bytes 2359300
  37.5 12.3 %collective-permute-start.2 = (bf16[4,15,512]{2,1,0:T(8,128)(2,1)S(1)}, bf16[4,15,512]{2,1,0:T(8,128)(2,1)S(1)}, u32[]{:S(2)}, u32[]{:S(2)}) collective-permute-start(bf16[4,15,512]{2,1,0:T(8,128)(2,1)S(1)} %get-tuple-element.86), channel_id=1, source_target_pairs={{0,1},{1,2},{2,3},{3,4},{4,5},{5,6},{6,7},{8,9},{9,10},{10,11},{11... | collective-permute-start | bytes 184328 | tf_op jit(solution)/shard_map/ppermute | solution.py:442
  42.6 7.2 %collective-permute-start.3 = (bf16[4,15,512]{2,1,0:T(8,128)(2,1)S(1)}, bf16[4,15,512]{2,1,0:T(8,128)(2,1)S(1)}, u32[]{:S(2)}, u32[]{:S(2)}) collective-permute-start(bf16[4,15,512]{2,1,0:T(8,128)(2,1)S(1)} %get-tuple-element.87), channel_id=1, source_target_pairs={{1,0},{2,1},{3,2},{4,3},{5,4},{6,5},{7,6},{9,8},{10,9},{11,10},{12... | collective-permute-start | bytes 184328 | tf_op jit(solution)/shard_map/ppermute | solution.py:444
  45.7 1.0 copy-start.11
  46.8 1.8 copy-start.17
  48.5 1.8 copy-start.7
  61.6 4.9 %copy-start.8 = (f32[4,256]{1,0:T(4,128)S(1)}, f32[4,256]{1,0:T(4,128)}, u32[]{:S(2)}) copy-start(f32[4,256]{1,0:T(4,128)} %copy-done.7) | copy-start | bytes 12292
  67.5 6.2 %copy-start.1 = (bf16[4,256,512]{2,1,0:T(8,128)(2,1)S(1)}, bf16[4,256,512]{2,1,0:T(8,128)(2,1)}, u32[]{:S(2)}) copy-start(bf16[4,256,512]{2,1,0:T(8,128)(2,1)} %get-tuple-element.100.ev_ref) | copy-start | bytes 3145732
  73.7 2.2 %copy-start.18 = (f32[4,256,512]{2,1,0:T(8,128)S(1)}, f32[4,256,512]{2,1,0:T(8,128)}, u32[]{:S(2)}) copy-start(f32[4,256,512]{2,1,0:T(8,128)} %copy-done.17) | copy-start | bytes 6291460
  75.9 0.8 copy-start.9
  75.9 1.9 copy-start.2
  77.8 6.1 %copy-start.12 = (bf16[512,512]{1,0:T(8,128)(2,1)S(1)}, bf16[512,512]{1,0:T(8,128)(2,1)}, u32[]{:S(2)}) copy-start(bf16[512,512]{1,0:T(8,128)(2,1)} %param.23) | copy-start | bytes 1572868
  78.2 11.6 %collective-permute-start.4 = (f32[4,15,512]{2,1,0:T(8,128)S(1)}, f32[4,15,512]{2,1,0:T(8,128)S(1)}, u32[]{:S(2)}, u32[]{:S(2)}) collective-permute-start(f32[4,15,512]{2,1,0:T(8,128)S(1)} %get-tuple-element.82), channel_id=1, source_target_pairs={{1,0},{2,1},{3,2},{4,3},{5,4},{6,5},{7,6},{9,8},{10,9},{11,10},{12... | collective-permute-start | bytes 368648 | tf_op jit(solution)/shard_map/ppermute | solution.py:454
  80.1 11.3 %collective-permute-start.5 = (f32[4,15,512]{2,1,0:T(8,128)S(1)}, f32[4,15,512]{2,1,0:T(8,128)S(1)}, u32[]{:S(2)}, u32[]{:S(2)}) collective-permute-start(f32[4,15,512]{2,1,0:T(8,128)S(1)} %get-tuple-element.81), channel_id=1, source_target_pairs={{0,1},{1,2},{2,3},{3,4},{4,5},{5,6},{6,7},{8,9},{9,10},{10,11},{11... | collective-permute-start | bytes 368648 | tf_op jit(solution)/shard_map/ppermute | solution.py:454
  84.0 1.4 copy-start.4
  94.0 2.2 %copy-start.16 = (f32[4,256,512]{2,1,0:T(8,128)S(1)}, f32[4,256,512]{2,1,0:T(8,128)}, u32[]{:S(2)}) copy-start(f32[4,256,512]{2,1,0:T(8,128)} %copy-done.15) | copy-start | bytes 6291460
  96.2 1.0 copy-start.14
  97.3 1.4 copy-start.3
  194.9 2.1 %copy-start.5 = (f32[768,512]{1,0:T(8,128)S(1)}, f32[768,512]{1,0:T(8,128)}, u32[]{:S(2)}) copy-start(f32[768,512]{1,0:T(8,128)} %get-tuple-element.71) | copy-start | bytes 4718596

commit v10 on v9

--- a/solution.py
+++ b/solution.py
@@ -249,7 +249,7 @@
     nz, zi, nbz, _ = lz
 
     rider = tiny_level(lc, True)
-    slot, sem = _rs_stage([(nc, core, nbc, 1, 0, rows, work)], work, rbuf, send_sem, recv_sem, slot, sem, rider)
+    slot, sem = _rs_stage([(nc, core, nbc, 2, 0, rows, work)], work, rbuf, send_sem, recv_sem, slot, sem, rider)
     tiny_done(nc)
     r0 = core * half
     a1, b1 = r0, r0 + quarter
@@ -300,7 +300,7 @@
         region = pl.ds(pl.multiple_of(at, 16), c1)
         half_ref[region] = o_ref[region].astype(half_ref.dtype)
     sem = _ag_stage([(ny, yi, nby, 2, a1, quarter, None), (nx, xi, nbx, 2, b1, quarter, None)], half_ref, hsend, hrecv, 0)
-    _ag_stage([(nc, core, nbc, 1, 0, rows, None)], half_ref, hsend, hrecv, sem)
+    _ag_stage([(nc, core, nbc, 2, 0, rows, None)], half_ref, hsend, hrecv, sem)
     start = 0
     for size, out_ref in zip(sizes, outs):
         out_ref[...] = half_ref[start : start + size].astype(out_ref.dtype)
@@ -311,7 +311,7 @@
     half, quarter = rows // 2, rows // 4
     c1 = quarter // 4
     slots = half + 3 * 2 * quarter // 4 + 3 * 2 * c1 // 4
-    sems = 1 + 3 * 4 + 3 * 2 + 7 + 3 * 2
+    sems = 2 + 3 * 4 + 3 * 2 + 7 + 3 * 2
     return slots, sems, 2 + 4 + 4 + 8, 1 + 3 + 3 + 7
 
 
@@ -338,8 +338,8 @@
             pltpu.SemaphoreType.DMA((tsems,)),
             pltpu.SemaphoreType.DMA((tsems,)),
             pltpu.VMEM((rows, lanes), jnp.bfloat16),
-            pltpu.SemaphoreType.DMA((13,)),
-            pltpu.SemaphoreType.DMA((13,)),
+            pltpu.SemaphoreType.DMA((14,)),
+            pltpu.SemaphoreType.DMA((14,)),
             pltpu.VMEM((rows, lanes), jnp.float32),
         ],
         compiler_params=pltpu.CompilerParams(

time: 201 us -> 202 us (level)
  no operation moved by 1% of the time
where the time goes in v10:
time: 202 us; the launch traced here: 201 us
  Pallas kernels  121 us (60%)
  local copies, waits for them, and re-layouts  24.2 us (12%)
  other arithmetic  21 us (10%)
  starting transfers between devices  19.6 us (10%)
  matrix products  12.6 us (6%)
  between operations  3.48 us (2%)
    pallas_call x1, Pallas kernels, all_sum(): pl.pallas_call(functools.partial(_kernel, sizes), out_shape=tuple((jax.Sh...  94.1 us
    pallas_call x1, Pallas kernels, small_sum(): pl.pallas_call(functools.partial(_small_kernel, names), out_shape=jax.Sha...  16 us
    ppermute x2, starting transfers between devices, padded_2(): lax.ppermute(tail, axis, [(i, (i + 1) % count) for i in range(ends)])  9.97 us
    unnamed x42, local copies, waits for them, and re-layouts  7.33 us
    ppermute x2, starting transfers between devices, from_behind(): lax.ppermute(value, axis, [(source, source + steps) for source in range(i...  5.75 us
    pallas_call x1, Pallas kernels, corr_bwd(): pl.pallas_call(_corr_bwd_kernel, grid=(clips,), in_specs=[pl.BlockSpec((N...  5.44 us
    pallas_call x1, Pallas kernels, corr_fwd(): pl.pallas_call(_corr_fwd_kernel, grid=(clips,), in_specs=[pl.BlockSpec((N...  5.13 us
    dot_general x2, matrix products, conv_grad(): jnp.einsum('rk,re->ke', columns, grad_before, preferred_element_type=jnp....  4.3 us
  transfers between devices with their start and end apart: 6, of which 0 were waited for; matrix products, arithmetic and copies ran while one was open for 10% of the time, Pallas kernels for 8%

profile of v10, /device:TPU:1, one launch (start us, length us, event | category | flops | bytes accessed | tf_op | source)
XLA Modules:
  0.0 201.5 jit_solution(15805137876659571080)
XLA Ops:
  0.6 0.9 pad_maximum_fusion.5
  1.5 4.9 %collective-permute-start = (bf16[2,4,1,256]{3,2,1,0:T(2,128)(2,1)S(1)}, bf16[2,4,1,256]{3,2,1,0:T(2,128)(2,1)S(1)}, u32[]{:S(2)}, u32[]{:S(2)}) collective-permute-start(bf16[2,4,1,256]{3,2,1,0:T(2,128)(2,1)S(1)} %get-tuple-element.88), channel_id=1, source_target_pairs={{0,1},{1,2},{2,3},{3,4},{4,5},{5,6},{6,7},{8,9},{9,10},{10,11},{11... | collective-permute-start | bytes 12296 | tf_op jit(solution)/shard_map/ppermute | solution.py:442
  6.5 1.9 collective-permute-start.1
  8.4 0.8 broadcast_add_fusion
  9.2 0.7 broadcast_compare_fusion
  9.9 1.2 broadcast_compare_fusion.1
  11.1 1.3 compare_convert_fusion
  12.5 1.3 subtract_reduce_fusion
  13.8 1.2 scatter.6.t_ref
  15.0 16.0 %shard_map.119 = s32[8,128]{1,0:T(8,128)} custom-call(s32[8,128]{1,0:T(8,128)} %scatter.6.t_ref), custom_call_target="tpu_custom_call" | custom-call | tf_op jit(solution)/shard_map/pallas_call | solution.py:122
  31.0 1.2 slice.156
  32.9 1.5 pad_maximum_fusion.3
  34.5 0.6 fusion.32
  35.1 1.0 fusion.28
  36.1 0.7 convolution_convert_fusion
  36.9 0.6 copy-done.15
  37.5 5.0 %collective-permute-start.2 = (bf16[4,15,512]{2,1,0:T(8,128)(2,1)S(1)}, bf16[4,15,512]{2,1,0:T(8,128)(2,1)S(1)}, u32[]{:S(2)}, u32[]{:S(2)}) collective-permute-start(bf16[4,15,512]{2,1,0:T(8,128)(2,1)S(1)} %get-tuple-element.86), channel_id=1, source_target_pairs={{0,1},{1,2},{2,3},{3,4},{4,5},{5,6},{6,7},{8,9},{9,10},{10,11},{11... | collective-permute-start | bytes 184328 | tf_op jit(solution)/shard_map/ppermute | solution.py:442
  42.6 1.9 collective-permute-start.3
  44.5 1.2 pad_maximum_fusion.1
  45.7 1.0 fusion.27
  46.8 1.8 fusion.2
  48.5 1.2 pad_maximum_fusion
  49.8 0.5 fusion
  50.3 0.3 reverse.5
  50.6 0.6 copy.13.inv_ref
  51.2 1.3 pad.31.win_ref
  52.5 5.1 %shard_map.120 = (f32[4,256,128]{2,1,0:T(8,128)}, f32[4,256,128]{2,1,0:T(8,128)}) custom-call(bf16[4,256,512]{2,1,0:T(8,128)(2,1)} %get-tuple-element.100.ev_ref, bf16[4,384,512]{2,1,0:T(8,128)(2,1)} %pad.31.win_ref, f32[4,1,384]{2,1,0:T(1,128)} %copy.13.inv_ref), custom_call_target="tpu_custom_call" | custom-call | tf_op jit(solution)/shard_map/pallas_call | solution.py:370
  57.6 1.2 slice.163
  58.9 0.7 slice.164
  59.6 1.3 slice.165
  60.9 0.7 slice.166
  61.6 1.6 multiply_reduce_fusion
  63.2 1.4 select_reduce_fusion
  64.6 1.9 multiply_reduce_fusion.1
  66.7 0.8 pad.34.at_ref
  67.5 0.8 pad.33.gd_ref
  68.3 5.4 %shard_map.121 = (f32[4,256,512]{2,1,0:T(8,128)}, f32[4,384,512]{2,1,0:T(8,128)}, f32[4,1,384]{2,1,0:T(1,128)}) custom-call(bf16[4,256,128]{2,1,0:T(8,128)(2,1)} %pad.33.gd_ref, f32[4,256,128]{2,1,0:T(8,128)} %pad.34.at_ref, bf16[4,256,512]{2,1,0:T(8,128)(2,1)} %get-tuple-element.100.ev_ref, bf16[4,384,512]{2,1,0:T(8,128)(2,1)} %pad.31.win_ref), custom_call_target="tpu_custom_call" | custom-call | tf_op jit(solution)/shard_map/pallas_call | solution.py:407
  73.7 2.0 %fusion.4 = bf16[4,256,512]{2,1,0:T(8,128)(2,1)S(1)} fusion(f32[4,256,512]{2,1,0:T(8,128)} %get-tuple-element.67, bf16[4,256,512]{2,1,0:T(8,128)(2,1)S(1)} %copy-done.1, f32[4,256]{1,0:T(4,128)S(1)} %fusion.24), kind=kLoop, calls=%fused_computation.8 | loop fusion | flops 2097152 | bytes 4198400 | tf_op jit(solution)/shard_map/convert_element_type | solution.py:584
  75.9 0.8 convolution_bitcast_fusion.refs_3_
  76.7 1.1 copy-done.2
  77.8 0.3 fusion.1
  78.2 1.9 collective-permute-start.4
  80.1 3.8 %collective-permute-start.5 = (f32[4,15,512]{2,1,0:T(8,128)S(1)}, f32[4,15,512]{2,1,0:T(8,128)S(1)}, u32[]{:S(2)}, u32[]{:S(2)}) collective-permute-start(f32[4,15,512]{2,1,0:T(8,128)S(1)} %get-tuple-element.81), channel_id=1, source_target_pairs={{0,1},{1,2},{2,3},{3,4},{4,5},{5,6},{6,7},{8,9},{9,10},{10,11},{11... | collective-permute-start | bytes 368648 | tf_op jit(solution)/shard_map/ppermute | solution.py:454
  84.0 1.2 fusion.11
  85.2 0.2 copy-done.4
  85.4 2.1 %fusion.35.refs_1_ = f32[768,512]{1,0:T(8,128)} fusion(bf16[1024,768]{1,0:T(8,128)(2,1)S(1)} %bitcast.95, bf16[1024,512]{1,0:T(8,128)(2,1)S(1)} %fusion.11), kind=kOutput, calls=%fused_computation.82 | convolution fusion | flops 805306368 | bytes 4194304 | tf_op jit(solution)/shard_map/rk,re->ke/dot_general | solution.py:510
  87.5 1.6 slice.185
  89.1 0.6 scatter.9.refs_4_
  89.8 1.6 scatter-add.6
  91.4 0.9 slice_add_fusion
  92.3 1.7 scatter-add.9
  94.0 1.9 convert_element_type.63
  95.9 0.3 copy-done.16
  96.2 0.8 convolution_bitcast_fusion.1.refs_2_
  97.0 0.2 copy-done.14
  97.3 1.2 fusion.18
  98.5 0.2 copy-done.3
  98.7 2.1 %fusion.34.refs_0_ = f32[768,512]{1,0:T(8,128)} fusion(bf16[1024,768]{1,0:T(8,128)(2,1)S(1)} %bitcast.94, bf16[1024,512]{1,0:T(8,128)(2,1)S(1)} %fusion.18), kind=kOutput, calls=%fused_computation.81 | convolution fusion | flops 805306368 | bytes 4194304 | tf_op jit(solution)/shard_map/rk,re->ke/dot_general | solution.py:510
  100.8 94.1 %shard_map.122 = (f32[768,512]{1,0:T(8,128)S(1)}, f32[768,512]{1,0:T(8,128)}, f32[512,512]{1,0:T(8,128)S(1)}, f32[512,512]{1,0:T(8,128)S(1)}, f32[8,128]{1,0:T(8,128)S(1)}) custom-call(f32[768,512]{1,0:T(8,128)} %fusion.34.refs_0_, f32[768,512]{1,0:T(8,128)} %fusion.35.refs_1_, f32[512,512]{1,0:T(8,128)S(1)} %convolution_bitcast_fusion.1.refs_2_, ...), custom_call_target="tpu_custom_call" | custom-call | tf_op jit(solution)/shard_map/pallas_call | solution.py:325
  194.9 0.5 slice.174
  196.1 1.1 copy.26
  197.3 1.0 copy.27
  198.2 1.1 copy.28
  199.4 1.0 copy.29
  (50 shorter events, 0.8 us)
Async XLA Ops:
  0.6 34.4 %copy-start = (bf16[3,256,512]{2,1,0:T(8,128)(2,1)S(1)}, bf16[3,256,512]{2,1,0:T(8,128)(2,1)}, u32[]{:S(2)}) copy-start(bf16[3,256,512]{2,1,0:T(8,128)(2,1)} %param.20) | copy-start | bytes 2359300
  1.5 31.4 %collective-permute-start = (bf16[2,4,1,256]{3,2,1,0:T(2,128)(2,1)S(1)}, bf16[2,4,1,256]{3,2,1,0:T(2,128)(2,1)S(1)}, u32[]{:S(2)}, u32[]{:S(2)}) collective-permute-start(bf16[2,4,1,256]{3,2,1,0:T(2,128)(2,1)S(1)} %get-tuple-element.88), channel_id=1, source_target_pairs={{0,1},{1,2},{2,3},{3,4},{4,5},{5,6},{6,7},{8,9},{9,10},{10,11},{11... | collective-permute-start | bytes 12296 | tf_op jit(solution)/shard_map/ppermute | solution.py:442
  6.5 26.4 %collective-permute-start.1 = (bf16[2,4,1,256]{3,2,1,0:T(2,128)(2,1)S(1)}, bf16[2,4,1,256]{3,2,1,0:T(2,128)(2,1)S(1)}, u32[]{:S(2)}, u32[]{:S(2)}) collective-permute-start(bf16[2,4,1,256]{3,2,1,0:T(2,128)(2,1)S(1)} %get-tuple-element.89), channel_id=1, source_target_pairs={{1,0},{2,1},{3,2},{4,3},{5,4},{6,5},{7,6},{9,8},{10,9},{11,10},{12... | collective-permute-start | bytes 12296 | tf_op jit(solution)/shard_map/ppermute | solution.py:444
  8.4 1.5 copy-start.6
  35.1 1.0 copy-start.13
  36.1 1.4 copy-start.15
  37.5 8.2 %copy-start.10 = (bf16[3,256,512]{2,1,0:T(8,128)(2,1)S(1)}, bf16[3,256,512]{2,1,0:T(8,128)(2,1)}, u32[]{:S(2)}) copy-start(bf16[3,256,512]{2,1,0:T(8,128)(2,1)} %param.22) | copy-start | bytes 2359300
  37.5 12.3 %collective-permute-start.2 = (bf16[4,15,512]{2,1,0:T(8,128)(2,1)S(1)}, bf16[4,15,512]{2,1,0:T(8,128)(2,1)S(1)}, u32[]{:S(2)}, u32[]{:S(2)}) collective-permute-start(bf16[4,15,512]{2,1,0:T(8,128)(2,1)S(1)} %get-tuple-element.86), channel_id=1, source_target_pairs={{0,1},{1,2},{2,3},{3,4},{4,5},{5,6},{6,7},{8,9},{9,10},{10,11},{11... | collective-permute-start | bytes 184328 | tf_op jit(solution)/shard_map/ppermute | solution.py:442
  42.6 7.2 %collective-permute-start.3 = (bf16[4,15,512]{2,1,0:T(8,128)(2,1)S(1)}, bf16[4,15,512]{2,1,0:T(8,128)(2,1)S(1)}, u32[]{:S(2)}, u32[]{:S(2)}) collective-permute-start(bf16[4,15,512]{2,1,0:T(8,128)(2,1)S(1)} %get-tuple-element.87), channel_id=1, source_target_pairs={{1,0},{2,1},{3,2},{4,3},{5,4},{6,5},{7,6},{9,8},{10,9},{11,10},{12... | collective-permute-start | bytes 184328 | tf_op jit(solution)/shard_map/ppermute | solution.py:444
  45.7 1.0 copy-start.11
  46.8 1.8 copy-start.17
  48.5 1.8 copy-start.7
  61.6 4.9 %copy-start.8 = (f32[4,256]{1,0:T(4,128)S(1)}, f32[4,256]{1,0:T(4,128)}, u32[]{:S(2)}) copy-start(f32[4,256]{1,0:T(4,128)} %copy-done.7) | copy-start | bytes 12292
  67.5 6.2 %copy-start.1 = (bf16[4,256,512]{2,1,0:T(8,128)(2,1)S(1)}, bf16[4,256,512]{2,1,0:T(8,128)(2,1)}, u32[]{:S(2)}) copy-start(bf16[4,256,512]{2,1,0:T(8,128)(2,1)} %get-tuple-element.100.ev_ref) | copy-start | bytes 3145732
  73.7 2.2 %copy-start.18 = (f32[4,256,512]{2,1,0:T(8,128)S(1)}, f32[4,256,512]{2,1,0:T(8,128)}, u32[]{:S(2)}) copy-start(f32[4,256,512]{2,1,0:T(8,128)} %copy-done.17) | copy-start | bytes 6291460
  75.9 0.8 copy-start.9
  75.9 1.9 copy-start.2
  77.8 6.1 %copy-start.12 = (bf16[512,512]{1,0:T(8,128)(2,1)S(1)}, bf16[512,512]{1,0:T(8,128)(2,1)}, u32[]{:S(2)}) copy-start(bf16[512,512]{1,0:T(8,128)(2,1)} %param.23) | copy-start | bytes 1572868
  78.2 11.6 %collective-permute-start.4 = (f32[4,15,512]{2,1,0:T(8,128)S(1)}, f32[4,15,512]{2,1,0:T(8,128)S(1)}, u32[]{:S(2)}, u32[]{:S(2)}) collective-permute-start(f32[4,15,512]{2,1,0:T(8,128)S(1)} %get-tuple-element.82), channel_id=1, source_target_pairs={{1,0},{2,1},{3,2},{4,3},{5,4},{6,5},{7,6},{9,8},{10,9},{11,10},{12... | collective-permute-start | bytes 368648 | tf_op jit(solution)/shard_map/ppermute | solution.py:454
  80.1 11.3 %collective-permute-start.5 = (f32[4,15,512]{2,1,0:T(8,128)S(1)}, f32[4,15,512]{2,1,0:T(8,128)S(1)}, u32[]{:S(2)}, u32[]{:S(2)}) collective-permute-start(f32[4,15,512]{2,1,0:T(8,128)S(1)} %get-tuple-element.81), channel_id=1, source_target_pairs={{0,1},{1,2},{2,3},{3,4},{4,5},{5,6},{6,7},{8,9},{9,10},{10,11},{11... | collective-permute-start | bytes 368648 | tf_op jit(solution)/shard_map/ppermute | solution.py:454
  84.0 1.4 copy-start.4
  94.0 2.2 %copy-start.16 = (f32[4,256,512]{2,1,0:T(8,128)S(1)}, f32[4,256,512]{2,1,0:T(8,128)}, u32[]{:S(2)}) copy-start(f32[4,256,512]{2,1,0:T(8,128)} %copy-done.15) | copy-start | bytes 6291460
  96.2 1.0 copy-start.14
  97.3 1.4 copy-start.3
  196.1 2.1 %copy-start.5 = (f32[768,512]{1,0:T(8,128)S(1)}, f32[768,512]{1,0:T(8,128)}, u32[]{:S(2)}) copy-start(f32[768,512]{1,0:T(8,128)} %get-tuple-element.71) | copy-start | bytes 4718596

commit v11 on v9

--- a/solution.py
+++ b/solution.py
@@ -358,9 +358,16 @@
     m = lax.dot_general(
         ev_ref[...], win_rev, (((1,), (1,)), ((), ())), preferred_element_type=jnp.float32
     )
-    dots_ref[...] = pltpu.roll(m, 0, 1, stride=1, stride_axis=0)[:, wide - lanes :]
+    rows = lax.broadcasted_iota(jnp.int32, (lanes, lanes), 0)
+    cols = lax.broadcasted_iota(jnp.int32, (lanes, lanes), 1)
+    back = (rows + cols == lanes - 1).astype(jnp.float32)
+
+    def unflip(x):
+        return jnp.dot(x, back, precision=lax.Precision.HIGHEST, preferred_element_type=jnp.float32)
+
+    dots_ref[...] = unflip(pltpu.roll(m, 0, 1, stride=1, stride_axis=0)[:, wide - lanes :])
     inv = jnp.broadcast_to(inv_ref[...], m.shape)
-    strip_ref[...] = pltpu.roll(inv, 0, 1, stride=1, stride_axis=0)[:, wide - lanes :]
+    strip_ref[...] = unflip(pltpu.roll(inv, 0, 1, stride=1, stride_axis=0)[:, wide - lanes :])
 
 
 def corr_fwd(emb_v, win_pad, inv_pad):
@@ -534,14 +541,14 @@
     wide_pad = -(-wide_len // 128) * 128
     win_pad = jnp.pad(window, ((0, 0), (0, wide_pad - wide_len), (0, 0)))
     inv_pad = jnp.pad(inv_win, ((0, 0), (0, wide_pad - wide_len)))[:, None, :]
-    dots_rev, strip_rev = corr_fwd(emb_v, win_pad, inv_pad[:, :, ::-1])
-    lagged_inner_terms = dots_rev[:, :, ::-1][:, :, :offsets]
-    reciprocal_lag_strip = strip_rev[:, :, ::-1][:, :, :offsets]
+    lagged_inner_terms, reciprocal_lag_strip = corr_fwd(emb_v, win_pad, inv_pad[:, :, ::-1])
+    lanes_used = lagged_inner_terms.shape[2]
     frame_ids = first_frame + jnp.arange(frame_num, dtype=jnp.int32)
-    shifts = jnp.arange(offsets, dtype=jnp.int32) - SPAN
+    shifts = jnp.arange(lanes_used, dtype=jnp.int32) - SPAN
     positions = frame_ids[:, None] + shifts[None, :]
     inside = frame_ids[None, :] < lengths[:, None]
     valid = inside[:, :, None] & (positions[None] >= 0) & (positions[None] < lengths[:, None, None])
+    valid = valid & (shifts < offsets - SPAN)[None, None, :]
     target_pos = frame_ids[None, :] + labels[:, None]
     counted = inside & (target_pos >= 0) & (target_pos < lengths[:, None])
     correct_lag_position = (shifts[None, :] == labels[:, None]).astype(jnp.float32)
@@ -566,9 +573,8 @@
     ).astype(jnp.bfloat16)
     grad_inv_v = jnp.sum(logit_derivative * lagged_inner_terms * reciprocal_lag_strip, axis=2)
     audio_term = logit_derivative * lagged_inner_terms * reciprocal_visual_length[:, :, None]
-    band_pad = ((0, 0), (0, 0), (0, 128 - offsets))
     lip_sum, win_sum_pad, ginv_pad = corr_bwd(
-        jnp.pad(grad_dots, band_pad), jnp.pad(audio_term, band_pad), emb_v, win_pad
+        grad_dots, audio_term, emb_v, win_pad
     )
     grad_inv_win = ginv_pad[:, 0, :wide_len]
     lip_vals = emb_v.astype(jnp.float32)

time: 201 us -> 195 us (0.970)
  local copies, waits for them, and re-layouts: 24.2 us -> 18.5 us
    slice x4 -> x0, local copies, waits for them, and re-layouts: 3.94 us -> none  [the longest x2 1.98 us: shards(): reciprocal_lag_strip = strip_rev[:, :, ::-1][:, :, :offsets]]
    unnamed x42 -> x40, local copies, waits for them, and re-layouts: 7.33 us -> 7.33 us
  transfers between devices with their start and end apart: 6 -> 6, of which waited for: 0 -> 0; matrix products, arithmetic and copies ran while one was open for 10% -> 9% of each run, Pallas kernels for 8% -> 8%
where the time goes in v11:
time: 195 us; the launch traced here: 194 us
  Pallas kernels  120 us (62%)
  other arithmetic  19.8 us (10%)
  starting transfers between devices  19.6 us (10%)
  local copies, waits for them, and re-layouts  18.5 us (9%)
  matrix products  12.6 us (6%)
  between operations  3.46 us (2%)
    pallas_call x1, Pallas kernels, all_sum(): pl.pallas_call(functools.partial(_kernel, sizes), out_shape=tuple((jax.Sh...  92.8 us
    pallas_call x1, Pallas kernels, small_sum(): pl.pallas_call(functools.partial(_small_kernel, names), out_shape=jax.Sha...  16 us
    ppermute x2, starting transfers between devices, padded_2(): lax.ppermute(tail, axis, [(i, (i + 1) % count) for i in range(ends)])  9.97 us
    unnamed x40, local copies, waits for them, and re-layouts  7.33 us
    pallas_call x1, Pallas kernels, corr_fwd(): pl.pallas_call(_corr_fwd_kernel, grid=(clips,), in_specs=[pl.BlockSpec((N...  6 us
    ppermute x2, starting transfers between devices, from_behind(): lax.ppermute(value, axis, [(source, source + steps) for source in range(i...  5.75 us
    pallas_call x1, Pallas kernels, corr_bwd(): pl.pallas_call(_corr_bwd_kernel, grid=(clips,), in_specs=[pl.BlockSpec((N...  5.44 us
    dot_general x2, matrix products, conv_grad(): jnp.einsum('rk,re->ke', columns, grad_before, preferred_element_type=jnp....  4.29 us
  transfers between devices with their start and end apart: 6, of which 0 were waited for; matrix products, arithmetic and copies ran while one was open for 9% of the time, Pallas kernels for 8%

profile of v11, /device:TPU:1, one launch (start us, length us, event | category | flops | bytes accessed | tf_op | source)
XLA Modules:
  0.0 194.2 jit_solution(2802491805891770069)
XLA Ops:
  0.6 0.0 copy-start
  0.6 0.9 pad_maximum_fusion.5
  1.5 4.9 %collective-permute-start = (bf16[2,4,1,256]{3,2,1,0:T(2,128)(2,1)S(1)}, bf16[2,4,1,256]{3,2,1,0:T(2,128)(2,1)S(1)}, u32[]{:S(2)}, u32[]{:S(2)}) collective-permute-start(bf16[2,4,1,256]{3,2,1,0:T(2,128)(2,1)S(1)} %get-tuple-element.88), channel_id=1, source_target_pairs={{0,1},{1,2},{2,3},{3,4},{4,5},{5,6},{6,7},{8,9},{9,10},{10,11},{11... | collective-permute-start | bytes 12296 | tf_op jit(solution)/shard_map/ppermute | solution.py:449
  6.5 1.9 collective-permute-start.1
  8.4 0.1 broadcast_add_fusion
  8.5 0.1 broadcast_compare_fusion
  8.6 0.7 broadcast_compare_fusion.1
  9.4 0.7 compare_convert_fusion
  10.1 1.3 subtract_reduce_fusion
  11.4 1.2 scatter.6.t_ref
  12.6 16.0 %shard_map.119 = s32[8,128]{1,0:T(8,128)} custom-call(s32[8,128]{1,0:T(8,128)} %scatter.6.t_ref), custom_call_target="tpu_custom_call" | custom-call | tf_op jit(solution)/shard_map/pallas_call | solution.py:122
  28.6 1.2 slice.144
  30.5 1.5 pad_maximum_fusion.3
  32.0 0.1 slice_bitcast_fusion
  32.1 0.5 fusion.32
  32.6 1.0 fusion.28
  33.6 0.1 copy-done.12
  33.7 0.8 convolution_convert_fusion
  34.4 0.6 copy-done.14
  35.0 5.0 %collective-permute-start.2 = (bf16[4,15,512]{2,1,0:T(8,128)(2,1)S(1)}, bf16[4,15,512]{2,1,0:T(8,128)(2,1)S(1)}, u32[]{:S(2)}, u32[]{:S(2)}) collective-permute-start(bf16[4,15,512]{2,1,0:T(8,128)(2,1)S(1)} %get-tuple-element.86), channel_id=1, source_target_pairs={{0,1},{1,2},{2,3},{3,4},{4,5},{5,6},{6,7},{8,9},{9,10},{10,11},{11... | collective-permute-start | bytes 184328 | tf_op jit(solution)/shard_map/ppermute | solution.py:449
  40.1 1.9 collective-permute-start.3
  42.0 1.2 pad_maximum_fusion.1
  43.3 1.0 fusion.27
  44.2 0.1 copy-done.10
  44.3 1.8 fusion.2
  46.1 1.2 pad_maximum_fusion
  47.3 0.5 fusion
  47.9 0.3 reverse.3
  48.1 0.6 copy.13.inv_ref
  48.7 1.3 pad.23.win_ref
  50.0 6.0 %shard_map.120 = (f32[4,256,128]{2,1,0:T(8,128)}, f32[4,256,128]{2,1,0:T(8,128)}) custom-call(bf16[4,256,512]{2,1,0:T(8,128)(2,1)} %get-tuple-element.100.ev_ref, bf16[4,384,512]{2,1,0:T(8,128)(2,1)} %pad.23.win_ref, f32[4,1,384]{2,1,0:T(1,128)} %copy.13.inv_ref), custom_call_target="tpu_custom_call" | custom-call | tf_op jit(solution)/shard_map/pallas_call | solution.py:377
  56.0 1.9 multiply_reduce_fusion
  57.9 0.7 select_reduce_fusion
  58.6 2.6 %multiply_reduce_fusion.1 = (f32[4,256]{1,0:T(4,128)S(1)}, f32[4,256,128]{2,1,0:T(8,128)S(1)}, bf16[4,256,128]{2,1,0:T(8,128)(2,1)}) fusion(f32[4,256,128]{2,1,0:T(8,128)} %get-tuple-element.64, f32[4,256,128]{2,1,0:T(8,128)} %get-tuple-element.63, f32[4,128]{1,0:T(4,128)S(1)} %compare_convert_fusion, f32[4,256]{1,0:T(4,128)S(1)} %get-tuple-element.76, ...), kind=kLoop, calls=%fused_computation.42 | loop fusion | flops 2096128 | bytes 2022544 | tf_op jit(solution)/shard_map/reduce_sum | solution.py:574
  61.3 1.0 broadcast_multiply_fusion.at_ref
  62.3 5.4 %shard_map.121 = (f32[4,256,512]{2,1,0:T(8,128)}, f32[4,384,512]{2,1,0:T(8,128)}, f32[4,1,384]{2,1,0:T(1,128)}) custom-call(bf16[4,256,128]{2,1,0:T(8,128)(2,1)} %get-tuple-element.83.gd_ref, f32[4,256,128]{2,1,0:T(8,128)} %broadcast_multiply_fusion.at_ref, bf16[4,256,512]{2,1,0:T(8,128)(2,1)} %get-tuple-element.100.ev_ref, bf16[4,384,512]{2,1,0:T(8,128)(2,1)} %pad.23.win_ref), custom_call_target="tpu_custom_call" | custom-call | tf_op jit(solution)/shard_map/pallas_call | solution.py:414
  67.7 2.1 %fusion.4 = bf16[4,256,512]{2,1,0:T(8,128)(2,1)S(1)} fusion(f32[4,256,512]{2,1,0:T(8,128)} %get-tuple-element.67, bf16[4,256,512]{2,1,0:T(8,128)(2,1)S(1)} %copy-done.1, f32[4,256]{1,0:T(4,128)S(1)} %fusion.24), kind=kLoop, calls=%fused_computation.8 | loop fusion | flops 2097152 | bytes 4198400 | tf_op jit(solution)/shard_map/convert_element_type | solution.py:590
  69.8 0.1 copy-done.17
  70.0 0.8 convolution_bitcast_fusion.refs_3_
  70.8 1.1 copy-done.2
  71.9 0.3 fusion.1
  72.2 1.9 collective-permute-start.4
  74.2 3.8 %collective-permute-start.5 = (f32[4,15,512]{2,1,0:T(8,128)S(1)}, f32[4,15,512]{2,1,0:T(8,128)S(1)}, u32[]{:S(2)}, u32[]{:S(2)}) collective-permute-start(f32[4,15,512]{2,1,0:T(8,128)S(1)} %get-tuple-element.81), channel_id=1, source_target_pairs={{0,1},{1,2},{2,3},{3,4},{4,5},{5,6},{6,7},{8,9},{9,10},{10,11},{11... | collective-permute-start | bytes 368648 | tf_op jit(solution)/shard_map/ppermute | solution.py:461
  78.0 1.2 fusion.11
  79.2 0.2 copy-done.4
  79.4 2.1 %fusion.35.refs_1_ = f32[768,512]{1,0:T(8,128)} fusion(bf16[1024,768]{1,0:T(8,128)(2,1)S(1)} %bitcast.95, bf16[1024,512]{1,0:T(8,128)(2,1)S(1)} %fusion.11), kind=kOutput, calls=%fused_computation.83 | convolution fusion | flops 805306368 | bytes 4194304 | tf_op jit(solution)/shard_map/rk,re->ke/dot_general | solution.py:517
  81.6 1.6 slice.169
  83.2 0.6 scatter.9.refs_4_
  83.8 1.6 scatter-add.6
  85.4 0.9 slice_add_fusion
  86.4 1.7 scatter-add.9
  88.0 1.9 convert_element_type.59
  89.9 0.3 copy-done.15
  90.2 0.8 convolution_bitcast_fusion.1.refs_2_
  91.0 0.3 copy-done.13
  91.3 1.1 fusion.18
  92.4 0.2 copy-done.3
  92.7 2.1 %fusion.34.refs_0_ = f32[768,512]{1,0:T(8,128)} fusion(bf16[1024,768]{1,0:T(8,128)(2,1)S(1)} %bitcast.94, bf16[1024,512]{1,0:T(8,128)(2,1)S(1)} %fusion.18), kind=kOutput, calls=%fused_computation.82 | convolution fusion | flops 805306368 | bytes 4194304 | tf_op jit(solution)/shard_map/rk,re->ke/dot_general | solution.py:517
  94.8 92.8 %shard_map.122 = (f32[768,512]{1,0:T(8,128)S(1)}, f32[768,512]{1,0:T(8,128)}, f32[512,512]{1,0:T(8,128)S(1)}, f32[512,512]{1,0:T(8,128)S(1)}, f32[8,128]{1,0:T(8,128)S(1)}) custom-call(f32[768,512]{1,0:T(8,128)} %fusion.34.refs_0_, f32[768,512]{1,0:T(8,128)} %fusion.35.refs_1_, f32[512,512]{1,0:T(8,128)S(1)} %convolution_bitcast_fusion.1.refs_2_, ...), custom_call_target="tpu_custom_call" | custom-call | tf_op jit(solution)/shard_map/pallas_call | solution.py:325
  187.7 0.5 slice.158
  188.9 1.1 copy.26
  190.0 1.0 copy.27
  191.0 1.1 copy.28
  192.1 1.0 copy.29
  (43 shorter events, 0.2 us)
Async XLA Ops:
  0.6 32.0 %copy-start = (bf16[3,256,512]{2,1,0:T(8,128)(2,1)S(1)}, bf16[3,256,512]{2,1,0:T(8,128)(2,1)}, u32[]{:S(2)}) copy-start(bf16[3,256,512]{2,1,0:T(8,128)(2,1)} %param.20) | copy-start | bytes 2359300
  1.5 29.0 %collective-permute-start = (bf16[2,4,1,256]{3,2,1,0:T(2,128)(2,1)S(1)}, bf16[2,4,1,256]{3,2,1,0:T(2,128)(2,1)S(1)}, u32[]{:S(2)}, u32[]{:S(2)}) collective-permute-start(bf16[2,4,1,256]{3,2,1,0:T(2,128)(2,1)S(1)} %get-tuple-element.88), channel_id=1, source_target_pairs={{0,1},{1,2},{2,3},{3,4},{4,5},{5,6},{6,7},{8,9},{9,10},{10,11},{11... | collective-permute-start | bytes 12296 | tf_op jit(solution)/shard_map/ppermute | solution.py:449
  6.5 24.1 %collective-permute-start.1 = (bf16[2,4,1,256]{3,2,1,0:T(2,128)(2,1)S(1)}, bf16[2,4,1,256]{3,2,1,0:T(2,128)(2,1)S(1)}, u32[]{:S(2)}, u32[]{:S(2)}) collective-permute-start(bf16[2,4,1,256]{3,2,1,0:T(2,128)(2,1)S(1)} %get-tuple-element.89), channel_id=1, source_target_pairs={{1,0},{2,1},{3,2},{4,3},{5,4},{6,5},{7,6},{9,8},{10,9},{11,10},{12... | collective-permute-start | bytes 12296 | tf_op jit(solution)/shard_map/ppermute | solution.py:451
  32.6 1.0 copy-start.12
  33.7 1.4 copy-start.14
  35.0 8.2 %copy-start.9 = (bf16[3,256,512]{2,1,0:T(8,128)(2,1)S(1)}, bf16[3,256,512]{2,1,0:T(8,128)(2,1)}, u32[]{:S(2)}) copy-start(bf16[3,256,512]{2,1,0:T(8,128)(2,1)} %param.22) | copy-start | bytes 2359300
  35.0 12.3 %collective-permute-start.2 = (bf16[4,15,512]{2,1,0:T(8,128)(2,1)S(1)}, bf16[4,15,512]{2,1,0:T(8,128)(2,1)S(1)}, u32[]{:S(2)}, u32[]{:S(2)}) collective-permute-start(bf16[4,15,512]{2,1,0:T(8,128)(2,1)S(1)} %get-tuple-element.86), channel_id=1, source_target_pairs={{0,1},{1,2},{2,3},{3,4},{4,5},{5,6},{6,7},{8,9},{9,10},{10,11},{11... | collective-permute-start | bytes 184328 | tf_op jit(solution)/shard_map/ppermute | solution.py:449
  40.1 7.2 %collective-permute-start.3 = (bf16[4,15,512]{2,1,0:T(8,128)(2,1)S(1)}, bf16[4,15,512]{2,1,0:T(8,128)(2,1)S(1)}, u32[]{:S(2)}, u32[]{:S(2)}) collective-permute-start(bf16[4,15,512]{2,1,0:T(8,128)(2,1)S(1)} %get-tuple-element.87), channel_id=1, source_target_pairs={{1,0},{2,1},{3,2},{4,3},{5,4},{6,5},{7,6},{9,8},{10,9},{11,10},{12... | collective-permute-start | bytes 184328 | tf_op jit(solution)/shard_map/ppermute | solution.py:451
  43.3 1.0 copy-start.10
  44.3 1.8 copy-start.16
  48.7 7.3 %copy-start.6 = (s32[4]{0:T(128)S(1)}, s32[4]{0:T(128)}, u32[]{:S(2)}) copy-start(s32[4]{0:T(128)} %param.18) | copy-start | bytes 52
  50.0 7.9 %copy-start.8 = (s32[4]{0:T(128)S(1)}, s32[4]{0:T(128)}, u32[]{:S(2)}) copy-start(s32[4]{0:T(128)} %param.19) | copy-start | bytes 52
  61.3 6.5 %copy-start.1 = (bf16[4,256,512]{2,1,0:T(8,128)(2,1)S(1)}, bf16[4,256,512]{2,1,0:T(8,128)(2,1)}, u32[]{:S(2)}) copy-start(bf16[4,256,512]{2,1,0:T(8,128)(2,1)} %get-tuple-element.100.ev_ref) | copy-start | bytes 3145732
  67.7 2.2 %copy-start.17 = (f32[4,256,512]{2,1,0:T(8,128)S(1)}, f32[4,256,512]{2,1,0:T(8,128)}, u32[]{:S(2)}) copy-start(f32[4,256,512]{2,1,0:T(8,128)} %copy-done.16) | copy-start | bytes 6291460
  70.0 0.8 copy-start.7
  70.0 1.9 copy-start.2
  71.9 6.1 %copy-start.11 = (bf16[512,512]{1,0:T(8,128)(2,1)S(1)}, bf16[512,512]{1,0:T(8,128)(2,1)}, u32[]{:S(2)}) copy-start(bf16[512,512]{1,0:T(8,128)(2,1)} %param.23) | copy-start | bytes 1572868
  72.2 11.6 %collective-permute-start.4 = (f32[4,15,512]{2,1,0:T(8,128)S(1)}, f32[4,15,512]{2,1,0:T(8,128)S(1)}, u32[]{:S(2)}, u32[]{:S(2)}) collective-permute-start(f32[4,15,512]{2,1,0:T(8,128)S(1)} %get-tuple-element.82), channel_id=1, source_target_pairs={{1,0},{2,1},{3,2},{4,3},{5,4},{6,5},{7,6},{9,8},{10,9},{11,10},{12... | collective-permute-start | bytes 368648 | tf_op jit(solution)/shard_map/ppermute | solution.py:461
  74.2 11.3 %collective-permute-start.5 = (f32[4,15,512]{2,1,0:T(8,128)S(1)}, f32[4,15,512]{2,1,0:T(8,128)S(1)}, u32[]{:S(2)}, u32[]{:S(2)}) collective-permute-start(f32[4,15,512]{2,1,0:T(8,128)S(1)} %get-tuple-element.81), channel_id=1, source_target_pairs={{0,1},{1,2},{2,3},{3,4},{4,5},{5,6},{6,7},{8,9},{9,10},{10,11},{11... | collective-permute-start | bytes 368648 | tf_op jit(solution)/shard_map/ppermute | solution.py:461
  78.0 1.4 copy-start.4
  88.0 2.2 %copy-start.15 = (f32[4,256,512]{2,1,0:T(8,128)S(1)}, f32[4,256,512]{2,1,0:T(8,128)}, u32[]{:S(2)}) copy-start(f32[4,256,512]{2,1,0:T(8,128)} %copy-done.14) | copy-start | bytes 6291460
  90.2 1.0 copy-start.13
  91.3 1.4 copy-start.3
  188.8 2.1 %copy-start.5 = (f32[768,512]{1,0:T(8,128)S(1)}, f32[768,512]{1,0:T(8,128)}, u32[]{:S(2)}) copy-start(f32[768,512]{1,0:T(8,128)} %get-tuple-element.71) | copy-start | bytes 4718596

commit v12 on v11

--- a/solution.py
+++ b/solution.py
@@ -595,8 +595,12 @@
     own_grad = win_sum[:, SPAN : SPAN + frame_num]
     from_after = from_behind(win_sum[:, :SPAN], "tm", -1)
     from_before = from_behind(win_sum[:, frame_num + SPAN :], "tm", 1)
-    own_grad = own_grad.at[:, frame_num - SPAN :].add(from_after)
-    own_grad = own_grad.at[:, :SPAN].add(from_before)
+    body = frame_num - SPAN
+    own_grad = (
+        own_grad
+        + jnp.pad(from_after, ((0, 0), (body, 0), (0, 0)))
+        + jnp.pad(from_before, ((0, 0), (0, body), (0, 0)))
+    )
     grad_audio = own_grad.astype(jnp.bfloat16).reshape(clip_num * frame_num, width)
     grad_lip = grad_lip.reshape(clip_num * frame_num, width)
     grad_ap = proj_grad(hid_a, grad_audio)

time: 195 us -> 188 us (0.964)
  local copies, waits for them, and re-layouts: 18.5 us -> 13.9 us
  other arithmetic: 19.8 us -> 17.3 us
    scatter-add x2 -> x0, local copies, waits for them, and re-layouts: 3.25 us -> none  [the longest x1 1.66 us: shards(): own_grad = own_grad.at[:, :SPAN].add(from_before)]
  transfers between devices with their start and end apart: 6 -> 6, of which waited for: 0 -> 0; matrix products, arithmetic and copies ran while one was open for 9% -> 8% of each run, Pallas kernels for 8% -> 9%
where the time goes in v12:
time: 188 us; the launch traced here: 187 us
  Pallas kernels  120 us (64%)
  starting transfers between devices  19.6 us (10%)
  other arithmetic  17.3 us (9%)
  local copies, waits for them, and re-layouts  13.9 us (7%)
  matrix products  12.7 us (7%)
  between operations  3.46 us (2%)
    pallas_call x1, Pallas kernels, all_sum(): pl.pallas_call(functools.partial(_kernel, sizes), out_shape=tuple((jax.Sh...  92.8 us
    pallas_call x1, Pallas kernels, small_sum(): pl.pallas_call(functools.partial(_small_kernel, names), out_shape=jax.Sha...  16 us
    ppermute x2, starting transfers between devices, padded_2(): lax.ppermute(tail, axis, [(i, (i + 1) % count) for i in range(ends)])  9.97 us
    unnamed x40, local copies, waits for them, and re-layouts  7.34 us
    pallas_call x1, Pallas kernels, corr_fwd(): pl.pallas_call(_corr_fwd_kernel, grid=(clips,), in_specs=[pl.BlockSpec((N...  6 us
    ppermute x2, starting transfers between devices, from_behind(): lax.ppermute(value, axis, [(source, source + steps) for source in range(i...  5.75 us
    pallas_call x1, Pallas kernels, corr_bwd(): pl.pallas_call(_corr_bwd_kernel, grid=(clips,), in_specs=[pl.BlockSpec((N...  5.44 us
    dot_general x2, matrix products, conv_grad(): jnp.einsum('rk,re->ke', columns, grad_before, preferred_element_type=jnp....  4.29 us
  transfers between devices with their start and end apart: 6, of which 0 were waited for; matrix products, arithmetic and copies ran while one was open for 8% of the time, Pallas kernels for 9%

profile of v12, /device:TPU:1, one launch (start us, length us, event | category | flops | bytes accessed | tf_op | source)
XLA Modules:
  0.0 187.1 jit_solution(14198826907003703305)
XLA Ops:
  0.6 0.0 copy-start
  0.6 0.9 pad_maximum_fusion.5
  1.5 4.9 %collective-permute-start = (bf16[2,4,1,256]{3,2,1,0:T(2,128)(2,1)S(1)}, bf16[2,4,1,256]{3,2,1,0:T(2,128)(2,1)S(1)}, u32[]{:S(2)}, u32[]{:S(2)}) collective-permute-start(bf16[2,4,1,256]{3,2,1,0:T(2,128)(2,1)S(1)} %get-tuple-element.64), channel_id=1, source_target_pairs={{0,1},{1,2},{2,3},{3,4},{4,5},{5,6},{6,7},{8,9},{9,10},{10,11},{11... | collective-permute-start | bytes 12296 | tf_op jit(solution)/shard_map/ppermute | solution.py:449
  6.5 1.9 %collective-permute-start.1 = (bf16[2,4,1,256]{3,2,1,0:T(2,128)(2,1)S(1)}, bf16[2,4,1,256]{3,2,1,0:T(2,128)(2,1)S(1)}, u32[]{:S(2)}, u32[]{:S(2)}) collective-permute-start(bf16[2,4,1,256]{3,2,1,0:T(2,128)(2,1)S(1)} %get-tuple-element.65), channel_id=1, source_target_pairs={{1,0},{2,1},{3,2},{4,3},{5,4},{6,5},{7,6},{9,8},{10,9},{11,10},{12... | collective-permute-start | bytes 12296 | tf_op jit(solution)/shard_map/ppermute | solution.py:451
  8.4 0.1 broadcast_add_fusion
  8.5 0.1 broadcast_compare_fusion
  8.6 0.7 broadcast_compare_fusion.1
  9.4 0.7 compare_convert_fusion
  10.1 1.3 subtract_reduce_fusion
  11.4 1.2 scatter.6.t_ref
  12.6 16.0 %shard_map.119 = s32[8,128]{1,0:T(8,128)} custom-call(s32[8,128]{1,0:T(8,128)} %scatter.6.t_ref), custom_call_target="tpu_custom_call" | custom-call | tf_op jit(solution)/shard_map/pallas_call | solution.py:122
  28.6 1.2 slice.95
  30.5 0.0 collective-permute-done.1
  30.5 1.5 pad_maximum_fusion.3
  32.0 0.1 slice_bitcast_fusion
  32.1 0.5 fusion.34
  32.6 0.0 copy-start.12
  32.6 1.0 fusion.30
  33.6 0.1 copy-done.12
  33.7 0.8 convolution_convert_fusion
  34.4 0.6 copy-done.14
  35.0 5.0 %collective-permute-start.2 = (bf16[4,15,512]{2,1,0:T(8,128)(2,1)S(1)}, bf16[4,15,512]{2,1,0:T(8,128)(2,1)S(1)}, u32[]{:S(2)}, u32[]{:S(2)}) collective-permute-start(bf16[4,15,512]{2,1,0:T(8,128)(2,1)S(1)} %get-tuple-element.62), channel_id=1, source_target_pairs={{0,1},{1,2},{2,3},{3,4},{4,5},{5,6},{6,7},{8,9},{9,10},{10,11},{11... | collective-permute-start | bytes 184328 | tf_op jit(solution)/shard_map/ppermute | solution.py:449
  40.1 1.9 %collective-permute-start.3 = (bf16[4,15,512]{2,1,0:T(8,128)(2,1)S(1)}, bf16[4,15,512]{2,1,0:T(8,128)(2,1)S(1)}, u32[]{:S(2)}, u32[]{:S(2)}) collective-permute-start(bf16[4,15,512]{2,1,0:T(8,128)(2,1)S(1)} %get-tuple-element.63), channel_id=1, source_target_pairs={{1,0},{2,1},{3,2},{4,3},{5,4},{6,5},{7,6},{9,8},{10,9},{11,10},{12... | collective-permute-start | bytes 184328 | tf_op jit(solution)/shard_map/ppermute | solution.py:451
  42.0 1.2 pad_maximum_fusion.1
  43.3 1.0 fusion.29
  44.2 0.1 copy-done.10
  44.3 1.8 fusion.2
  46.1 1.2 pad_maximum_fusion
  47.3 0.5 fusion
  47.9 0.3 reverse.3
  48.1 0.6 copy.13.inv_ref
  48.7 1.3 pad.27.win_ref
  50.0 6.0 %shard_map.120 = (f32[4,256,128]{2,1,0:T(8,128)}, f32[4,256,128]{2,1,0:T(8,128)}) custom-call(bf16[4,256,512]{2,1,0:T(8,128)(2,1)} %get-tuple-element.76.ev_ref, bf16[4,384,512]{2,1,0:T(8,128)(2,1)} %pad.27.win_ref, f32[4,1,384]{2,1,0:T(1,128)} %copy.13.inv_ref), custom_call_target="tpu_custom_call" | custom-call | tf_op jit(solution)/shard_map/pallas_call | solution.py:377
  56.0 1.9 multiply_reduce_fusion
  57.9 0.7 select_reduce_fusion
  58.6 2.6 %multiply_reduce_fusion.1 = (f32[4,256]{1,0:T(4,128)S(1)}, f32[4,256,128]{2,1,0:T(8,128)S(1)}, bf16[4,256,128]{2,1,0:T(8,128)(2,1)}) fusion(f32[4,256,128]{2,1,0:T(8,128)} %get-tuple-element.40, f32[4,256,128]{2,1,0:T(8,128)} %get-tuple-element.39, f32[4,128]{1,0:T(4,128)S(1)} %compare_convert_fusion, f32[4,256]{1,0:T(4,128)S(1)} %get-tuple-element.52, ...), kind=kLoop, calls=%fused_computation.45 | loop fusion | flops 2096128 | bytes 2022544 | tf_op jit(solution)/shard_map/reduce_sum | solution.py:574
  61.3 0.0 copy-start.1
  61.3 1.0 broadcast_multiply_fusion.at_ref
  62.3 5.4 %shard_map.121 = (f32[4,256,512]{2,1,0:T(8,128)}, f32[4,384,512]{2,1,0:T(8,128)}, f32[4,1,384]{2,1,0:T(1,128)}) custom-call(bf16[4,256,128]{2,1,0:T(8,128)(2,1)} %get-tuple-element.59.gd_ref, f32[4,256,128]{2,1,0:T(8,128)} %broadcast_multiply_fusion.at_ref, bf16[4,256,512]{2,1,0:T(8,128)(2,1)} %get-tuple-element.76.ev_ref, bf16[4,384,512]{2,1,0:T(8,128)(2,1)} %pad.27.win_ref), custom_call_target="tpu_custom_call" | custom-call | tf_op jit(solution)/shard_map/pallas_call | solution.py:414
  67.7 2.1 %fusion.4 = bf16[4,256,512]{2,1,0:T(8,128)(2,1)S(1)} fusion(f32[4,256,512]{2,1,0:T(8,128)} %get-tuple-element.43, bf16[4,256,512]{2,1,0:T(8,128)(2,1)S(1)} %copy-done.1, f32[4,256]{1,0:T(4,128)S(1)} %fusion.26), kind=kLoop, calls=%fused_computation.8 | loop fusion | flops 2097152 | bytes 4198400 | tf_op jit(solution)/shard_map/convert_element_type | solution.py:590
  69.8 0.1 copy-done.17
  70.0 0.8 convolution_bitcast_fusion.refs_3_
  70.8 1.1 copy-done.2
  71.9 0.3 fusion.1
  72.2 1.9 %collective-permute-start.4 = (f32[4,15,512]{2,1,0:T(8,128)S(1)}, f32[4,15,512]{2,1,0:T(8,128)S(1)}, u32[]{:S(2)}, u32[]{:S(2)}) collective-permute-start(f32[4,15,512]{2,1,0:T(8,128)S(1)} %get-tuple-element.57), channel_id=1, source_target_pairs={{1,0},{2,1},{3,2},{4,3},{5,4},{6,5},{7,6},{9,8},{10,9},{11,10},{12... | collective-permute-start | bytes 368648 | tf_op jit(solution)/shard_map/ppermute | solution.py:461
  74.2 3.8 %collective-permute-start.5 = (f32[4,15,512]{2,1,0:T(8,128)S(1)}, f32[4,15,512]{2,1,0:T(8,128)S(1)}, u32[]{:S(2)}, u32[]{:S(2)}) collective-permute-start(f32[4,15,512]{2,1,0:T(8,128)S(1)} %get-tuple-element.58), channel_id=1, source_target_pairs={{0,1},{1,2},{2,3},{3,4},{4,5},{5,6},{6,7},{8,9},{9,10},{10,11},{11... | collective-permute-start | bytes 368648 | tf_op jit(solution)/shard_map/ppermute | solution.py:461
  78.0 1.2 fusion.13
  79.2 0.2 copy-done.4
  79.4 2.1 %fusion.37.refs_1_ = f32[768,512]{1,0:T(8,128)} fusion(bf16[1024,768]{1,0:T(8,128)(2,1)S(1)} %bitcast.95, bf16[1024,512]{1,0:T(8,128)(2,1)S(1)} %fusion.13), kind=kOutput, calls=%fused_computation.84 | convolution fusion | flops 805306368 | bytes 4194304 | tf_op jit(solution)/shard_map/rk,re->ke/dot_general | solution.py:517
  81.6 0.8 scatter.9.refs_4_
  82.4 0.0 collective-permute-done.5
  82.4 0.3 fusion.6
  82.7 0.4 copy-done.15
  83.2 0.8 convolution_bitcast_fusion.1.refs_2_
  84.0 0.2 copy-done.13
  84.2 1.2 fusion.20
  85.4 0.2 copy-done.3
  85.6 2.1 %fusion.36.refs_0_ = f32[768,512]{1,0:T(8,128)} fusion(bf16[1024,768]{1,0:T(8,128)(2,1)S(1)} %bitcast.94, bf16[1024,512]{1,0:T(8,128)(2,1)S(1)} %fusion.20), kind=kOutput, calls=%fused_computation.83 | convolution fusion | flops 805306368 | bytes 4194304 | tf_op jit(solution)/shard_map/rk,re->ke/dot_general | solution.py:517
  87.8 92.8 %shard_map.122 = (f32[768,512]{1,0:T(8,128)S(1)}, f32[768,512]{1,0:T(8,128)}, f32[512,512]{1,0:T(8,128)S(1)}, f32[512,512]{1,0:T(8,128)S(1)}, f32[8,128]{1,0:T(8,128)S(1)}) custom-call(f32[768,512]{1,0:T(8,128)} %fusion.36.refs_0_, f32[768,512]{1,0:T(8,128)} %fusion.37.refs_1_, f32[512,512]{1,0:T(8,128)S(1)} %convolution_bitcast_fusion.1.refs_2_, ...), custom_call_target="tpu_custom_call" | custom-call | tf_op jit(solution)/shard_map/pallas_call | solution.py:325
  180.6 0.5 slice.107
  181.8 1.1 copy.24
  182.9 1.0 copy.25
  183.9 1.1 copy.26
  185.0 1.0 copy.27
  (38 shorter events, 0.2 us)
Async XLA Ops:
  0.6 32.0 %copy-start = (bf16[3,256,512]{2,1,0:T(8,128)(2,1)S(1)}, bf16[3,256,512]{2,1,0:T(8,128)(2,1)}, u32[]{:S(2)}) copy-start(bf16[3,256,512]{2,1,0:T(8,128)(2,1)} %param.16) | copy-start | bytes 2359300
  1.5 29.0 %collective-permute-start = (bf16[2,4,1,256]{3,2,1,0:T(2,128)(2,1)S(1)}, bf16[2,4,1,256]{3,2,1,0:T(2,128)(2,1)S(1)}, u32[]{:S(2)}, u32[]{:S(2)}) collective-permute-start(bf16[2,4,1,256]{3,2,1,0:T(2,128)(2,1)S(1)} %get-tuple-element.64), channel_id=1, source_target_pairs={{0,1},{1,2},{2,3},{3,4},{4,5},{5,6},{6,7},{8,9},{9,10},{10,11},{11... | collective-permute-start | bytes 12296 | tf_op jit(solution)/shard_map/ppermute | solution.py:449
  6.5 24.1 %collective-permute-start.1 = (bf16[2,4,1,256]{3,2,1,0:T(2,128)(2,1)S(1)}, bf16[2,4,1,256]{3,2,1,0:T(2,128)(2,1)S(1)}, u32[]{:S(2)}, u32[]{:S(2)}) collective-permute-start(bf16[2,4,1,256]{3,2,1,0:T(2,128)(2,1)S(1)} %get-tuple-element.65), channel_id=1, source_target_pairs={{1,0},{2,1},{3,2},{4,3},{5,4},{6,5},{7,6},{9,8},{10,9},{11,10},{12... | collective-permute-start | bytes 12296 | tf_op jit(solution)/shard_map/ppermute | solution.py:451
  32.6 1.0 copy-start.12
  33.7 1.4 copy-start.14
  35.0 8.2 %copy-start.9 = (bf16[3,256,512]{2,1,0:T(8,128)(2,1)S(1)}, bf16[3,256,512]{2,1,0:T(8,128)(2,1)}, u32[]{:S(2)}) copy-start(bf16[3,256,512]{2,1,0:T(8,128)(2,1)} %param.18) | copy-start | bytes 2359300
  35.0 12.3 %collective-permute-start.2 = (bf16[4,15,512]{2,1,0:T(8,128)(2,1)S(1)}, bf16[4,15,512]{2,1,0:T(8,128)(2,1)S(1)}, u32[]{:S(2)}, u32[]{:S(2)}) collective-permute-start(bf16[4,15,512]{2,1,0:T(8,128)(2,1)S(1)} %get-tuple-element.62), channel_id=1, source_target_pairs={{0,1},{1,2},{2,3},{3,4},{4,5},{5,6},{6,7},{8,9},{9,10},{10,11},{11... | collective-permute-start | bytes 184328 | tf_op jit(solution)/shard_map/ppermute | solution.py:449
  40.1 7.2 %collective-permute-start.3 = (bf16[4,15,512]{2,1,0:T(8,128)(2,1)S(1)}, bf16[4,15,512]{2,1,0:T(8,128)(2,1)S(1)}, u32[]{:S(2)}, u32[]{:S(2)}) collective-permute-start(bf16[4,15,512]{2,1,0:T(8,128)(2,1)S(1)} %get-tuple-element.63), channel_id=1, source_target_pairs={{1,0},{2,1},{3,2},{4,3},{5,4},{6,5},{7,6},{9,8},{10,9},{11,10},{12... | collective-permute-start | bytes 184328 | tf_op jit(solution)/shard_map/ppermute | solution.py:451
  43.3 1.0 copy-start.10
  44.3 1.8 copy-start.16
  48.7 7.3 %copy-start.6 = (s32[4]{0:T(128)S(1)}, s32[4]{0:T(128)}, u32[]{:S(2)}) copy-start(s32[4]{0:T(128)} %param.14) | copy-start | bytes 52
  50.0 7.9 %copy-start.8 = (s32[4]{0:T(128)S(1)}, s32[4]{0:T(128)}, u32[]{:S(2)}) copy-start(s32[4]{0:T(128)} %param.15) | copy-start | bytes 52
  61.3 6.5 %copy-start.1 = (bf16[4,256,512]{2,1,0:T(8,128)(2,1)S(1)}, bf16[4,256,512]{2,1,0:T(8,128)(2,1)}, u32[]{:S(2)}) copy-start(bf16[4,256,512]{2,1,0:T(8,128)(2,1)} %get-tuple-element.76.ev_ref) | copy-start | bytes 3145732
  67.7 2.2 %copy-start.17 = (f32[4,256,512]{2,1,0:T(8,128)S(1)}, f32[4,256,512]{2,1,0:T(8,128)}, u32[]{:S(2)}) copy-start(f32[4,256,512]{2,1,0:T(8,128)} %copy-done.16) | copy-start | bytes 6291460
  70.0 0.8 copy-start.7
  70.0 1.9 %copy-start.2 = (f32[4,384,512]{2,1,0:T(8,128)S(1)}, f32[4,384,512]{2,1,0:T(8,128)}, u32[]{:S(2)}) copy-start(f32[4,384,512]{2,1,0:T(8,128)} %get-tuple-element.41) | copy-start | bytes 9437188
  71.9 6.1 %copy-start.11 = (bf16[512,512]{1,0:T(8,128)(2,1)S(1)}, bf16[512,512]{1,0:T(8,128)(2,1)}, u32[]{:S(2)}) copy-start(bf16[512,512]{1,0:T(8,128)(2,1)} %param.19) | copy-start | bytes 1572868
  72.2 10.1 %collective-permute-start.4 = (f32[4,15,512]{2,1,0:T(8,128)S(1)}, f32[4,15,512]{2,1,0:T(8,128)S(1)}, u32[]{:S(2)}, u32[]{:S(2)}) collective-permute-start(f32[4,15,512]{2,1,0:T(8,128)S(1)} %get-tuple-element.57), channel_id=1, source_target_pairs={{1,0},{2,1},{3,2},{4,3},{5,4},{6,5},{7,6},{9,8},{10,9},{11,10},{12... | collective-permute-start | bytes 368648 | tf_op jit(solution)/shard_map/ppermute | solution.py:461
  74.2 8.2 %collective-permute-start.5 = (f32[4,15,512]{2,1,0:T(8,128)S(1)}, f32[4,15,512]{2,1,0:T(8,128)S(1)}, u32[]{:S(2)}, u32[]{:S(2)}) collective-permute-start(f32[4,15,512]{2,1,0:T(8,128)S(1)} %get-tuple-element.58), channel_id=1, source_target_pairs={{0,1},{1,2},{2,3},{3,4},{4,5},{5,6},{6,7},{8,9},{9,10},{10,11},{11... | collective-permute-start | bytes 368648 | tf_op jit(solution)/shard_map/ppermute | solution.py:461
  78.0 1.4 copy-start.4
  81.6 1.6 copy-start.15
  83.2 1.0 copy-start.13
  84.2 1.4 copy-start.3
  181.8 2.1 %copy-start.5 = (f32[768,512]{1,0:T(8,128)S(1)}, f32[768,512]{1,0:T(8,128)}, u32[]{:S(2)}) copy-start(f32[768,512]{1,0:T(8,128)} %get-tuple-element.47) | copy-start | bytes 4718596

commit v13 on v12

--- a/solution.py
+++ b/solution.py
@@ -534,7 +534,8 @@
     cols_a, pre_a, hid_a = (flatten_rows(cols_a), flatten_rows(pre_a), flatten_rows(hid_a))
     cols_v, pre_v, hid_v = (flatten_rows(cols_v), flatten_rows(pre_v), flatten_rows(hid_v))
     count_part = jnp.sum(lengths - jnp.abs(labels))
-    count_block = jnp.zeros((8, 128), jnp.int32).at[0, 0].set(count_part)
+    corner = (lax.broadcasted_iota(jnp.int32, (8, 128), 0) + lax.broadcasted_iota(jnp.int32, (8, 128), 1)) == 0
+    count_block = jnp.where(corner, count_part, 0)
     count = small_sum(count_block, ("k",), 1)[0, 0].astype(jnp.float32)
     inv_win = inverse_norm(window)
     reciprocal_visual_length = inverse_norm(emb_v)
@@ -609,7 +610,7 @@
     grad_vc = conv_grad(cols_v, pre_v, grad_lip, w_lip_proj, w_lip_conv)
     parts = (grad_ac, grad_vc, grad_ap, grad_vp)
     lanes = grad_ap.shape[1]
-    loss_block = jnp.zeros((8, 128), jnp.float32).at[0, 0].set(loss_local)
+    loss_block = jnp.where(corner, loss_local, 0.0)
     *sums, loss_total = all_sum([g.reshape(-1, lanes) for g in parts], loss_block)
     grad_ac, grad_vc, grad_ap, grad_vp = (t.reshape(g.shape) for t, g in zip(sums, parts))
     loss_sum = loss_total[0, 0]

time: 188 us -> 188 us (level)
  local copies, waits for them, and re-layouts: 13.9 us -> 11.8 us
  other arithmetic: 17.3 us -> 19.3 us
    select_n x0 -> x2, other arithmetic: none -> 2.03 us  [the longest x1 1.24 us: shards(): count_block = jnp.where(corner, count_part, 0)]
    scatter x2 -> x0, local copies, waits for them, and re-layouts: 2.02 us -> none  [the longest x1 1.24 us: shards(): count_block = jnp.zeros((8, 128), jnp.int32).at[0, 0].set(count_part)]
where the time goes in v13:
time: 188 us; the launch traced here: 187 us
  Pallas kernels  120 us (64%)
  starting transfers between devices  19.6 us (10%)
  other arithmetic  19.3 us (10%)
  matrix products  12.7 us (7%)
  local copies, waits for them, and re-layouts  11.8 us (6%)
  between operations  3.46 us (2%)
    pallas_call x1, Pallas kernels, all_sum(): pl.pallas_call(functools.partial(_kernel, sizes), out_shape=tuple((jax.Sh...  92.7 us
    pallas_call x1, Pallas kernels, small_sum(): pl.pallas_call(functools.partial(_small_kernel, names), out_shape=jax.Sha...  16 us
    ppermute x2, starting transfers between devices, padded_2(): lax.ppermute(tail, axis, [(i, (i + 1) % count) for i in range(ends)])  9.97 us
    unnamed x40, local copies, waits for them, and re-layouts  7.35 us
    pallas_call x1, Pallas kernels, corr_fwd(): pl.pallas_call(_corr_fwd_kernel, grid=(clips,), in_specs=[pl.BlockSpec((N...  6 us
    ppermute x2, starting transfers between devices, from_behind(): lax.ppermute(value, axis, [(source, source + steps) for source in range(i...  5.75 us
    pallas_call x1, Pallas kernels, corr_bwd(): pl.pallas_call(_corr_bwd_kernel, grid=(clips,), in_specs=[pl.BlockSpec((N...  5.44 us
    dot_general x2, matrix products, conv_grad(): jnp.einsum('rk,re->ke', columns, grad_before, preferred_element_type=jnp....  4.29 us
  transfers between devices with their start and end apart: 6, of which 0 were waited for; matrix products, arithmetic and copies ran while one was open for 8% of the time, Pallas kernels for 9%

profile of v13, /device:TPU:1, one launch (start us, length us, event | category | flops | bytes accessed | tf_op | source)
XLA Modules:
  0.0 187.0 jit_solution(3979263872682811049)
XLA Ops:
  0.6 0.0 copy-start
  0.6 0.9 pad_maximum_fusion.5
  1.5 4.9 %collective-permute-start = (bf16[2,4,1,256]{3,2,1,0:T(2,128)(2,1)S(1)}, bf16[2,4,1,256]{3,2,1,0:T(2,128)(2,1)S(1)}, u32[]{:S(2)}, u32[]{:S(2)}) collective-permute-start(bf16[2,4,1,256]{3,2,1,0:T(2,128)(2,1)S(1)} %get-tuple-element.40), channel_id=1, source_target_pairs={{0,1},{1,2},{2,3},{3,4},{4,5},{5,6},{6,7},{8,9},{9,10},{10,11},{11... | collective-permute-start | bytes 12296 | tf_op jit(solution)/shard_map/ppermute | solution.py:449
  6.5 1.9 %collective-permute-start.1 = (bf16[2,4,1,256]{3,2,1,0:T(2,128)(2,1)S(1)}, bf16[2,4,1,256]{3,2,1,0:T(2,128)(2,1)S(1)}, u32[]{:S(2)}, u32[]{:S(2)}) collective-permute-start(bf16[2,4,1,256]{3,2,1,0:T(2,128)(2,1)S(1)} %get-tuple-element.41), channel_id=1, source_target_pairs={{1,0},{2,1},{3,2},{4,3},{5,4},{6,5},{7,6},{9,8},{10,9},{11,10},{12... | collective-permute-start | bytes 12296 | tf_op jit(solution)/shard_map/ppermute | solution.py:451
  8.4 0.1 broadcast_add_fusion
  8.5 0.1 broadcast_compare_fusion
  8.6 0.7 broadcast_compare_fusion.1
  9.4 0.7 compare_convert_fusion
  10.1 1.3 subtract_reduce_fusion
  11.4 1.2 fusion.28.t_ref
  12.6 16.0 %shard_map.119 = s32[8,128]{1,0:T(8,128)} custom-call(s32[8,128]{1,0:T(8,128)} %fusion.28.t_ref), custom_call_target="tpu_custom_call" | custom-call | tf_op jit(solution)/shard_map/pallas_call | solution.py:122
  28.6 1.2 slice.63
  30.5 0.0 collective-permute-done
  30.5 1.5 pad_maximum_fusion.3
  32.0 0.1 slice_bitcast_fusion
  32.1 0.5 fusion.36
  32.6 0.0 copy-start.12
  32.6 1.0 fusion.32
  33.6 0.1 copy-done.12
  33.7 0.8 convolution_convert_fusion
  34.4 0.6 copy-done.14
  35.0 5.0 %collective-permute-start.2 = (bf16[4,15,512]{2,1,0:T(8,128)(2,1)S(1)}, bf16[4,15,512]{2,1,0:T(8,128)(2,1)S(1)}, u32[]{:S(2)}, u32[]{:S(2)}) collective-permute-start(bf16[4,15,512]{2,1,0:T(8,128)(2,1)S(1)} %get-tuple-element.38), channel_id=1, source_target_pairs={{0,1},{1,2},{2,3},{3,4},{4,5},{5,6},{6,7},{8,9},{9,10},{10,11},{11... | collective-permute-start | bytes 184328 | tf_op jit(solution)/shard_map/ppermute | solution.py:449
  40.1 1.9 %collective-permute-start.3 = (bf16[4,15,512]{2,1,0:T(8,128)(2,1)S(1)}, bf16[4,15,512]{2,1,0:T(8,128)(2,1)S(1)}, u32[]{:S(2)}, u32[]{:S(2)}) collective-permute-start(bf16[4,15,512]{2,1,0:T(8,128)(2,1)S(1)} %get-tuple-element.39), channel_id=1, source_target_pairs={{1,0},{2,1},{3,2},{4,3},{5,4},{6,5},{7,6},{9,8},{10,9},{11,10},{12... | collective-permute-start | bytes 184328 | tf_op jit(solution)/shard_map/ppermute | solution.py:451
  42.0 1.2 pad_maximum_fusion.1
  43.3 1.0 fusion.31
  44.2 0.1 copy-done.10
  44.3 1.8 fusion.2
  46.1 1.2 pad_maximum_fusion
  47.3 0.5 fusion
  47.9 0.3 reverse.3
  48.1 0.6 copy.13.inv_ref
  48.7 1.3 pad.16.win_ref
  50.0 6.0 %shard_map.120 = (f32[4,256,128]{2,1,0:T(8,128)}, f32[4,256,128]{2,1,0:T(8,128)}) custom-call(bf16[4,256,512]{2,1,0:T(8,128)(2,1)} %get-tuple-element.52.ev_ref, bf16[4,384,512]{2,1,0:T(8,128)(2,1)} %pad.16.win_ref, f32[4,1,384]{2,1,0:T(1,128)} %copy.13.inv_ref), custom_call_target="tpu_custom_call" | custom-call | tf_op jit(solution)/shard_map/pallas_call | solution.py:377
  56.0 1.9 multiply_reduce_fusion
  57.9 0.7 select_reduce_fusion
  58.6 2.6 %multiply_reduce_fusion.1 = (f32[4,256]{1,0:T(4,128)S(1)}, f32[4,256,128]{2,1,0:T(8,128)S(1)}, bf16[4,256,128]{2,1,0:T(8,128)(2,1)}) fusion(f32[4,256,128]{2,1,0:T(8,128)} %get-tuple-element.16, f32[4,256,128]{2,1,0:T(8,128)} %get-tuple-element.15, f32[4,128]{1,0:T(4,128)S(1)} %compare_convert_fusion, f32[4,256]{1,0:T(4,128)S(1)} %get-tuple-element.28, ...), kind=kLoop, calls=%fused_computation.45 | loop fusion | flops 2096128 | bytes 2022544 | tf_op jit(solution)/shard_map/reduce_sum | solution.py:575
  61.3 0.0 copy-start.1
  61.3 1.0 broadcast_multiply_fusion.at_ref
  62.3 5.4 %shard_map.121 = (f32[4,256,512]{2,1,0:T(8,128)}, f32[4,384,512]{2,1,0:T(8,128)}, f32[4,1,384]{2,1,0:T(1,128)}) custom-call(bf16[4,256,128]{2,1,0:T(8,128)(2,1)} %get-tuple-element.35.gd_ref, f32[4,256,128]{2,1,0:T(8,128)} %broadcast_multiply_fusion.at_ref, bf16[4,256,512]{2,1,0:T(8,128)(2,1)} %get-tuple-element.52.ev_ref, bf16[4,384,512]{2,1,0:T(8,128)(2,1)} %pad.16.win_ref), custom_call_target="tpu_custom_call" | custom-call | tf_op jit(solution)/shard_map/pallas_call | solution.py:414
  67.7 2.1 %fusion.4 = bf16[4,256,512]{2,1,0:T(8,128)(2,1)S(1)} fusion(f32[4,256,512]{2,1,0:T(8,128)} %get-tuple-element.19, bf16[4,256,512]{2,1,0:T(8,128)(2,1)S(1)} %copy-done.1, f32[4,256]{1,0:T(4,128)S(1)} %fusion.26), kind=kLoop, calls=%fused_computation.8 | loop fusion | flops 2097152 | bytes 4198400 | tf_op jit(solution)/shard_map/convert_element_type | solution.py:591
  69.8 0.1 copy-done.17
  70.0 0.8 convolution_bitcast_fusion.refs_3_
  70.8 1.1 copy-done.2
  71.9 0.3 fusion.1
  72.2 1.9 %collective-permute-start.4 = (f32[4,15,512]{2,1,0:T(8,128)S(1)}, f32[4,15,512]{2,1,0:T(8,128)S(1)}, u32[]{:S(2)}, u32[]{:S(2)}) collective-permute-start(f32[4,15,512]{2,1,0:T(8,128)S(1)} %get-tuple-element.33), channel_id=1, source_target_pairs={{1,0},{2,1},{3,2},{4,3},{5,4},{6,5},{7,6},{9,8},{10,9},{11,10},{12... | collective-permute-start | bytes 368648 | tf_op jit(solution)/shard_map/ppermute | solution.py:461
  74.2 3.8 %collective-permute-start.5 = (f32[4,15,512]{2,1,0:T(8,128)S(1)}, f32[4,15,512]{2,1,0:T(8,128)S(1)}, u32[]{:S(2)}, u32[]{:S(2)}) collective-permute-start(f32[4,15,512]{2,1,0:T(8,128)S(1)} %get-tuple-element.34), channel_id=1, source_target_pairs={{0,1},{1,2},{2,3},{3,4},{4,5},{5,6},{6,7},{8,9},{9,10},{10,11},{11... | collective-permute-start | bytes 368648 | tf_op jit(solution)/shard_map/ppermute | solution.py:461
  78.0 1.2 fusion.13
  79.2 0.2 copy-done.4
  79.4 2.1 %fusion.39.refs_1_ = f32[768,512]{1,0:T(8,128)} fusion(bf16[1024,768]{1,0:T(8,128)(2,1)S(1)} %bitcast.93, bf16[1024,512]{1,0:T(8,128)(2,1)S(1)} %fusion.13), kind=kOutput, calls=%fused_computation.87 | convolution fusion | flops 805306368 | bytes 4194304 | tf_op jit(solution)/shard_map/rk,re->ke/dot_general | solution.py:517
  81.6 0.8 fusion.27.refs_4_
  82.4 0.0 collective-permute-done.5
  82.4 0.3 fusion.6
  82.7 0.4 copy-done.15
  83.2 0.8 convolution_bitcast_fusion.1.refs_2_
  84.0 0.2 copy-done.13
  84.2 1.2 fusion.20
  85.4 0.2 copy-done.3
  85.6 2.1 %fusion.38.refs_0_ = f32[768,512]{1,0:T(8,128)} fusion(bf16[1024,768]{1,0:T(8,128)(2,1)S(1)} %bitcast.92, bf16[1024,512]{1,0:T(8,128)(2,1)S(1)} %fusion.20), kind=kOutput, calls=%fused_computation.86 | convolution fusion | flops 805306368 | bytes 4194304 | tf_op jit(solution)/shard_map/rk,re->ke/dot_general | solution.py:517
  87.8 92.7 %shard_map.122 = (f32[768,512]{1,0:T(8,128)S(1)}, f32[768,512]{1,0:T(8,128)}, f32[512,512]{1,0:T(8,128)S(1)}, f32[512,512]{1,0:T(8,128)S(1)}, f32[8,128]{1,0:T(8,128)S(1)}) custom-call(f32[768,512]{1,0:T(8,128)} %fusion.38.refs_0_, f32[768,512]{1,0:T(8,128)} %fusion.39.refs_1_, f32[512,512]{1,0:T(8,128)S(1)} %convolution_bitcast_fusion.1.refs_2_, ...), custom_call_target="tpu_custom_call" | custom-call | tf_op jit(solution)/shard_map/pallas_call | solution.py:325
  180.4 0.5 slice.75
  181.6 1.1 copy.24
  182.8 1.0 copy.25
  183.7 1.1 copy.26
  184.9 1.0 copy.27
  (38 shorter events, 0.2 us)
Async XLA Ops:
  0.6 32.0 %copy-start = (bf16[3,256,512]{2,1,0:T(8,128)(2,1)S(1)}, bf16[3,256,512]{2,1,0:T(8,128)(2,1)}, u32[]{:S(2)}) copy-start(bf16[3,256,512]{2,1,0:T(8,128)(2,1)} %param.12) | copy-start | bytes 2359300
  1.5 29.0 %collective-permute-start = (bf16[2,4,1,256]{3,2,1,0:T(2,128)(2,1)S(1)}, bf16[2,4,1,256]{3,2,1,0:T(2,128)(2,1)S(1)}, u32[]{:S(2)}, u32[]{:S(2)}) collective-permute-start(bf16[2,4,1,256]{3,2,1,0:T(2,128)(2,1)S(1)} %get-tuple-element.40), channel_id=1, source_target_pairs={{0,1},{1,2},{2,3},{3,4},{4,5},{5,6},{6,7},{8,9},{9,10},{10,11},{11... | collective-permute-start | bytes 12296 | tf_op jit(solution)/shard_map/ppermute | solution.py:449
  6.5 24.1 %collective-permute-start.1 = (bf16[2,4,1,256]{3,2,1,0:T(2,128)(2,1)S(1)}, bf16[2,4,1,256]{3,2,1,0:T(2,128)(2,1)S(1)}, u32[]{:S(2)}, u32[]{:S(2)}) collective-permute-start(bf16[2,4,1,256]{3,2,1,0:T(2,128)(2,1)S(1)} %get-tuple-element.41), channel_id=1, source_target_pairs={{1,0},{2,1},{3,2},{4,3},{5,4},{6,5},{7,6},{9,8},{10,9},{11,10},{12... | collective-permute-start | bytes 12296 | tf_op jit(solution)/shard_map/ppermute | solution.py:451
  32.6 1.0 copy-start.12
  33.7 1.4 copy-start.14
  35.0 8.2 %copy-start.9 = (bf16[3,256,512]{2,1,0:T(8,128)(2,1)S(1)}, bf16[3,256,512]{2,1,0:T(8,128)(2,1)}, u32[]{:S(2)}) copy-start(bf16[3,256,512]{2,1,0:T(8,128)(2,1)} %param.14) | copy-start | bytes 2359300
  35.0 12.3 %collective-permute-start.2 = (bf16[4,15,512]{2,1,0:T(8,128)(2,1)S(1)}, bf16[4,15,512]{2,1,0:T(8,128)(2,1)S(1)}, u32[]{:S(2)}, u32[]{:S(2)}) collective-permute-start(bf16[4,15,512]{2,1,0:T(8,128)(2,1)S(1)} %get-tuple-element.38), channel_id=1, source_target_pairs={{0,1},{1,2},{2,3},{3,4},{4,5},{5,6},{6,7},{8,9},{9,10},{10,11},{11... | collective-permute-start | bytes 184328 | tf_op jit(solution)/shard_map/ppermute | solution.py:449
  40.1 7.2 %collective-permute-start.3 = (bf16[4,15,512]{2,1,0:T(8,128)(2,1)S(1)}, bf16[4,15,512]{2,1,0:T(8,128)(2,1)S(1)}, u32[]{:S(2)}, u32[]{:S(2)}) collective-permute-start(bf16[4,15,512]{2,1,0:T(8,128)(2,1)S(1)} %get-tuple-element.39), channel_id=1, source_target_pairs={{1,0},{2,1},{3,2},{4,3},{5,4},{6,5},{7,6},{9,8},{10,9},{11,10},{12... | collective-permute-start | bytes 184328 | tf_op jit(solution)/shard_map/ppermute | solution.py:451
  43.3 1.0 copy-start.10
  44.3 1.8 copy-start.16
  48.7 7.3 %copy-start.6 = (s32[4]{0:T(128)S(1)}, s32[4]{0:T(128)}, u32[]{:S(2)}) copy-start(s32[4]{0:T(128)} %param.10) | copy-start | bytes 52
  50.0 7.9 %copy-start.8 = (s32[4]{0:T(128)S(1)}, s32[4]{0:T(128)}, u32[]{:S(2)}) copy-start(s32[4]{0:T(128)} %param.11) | copy-start | bytes 52
  61.3 6.5 %copy-start.1 = (bf16[4,256,512]{2,1,0:T(8,128)(2,1)S(1)}, bf16[4,256,512]{2,1,0:T(8,128)(2,1)}, u32[]{:S(2)}) copy-start(bf16[4,256,512]{2,1,0:T(8,128)(2,1)} %get-tuple-element.52.ev_ref) | copy-start | bytes 3145732
  67.7 2.2 %copy-start.17 = (f32[4,256,512]{2,1,0:T(8,128)S(1)}, f32[4,256,512]{2,1,0:T(8,128)}, u32[]{:S(2)}) copy-start(f32[4,256,512]{2,1,0:T(8,128)} %copy-done.16) | copy-start | bytes 6291460
  70.0 0.8 copy-start.7
  70.0 1.9 %copy-start.2 = (f32[4,384,512]{2,1,0:T(8,128)S(1)}, f32[4,384,512]{2,1,0:T(8,128)}, u32[]{:S(2)}) copy-start(f32[4,384,512]{2,1,0:T(8,128)} %get-tuple-element.17) | copy-start | bytes 9437188
  71.9 6.1 %copy-start.11 = (bf16[512,512]{1,0:T(8,128)(2,1)S(1)}, bf16[512,512]{1,0:T(8,128)(2,1)}, u32[]{:S(2)}) copy-start(bf16[512,512]{1,0:T(8,128)(2,1)} %param.15) | copy-start | bytes 1572868
  72.2 10.1 %collective-permute-start.4 = (f32[4,15,512]{2,1,0:T(8,128)S(1)}, f32[4,15,512]{2,1,0:T(8,128)S(1)}, u32[]{:S(2)}, u32[]{:S(2)}) collective-permute-start(f32[4,15,512]{2,1,0:T(8,128)S(1)} %get-tuple-element.33), channel_id=1, source_target_pairs={{1,0},{2,1},{3,2},{4,3},{5,4},{6,5},{7,6},{9,8},{10,9},{11,10},{12... | collective-permute-start | bytes 368648 | tf_op jit(solution)/shard_map/ppermute | solution.py:461
  74.2 8.2 %collective-permute-start.5 = (f32[4,15,512]{2,1,0:T(8,128)S(1)}, f32[4,15,512]{2,1,0:T(8,128)S(1)}, u32[]{:S(2)}, u32[]{:S(2)}) collective-permute-start(f32[4,15,512]{2,1,0:T(8,128)S(1)} %get-tuple-element.34), channel_id=1, source_target_pairs={{0,1},{1,2},{2,3},{3,4},{4,5},{5,6},{6,7},{8,9},{9,10},{10,11},{11... | collective-permute-start | bytes 368648 | tf_op jit(solution)/shard_map/ppermute | solution.py:461
  78.0 1.4 copy-start.4
  81.6 1.6 copy-start.15
  83.2 1.0 copy-start.13
  84.2 1.4 copy-start.3
  181.6 2.1 %copy-start.5 = (f32[768,512]{1,0:T(8,128)S(1)}, f32[768,512]{1,0:T(8,128)}, u32[]{:S(2)}) copy-start(f32[768,512]{1,0:T(8,128)} %get-tuple-element.23) | copy-start | bytes 4718596

commit v14 on v12

--- a/solution.py
+++ b/solution.py
@@ -303,7 +303,7 @@
     _ag_stage([(nc, core, nbc, 1, 0, rows, None)], half_ref, hsend, hrecv, sem)
     start = 0
     for size, out_ref in zip(sizes, outs):
-        out_ref[...] = half_ref[start : start + size].astype(out_ref.dtype)
+        out_ref[...] = half_ref[start : start + size]
         start += size
 
 
@@ -324,7 +324,7 @@
     vmem = pl.BlockSpec(memory_space=pltpu.VMEM)
     return pl.pallas_call(
         functools.partial(_kernel, sizes),
-        out_shape=tuple(jax.ShapeDtypeStruct(p.shape, p.dtype) for p in parts)
+        out_shape=tuple(jax.ShapeDtypeStruct(p.shape, jnp.bfloat16) for p in parts)
         + (jax.ShapeDtypeStruct(small.shape, small.dtype),),
         in_specs=[vmem] * (len(parts) + 1),
         out_specs=(vmem,) * (len(parts) + 1),
@@ -611,7 +611,9 @@
     lanes = grad_ap.shape[1]
     loss_block = jnp.zeros((8, 128), jnp.float32).at[0, 0].set(loss_local)
     *sums, loss_total = all_sum([g.reshape(-1, lanes) for g in parts], loss_block)
-    grad_ac, grad_vc, grad_ap, grad_vp = (t.reshape(g.shape) for t, g in zip(sums, parts))
+    grad_ac, grad_vc, grad_ap, grad_vp = (
+        t.astype(jnp.float32).reshape(g.shape) for t, g in zip(sums, parts)
+    )
     loss_sum = loss_total[0, 0]
     return (loss_sum / count, grad_ac, grad_ap, grad_vc, grad_vp)
 

time: 188 us -> 187 us (level)
  other arithmetic: 17.3 us -> 22.2 us
  local copies, waits for them, and re-layouts: 13.9 us -> 9.71 us
    unnamed x40 -> x34, local copies, waits for them, and re-layouts: 7.34 us -> 3.18 us
    reshape x0 -> x2, other arithmetic: none -> 2.7 us  [shards(): t.astype(jnp.float32).reshape(g.shape)]
    convert_element_type x0 -> x2, other arithmetic: none -> 2.19 us  [shards(): t.astype(jnp.float32).reshape(g.shape)]
where the time goes in v14:
time: 187 us
  Pallas kernels  119 us (64%)
  other arithmetic  22.2 us (12%)
  starting transfers between devices  19.6 us (10%)
  matrix products  12.6 us (7%)
  local copies, waits for them, and re-layouts  9.71 us (5%)
  between operations  3.44 us (2%)
    pallas_call x1, Pallas kernels, all_sum(): pl.pallas_call(functools.partial(_kernel, sizes), out_shape=tuple((jax.Sh...  91.6 us
    pallas_call x1, Pallas kernels, small_sum(): pl.pallas_call(functools.partial(_small_kernel, names), out_shape=jax.Sha...  16 us
    ppermute x2, starting transfers between devices, padded_2(): lax.ppermute(tail, axis, [(i, (i + 1) % count) for i in range(ends)])  9.97 us
    pallas_call x1, Pallas kernels, corr_fwd(): pl.pallas_call(_corr_fwd_kernel, grid=(clips,), in_specs=[pl.BlockSpec((N...  6.01 us
    ppermute x2, starting transfers between devices, from_behind(): lax.ppermute(value, axis, [(source, source + steps) for source in range(i...  5.74 us
    pallas_call x1, Pallas kernels, corr_bwd(): pl.pallas_call(_corr_bwd_kernel, grid=(clips,), in_specs=[pl.BlockSpec((N...  5.45 us
    dot_general x2, matrix products, conv_grad(): jnp.einsum('rk,re->ke', columns, grad_before, preferred_element_type=jnp....  4.3 us
    ppermute x2, starting transfers between devices, padded_2(): lax.ppermute(head, axis, [((i + 1) % count, i) for i in range(ends)])  3.84 us
  transfers between devices with their start and end apart: 6, of which 0 were waited for; matrix products, arithmetic and copies ran while one was open for 8% of the time, Pallas kernels for 9%

profile of v14, /device:TPU:1, one launch (start us, length us, event | category | flops | bytes accessed | tf_op | source)
XLA Modules:
  0.0 186.6 jit_solution(4678994600116388454)
XLA Ops:
  0.6 0.0 copy-start
  0.6 0.9 pad_maximum_fusion.5
  1.5 4.9 %collective-permute-start = (bf16[2,4,1,256]{3,2,1,0:T(2,128)(2,1)S(1)}, bf16[2,4,1,256]{3,2,1,0:T(2,128)(2,1)S(1)}, u32[]{:S(2)}, u32[]{:S(2)}) collective-permute-start(bf16[2,4,1,256]{3,2,1,0:T(2,128)(2,1)S(1)} %get-tuple-element.64), channel_id=1, source_target_pairs={{0,1},{1,2},{2,3},{3,4},{4,5},{5,6},{6,7},{8,9},{9,10},{10,11},{11... | collective-permute-start | bytes 12296 | tf_op jit(solution)/shard_map/ppermute | solution.py:449
  6.5 1.9 %collective-permute-start.1 = (bf16[2,4,1,256]{3,2,1,0:T(2,128)(2,1)S(1)}, bf16[2,4,1,256]{3,2,1,0:T(2,128)(2,1)S(1)}, u32[]{:S(2)}, u32[]{:S(2)}) collective-permute-start(bf16[2,4,1,256]{3,2,1,0:T(2,128)(2,1)S(1)} %get-tuple-element.65), channel_id=1, source_target_pairs={{1,0},{2,1},{3,2},{4,3},{5,4},{6,5},{7,6},{9,8},{10,9},{11,10},{12... | collective-permute-start | bytes 12296 | tf_op jit(solution)/shard_map/ppermute | solution.py:451
  8.4 0.1 broadcast_add_fusion
  8.5 0.1 broadcast_compare_fusion
  8.6 0.7 broadcast_compare_fusion.1
  9.4 0.7 compare_convert_fusion
  10.1 1.3 subtract_reduce_fusion
  11.4 1.2 scatter.6.t_ref
  12.6 16.0 %shard_map.119 = s32[8,128]{1,0:T(8,128)} custom-call(s32[8,128]{1,0:T(8,128)} %scatter.6.t_ref), custom_call_target="tpu_custom_call" | custom-call | tf_op jit(solution)/shard_map/pallas_call | solution.py:122
  28.6 1.2 slice.95
  30.5 0.0 collective-permute-done
  30.5 0.0 collective-permute-done.1
  30.5 1.5 pad_maximum_fusion.3
  32.0 0.1 slice_bitcast_fusion
  32.1 0.5 fusion.34
  32.6 0.0 copy-start.11
  32.6 1.0 fusion.30
  33.6 0.1 copy-done.11
  33.7 0.7 convolution_convert_fusion
  34.4 0.6 copy-done.13
  35.1 5.0 %collective-permute-start.2 = (bf16[4,15,512]{2,1,0:T(8,128)(2,1)S(1)}, bf16[4,15,512]{2,1,0:T(8,128)(2,1)S(1)}, u32[]{:S(2)}, u32[]{:S(2)}) collective-permute-start(bf16[4,15,512]{2,1,0:T(8,128)(2,1)S(1)} %get-tuple-element.62), channel_id=1, source_target_pairs={{0,1},{1,2},{2,3},{3,4},{4,5},{5,6},{6,7},{8,9},{9,10},{10,11},{11... | collective-permute-start | bytes 184328 | tf_op jit(solution)/shard_map/ppermute | solution.py:449
  40.1 1.9 %collective-permute-start.3 = (bf16[4,15,512]{2,1,0:T(8,128)(2,1)S(1)}, bf16[4,15,512]{2,1,0:T(8,128)(2,1)S(1)}, u32[]{:S(2)}, u32[]{:S(2)}) collective-permute-start(bf16[4,15,512]{2,1,0:T(8,128)(2,1)S(1)} %get-tuple-element.63), channel_id=1, source_target_pairs={{1,0},{2,1},{3,2},{4,3},{5,4},{6,5},{7,6},{9,8},{10,9},{11,10},{12... | collective-permute-start | bytes 184328 | tf_op jit(solution)/shard_map/ppermute | solution.py:451
  42.0 1.2 pad_maximum_fusion.1
  43.3 1.0 fusion.29
  44.2 0.1 copy-done.9
  44.3 1.8 fusion.2
  46.1 1.2 pad_maximum_fusion
  47.3 0.5 fusion
  47.9 0.3 reverse.3
  48.2 0.6 copy.13.inv_ref
  48.8 1.3 pad.27.win_ref
  50.0 6.0 %shard_map.120 = (f32[4,256,128]{2,1,0:T(8,128)}, f32[4,256,128]{2,1,0:T(8,128)}) custom-call(bf16[4,256,512]{2,1,0:T(8,128)(2,1)} %get-tuple-element.76.ev_ref, bf16[4,384,512]{2,1,0:T(8,128)(2,1)} %pad.27.win_ref, f32[4,1,384]{2,1,0:T(1,128)} %copy.13.inv_ref), custom_call_target="tpu_custom_call" | custom-call | tf_op jit(solution)/shard_map/pallas_call | solution.py:377
  56.1 1.9 multiply_reduce_fusion
  57.9 0.7 select_reduce_fusion
  58.6 2.6 %multiply_reduce_fusion.1 = (f32[4,256]{1,0:T(4,128)S(1)}, f32[4,256,128]{2,1,0:T(8,128)S(1)}, bf16[4,256,128]{2,1,0:T(8,128)(2,1)}) fusion(f32[4,256,128]{2,1,0:T(8,128)} %get-tuple-element.40, f32[4,256,128]{2,1,0:T(8,128)} %get-tuple-element.39, f32[4,128]{1,0:T(4,128)S(1)} %compare_convert_fusion, f32[4,256]{1,0:T(4,128)S(1)} %get-tuple-element.52, ...), kind=kLoop, calls=%fused_computation.45 | loop fusion | flops 2096128 | bytes 2022544 | tf_op jit(solution)/shard_map/reduce_sum | solution.py:574
  61.3 0.0 copy-start.1
  61.3 1.0 broadcast_multiply_fusion.at_ref
  62.3 5.4 %shard_map.121 = (f32[4,256,512]{2,1,0:T(8,128)}, f32[4,384,512]{2,1,0:T(8,128)}, f32[4,1,384]{2,1,0:T(1,128)}) custom-call(bf16[4,256,128]{2,1,0:T(8,128)(2,1)} %get-tuple-element.59.gd_ref, f32[4,256,128]{2,1,0:T(8,128)} %broadcast_multiply_fusion.at_ref, bf16[4,256,512]{2,1,0:T(8,128)(2,1)} %get-tuple-element.76.ev_ref, bf16[4,384,512]{2,1,0:T(8,128)(2,1)} %pad.27.win_ref), custom_call_target="tpu_custom_call" | custom-call | tf_op jit(solution)/shard_map/pallas_call | solution.py:414
  67.8 2.1 %fusion.4 = bf16[4,256,512]{2,1,0:T(8,128)(2,1)S(1)} fusion(f32[4,256,512]{2,1,0:T(8,128)} %get-tuple-element.43, bf16[4,256,512]{2,1,0:T(8,128)(2,1)S(1)} %copy-done.1, f32[4,256]{1,0:T(4,128)S(1)} %fusion.26), kind=kLoop, calls=%fused_computation.8 | loop fusion | flops 2097152 | bytes 4198400 | tf_op jit(solution)/shard_map/convert_element_type | solution.py:590
  69.8 0.1 copy-done.16
  70.0 0.8 convolution_bitcast_fusion.refs_3_
  70.8 1.1 copy-done.2
  71.9 0.3 fusion.1
  72.2 1.9 %collective-permute-start.4 = (f32[4,15,512]{2,1,0:T(8,128)S(1)}, f32[4,15,512]{2,1,0:T(8,128)S(1)}, u32[]{:S(2)}, u32[]{:S(2)}) collective-permute-start(f32[4,15,512]{2,1,0:T(8,128)S(1)} %get-tuple-element.57), channel_id=1, source_target_pairs={{1,0},{2,1},{3,2},{4,3},{5,4},{6,5},{7,6},{9,8},{10,9},{11,10},{12... | collective-permute-start | bytes 368648 | tf_op jit(solution)/shard_map/ppermute | solution.py:461
  74.2 3.8 %collective-permute-start.5 = (f32[4,15,512]{2,1,0:T(8,128)S(1)}, f32[4,15,512]{2,1,0:T(8,128)S(1)}, u32[]{:S(2)}, u32[]{:S(2)}) collective-permute-start(f32[4,15,512]{2,1,0:T(8,128)S(1)} %get-tuple-element.58), channel_id=1, source_target_pairs={{0,1},{1,2},{2,3},{3,4},{4,5},{5,6},{6,7},{8,9},{9,10},{10,11},{11... | collective-permute-start | bytes 368648 | tf_op jit(solution)/shard_map/ppermute | solution.py:461
  78.0 1.2 fusion.13
  79.2 0.2 copy-done.4
  79.4 2.1 %fusion.37.refs_1_ = f32[768,512]{1,0:T(8,128)} fusion(bf16[1024,768]{1,0:T(8,128)(2,1)S(1)} %bitcast.98, bf16[1024,512]{1,0:T(8,128)(2,1)S(1)} %fusion.13), kind=kOutput, calls=%fused_computation.84 | convolution fusion | flops 805306368 | bytes 4194304 | tf_op jit(solution)/shard_map/rk,re->ke/dot_general | solution.py:517
  81.6 0.8 scatter.9.refs_4_
  82.4 0.3 fusion.6
  82.7 0.4 copy-done.14
  83.2 0.8 convolution_bitcast_fusion.1.refs_2_
  83.9 0.3 copy-done.12
  84.2 1.2 fusion.20
  85.4 0.2 copy-done.3
  85.6 2.1 %fusion.36.refs_0_ = f32[768,512]{1,0:T(8,128)} fusion(bf16[1024,768]{1,0:T(8,128)(2,1)S(1)} %bitcast.97, bf16[1024,512]{1,0:T(8,128)(2,1)S(1)} %fusion.20), kind=kOutput, calls=%fused_computation.83 | convolution fusion | flops 805306368 | bytes 4194304 | tf_op jit(solution)/shard_map/rk,re->ke/dot_general | solution.py:517
  87.8 91.6 %shard_map.122 = (bf16[768,512]{1,0:T(8,128)(2,1)S(1)}, bf16[768,512]{1,0:T(8,128)(2,1)S(1)}, bf16[512,512]{1,0:T(8,128)(2,1)S(1)}, bf16[512,512]{1,0:T(8,128)(2,1)S(1)}, f32[8,128]{1,0:T(8,128)S(1)}) custom-call(f32[768,512]{1,0:T(8,128)} %fusion.36.refs_0_, f32[768,512]{1,0:T(8,128)} %fusion.37.refs_1_, f32[512,512]{1,0:T(8,128)S(1)} %convolution_bitcast_fusion.1.refs_2_, ...), custom_call_target="tpu_custom_call" | custom-call | tf_op jit(solution)/shard_map/pallas_call | solution.py:325
  179.4 1.4 convert.2
  180.7 1.3 convert.3
  182.1 1.1 convert_element_type.75
  183.2 1.1 convert_element_type.76
  184.3 0.5 slice.107
  (36 shorter events, 0.2 us)
Async XLA Ops:
  0.6 32.0 %copy-start = (bf16[3,256,512]{2,1,0:T(8,128)(2,1)S(1)}, bf16[3,256,512]{2,1,0:T(8,128)(2,1)}, u32[]{:S(2)}) copy-start(bf16[3,256,512]{2,1,0:T(8,128)(2,1)} %param.16) | copy-start | bytes 2359300
  1.5 29.0 %collective-permute-start = (bf16[2,4,1,256]{3,2,1,0:T(2,128)(2,1)S(1)}, bf16[2,4,1,256]{3,2,1,0:T(2,128)(2,1)S(1)}, u32[]{:S(2)}, u32[]{:S(2)}) collective-permute-start(bf16[2,4,1,256]{3,2,1,0:T(2,128)(2,1)S(1)} %get-tuple-element.64), channel_id=1, source_target_pairs={{0,1},{1,2},{2,3},{3,4},{4,5},{5,6},{6,7},{8,9},{9,10},{10,11},{11... | collective-permute-start | bytes 12296 | tf_op jit(solution)/shard_map/ppermute | solution.py:449
  6.5 24.1 %collective-permute-start.1 = (bf16[2,4,1,256]{3,2,1,0:T(2,128)(2,1)S(1)}, bf16[2,4,1,256]{3,2,1,0:T(2,128)(2,1)S(1)}, u32[]{:S(2)}, u32[]{:S(2)}) collective-permute-start(bf16[2,4,1,256]{3,2,1,0:T(2,128)(2,1)S(1)} %get-tuple-element.65), channel_id=1, source_target_pairs={{1,0},{2,1},{3,2},{4,3},{5,4},{6,5},{7,6},{9,8},{10,9},{11,10},{12... | collective-permute-start | bytes 12296 | tf_op jit(solution)/shard_map/ppermute | solution.py:451
  32.6 1.0 copy-start.11
  33.7 1.4 copy-start.13
  35.0 8.2 %copy-start.8 = (bf16[3,256,512]{2,1,0:T(8,128)(2,1)S(1)}, bf16[3,256,512]{2,1,0:T(8,128)(2,1)}, u32[]{:S(2)}) copy-start(bf16[3,256,512]{2,1,0:T(8,128)(2,1)} %param.18) | copy-start | bytes 2359300
  35.1 12.3 %collective-permute-start.2 = (bf16[4,15,512]{2,1,0:T(8,128)(2,1)S(1)}, bf16[4,15,512]{2,1,0:T(8,128)(2,1)S(1)}, u32[]{:S(2)}, u32[]{:S(2)}) collective-permute-start(bf16[4,15,512]{2,1,0:T(8,128)(2,1)S(1)} %get-tuple-element.62), channel_id=1, source_target_pairs={{0,1},{1,2},{2,3},{3,4},{4,5},{5,6},{6,7},{8,9},{9,10},{10,11},{11... | collective-permute-start | bytes 184328 | tf_op jit(solution)/shard_map/ppermute | solution.py:449
  40.1 7.2 %collective-permute-start.3 = (bf16[4,15,512]{2,1,0:T(8,128)(2,1)S(1)}, bf16[4,15,512]{2,1,0:T(8,128)(2,1)S(1)}, u32[]{:S(2)}, u32[]{:S(2)}) collective-permute-start(bf16[4,15,512]{2,1,0:T(8,128)(2,1)S(1)} %get-tuple-element.63), channel_id=1, source_target_pairs={{1,0},{2,1},{3,2},{4,3},{5,4},{6,5},{7,6},{9,8},{10,9},{11,10},{12... | collective-permute-start | bytes 184328 | tf_op jit(solution)/shard_map/ppermute | solution.py:451
  43.3 1.0 copy-start.9
  44.3 1.8 copy-start.15
  48.8 7.3 %copy-start.5 = (s32[4]{0:T(128)S(1)}, s32[4]{0:T(128)}, u32[]{:S(2)}) copy-start(s32[4]{0:T(128)} %param.14) | copy-start | bytes 52
  50.0 7.9 %copy-start.7 = (s32[4]{0:T(128)S(1)}, s32[4]{0:T(128)}, u32[]{:S(2)}) copy-start(s32[4]{0:T(128)} %param.15) | copy-start | bytes 52
  61.3 6.5 %copy-start.1 = (bf16[4,256,512]{2,1,0:T(8,128)(2,1)S(1)}, bf16[4,256,512]{2,1,0:T(8,128)(2,1)}, u32[]{:S(2)}) copy-start(bf16[4,256,512]{2,1,0:T(8,128)(2,1)} %get-tuple-element.76.ev_ref) | copy-start | bytes 3145732
  67.7 2.2 %copy-start.16 = (f32[4,256,512]{2,1,0:T(8,128)S(1)}, f32[4,256,512]{2,1,0:T(8,128)}, u32[]{:S(2)}) copy-start(f32[4,256,512]{2,1,0:T(8,128)} %copy-done.15) | copy-start | bytes 6291460
  70.0 0.8 copy-start.6
  70.0 1.9 %copy-start.2 = (f32[4,384,512]{2,1,0:T(8,128)S(1)}, f32[4,384,512]{2,1,0:T(8,128)}, u32[]{:S(2)}) copy-start(f32[4,384,512]{2,1,0:T(8,128)} %get-tuple-element.41) | copy-start | bytes 9437188
  71.9 6.1 %copy-start.10 = (bf16[512,512]{1,0:T(8,128)(2,1)S(1)}, bf16[512,512]{1,0:T(8,128)(2,1)}, u32[]{:S(2)}) copy-start(bf16[512,512]{1,0:T(8,128)(2,1)} %param.19) | copy-start | bytes 1572868
  72.2 10.1 %collective-permute-start.4 = (f32[4,15,512]{2,1,0:T(8,128)S(1)}, f32[4,15,512]{2,1,0:T(8,128)S(1)}, u32[]{:S(2)}, u32[]{:S(2)}) collective-permute-start(f32[4,15,512]{2,1,0:T(8,128)S(1)} %get-tuple-element.57), channel_id=1, source_target_pairs={{1,0},{2,1},{3,2},{4,3},{5,4},{6,5},{7,6},{9,8},{10,9},{11,10},{12... | collective-permute-start | bytes 368648 | tf_op jit(solution)/shard_map/ppermute | solution.py:461
  74.2 8.2 %collective-permute-start.5 = (f32[4,15,512]{2,1,0:T(8,128)S(1)}, f32[4,15,512]{2,1,0:T(8,128)S(1)}, u32[]{:S(2)}, u32[]{:S(2)}) collective-permute-start(f32[4,15,512]{2,1,0:T(8,128)S(1)} %get-tuple-element.58), channel_id=1, source_target_pairs={{0,1},{1,2},{2,3},{3,4},{4,5},{5,6},{6,7},{8,9},{9,10},{10,11},{11... | collective-permute-start | bytes 368648 | tf_op jit(solution)/shard_map/ppermute | solution.py:461
  78.0 1.4 copy-start.4
  81.6 1.6 copy-start.14
  83.2 1.0 copy-start.12
  84.2 1.4 copy-start.3

commit v15 on v14

--- a/solution.py
+++ b/solution.py
@@ -438,7 +438,7 @@
 epsilon = 1e-06
 
 
-def padded_2(cells, sides, width):
+def padded_2(cells, sides, width, extra=0):
     for axis, dim in sides:
         count = lax.axis_size(axis)
         ends = count - 1
@@ -449,7 +449,8 @@
                 lax.ppermute(tail, axis, [(i, (i + 1) % count) for i in range(ends)]),
                 cells,
                 lax.ppermute(head, axis, [((i + 1) % count, i) for i in range(ends)]),
-            ],
+            ]
+            + ([jnp.zeros(cells.shape[:dim] + (extra,) + cells.shape[dim + 1 :], cells.dtype)] if extra else []),
             axis=dim,
         )
     return cells
@@ -530,7 +531,10 @@
     padded = padded_2(stacked, (("tm", 2),), 1)
     cols_a, pre_a, hid_a, emb_a = encoder(padded[0], w_audio_conv, w_audio_proj)
     cols_v, pre_v, hid_v, emb_v = encoder(padded[1], w_lip_conv, w_lip_proj)
-    window = padded_2(emb_a, (("tm", 1),), SPAN)
+    wide_len = frame_num + 2 * SPAN
+    wide_pad = -(-wide_len // 128) * 128
+    win_pad = padded_2(emb_a, (("tm", 1),), SPAN, wide_pad - wide_len)
+    window = win_pad[:, :wide_len]
     cols_a, pre_a, hid_a = (flatten_rows(cols_a), flatten_rows(pre_a), flatten_rows(hid_a))
     cols_v, pre_v, hid_v = (flatten_rows(cols_v), flatten_rows(pre_v), flatten_rows(hid_v))
     count_part = jnp.sum(lengths - jnp.abs(labels))
@@ -538,8 +542,6 @@
     count = small_sum(count_block, ("k",), 1)[0, 0].astype(jnp.float32)
     inv_win = inverse_norm(window)
     reciprocal_visual_length = inverse_norm(emb_v)
-    wide_pad = -(-wide_len // 128) * 128
-    win_pad = jnp.pad(window, ((0, 0), (0, wide_pad - wide_len), (0, 0)))
     inv_pad = jnp.pad(inv_win, ((0, 0), (0, wide_pad - wide_len)))[:, None, :]
     lagged_inner_terms, reciprocal_lag_strip = corr_fwd(emb_v, win_pad, inv_pad[:, :, ::-1])
     lanes_used = lagged_inner_terms.shape[2]

time: 187 us -> 188 us (level)
  no operation moved by 1% of the time
where the time goes in v15:
time: 188 us; the launch traced here: 187 us
  Pallas kernels  119 us (63%)
  other arithmetic  23.9 us (13%)
  starting transfers between devices  19.6 us (10%)
  matrix products  12.6 us (7%)
  local copies, waits for them, and re-layouts  8.61 us (5%)
  between operations  3.46 us (2%)
    pallas_call x1, Pallas kernels, all_sum(): pl.pallas_call(functools.partial(_kernel, sizes), out_shape=tuple((jax.Sh...  91.6 us
    pallas_call x1, Pallas kernels, small_sum(): pl.pallas_call(functools.partial(_small_kernel, names), out_shape=jax.Sha...  16 us
    ppermute x2, starting transfers between devices, padded_2(): lax.ppermute(tail, axis, [(i, (i + 1) % count) for i in range(ends)])  9.97 us
    pallas_call x1, Pallas kernels, corr_fwd(): pl.pallas_call(_corr_fwd_kernel, grid=(clips,), in_specs=[pl.BlockSpec((N...  5.99 us
    ppermute x2, starting transfers between devices, from_behind(): lax.ppermute(value, axis, [(source, source + steps) for source in range(i...  5.74 us
    pallas_call x1, Pallas kernels, corr_bwd(): pl.pallas_call(_corr_bwd_kernel, grid=(clips,), in_specs=[pl.BlockSpec((N...  5.44 us
    dot_general x2, matrix products, conv_grad(): jnp.einsum('rk,re->ke', columns, grad_before, preferred_element_type=jnp....  4.29 us
    ppermute x2, starting transfers between devices, padded_2(): lax.ppermute(head, axis, [((i + 1) % count, i) for i in range(ends)])  3.84 us
  transfers between devices with their start and end apart: 6, of which 0 were waited for; matrix products, arithmetic and copies ran while one was open for 8% of the time, Pallas kernels for 9%

profile of v15, /device:TPU:1, one launch (start us, length us, event | category | flops | bytes accessed | tf_op | source)
XLA Modules:
  0.0 187.2 jit_solution(15676376958017015353)
XLA Ops:
  0.6 0.0 copy-start
  0.6 0.9 pad_maximum_fusion.5
  1.5 4.9 %collective-permute-start = (bf16[2,4,1,256]{3,2,1,0:T(2,128)(2,1)S(1)}, bf16[2,4,1,256]{3,2,1,0:T(2,128)(2,1)S(1)}, u32[]{:S(2)}, u32[]{:S(2)}) collective-permute-start(bf16[2,4,1,256]{3,2,1,0:T(2,128)(2,1)S(1)} %get-tuple-element.62), channel_id=1, source_target_pairs={{0,1},{1,2},{2,3},{3,4},{4,5},{5,6},{6,7},{8,9},{9,10},{10,11},{11... | collective-permute-start | bytes 12296 | tf_op jit(solution)/shard_map/ppermute | solution.py:449
  6.5 1.9 %collective-permute-start.1 = (bf16[2,4,1,256]{3,2,1,0:T(2,128)(2,1)S(1)}, bf16[2,4,1,256]{3,2,1,0:T(2,128)(2,1)S(1)}, u32[]{:S(2)}, u32[]{:S(2)}) collective-permute-start(bf16[2,4,1,256]{3,2,1,0:T(2,128)(2,1)S(1)} %get-tuple-element.63), channel_id=1, source_target_pairs={{1,0},{2,1},{3,2},{4,3},{5,4},{6,5},{7,6},{9,8},{10,9},{11,10},{12... | collective-permute-start | bytes 12296 | tf_op jit(solution)/shard_map/ppermute | solution.py:451
  8.4 0.1 broadcast_add_fusion
  8.5 0.1 broadcast_compare_fusion
  8.6 0.7 broadcast_compare_fusion.1
  9.4 0.7 compare_convert_fusion
  10.1 1.3 subtract_reduce_fusion
  11.4 1.2 scatter.6.t_ref
  12.6 16.0 %shard_map.119 = s32[8,128]{1,0:T(8,128)} custom-call(s32[8,128]{1,0:T(8,128)} %scatter.6.t_ref), custom_call_target="tpu_custom_call" | custom-call | tf_op jit(solution)/shard_map/pallas_call | solution.py:122
  28.6 1.2 slice.97
  30.5 0.1 pad.32.clone
  30.6 0.0 collective-permute-done
  30.6 1.5 pad_maximum_fusion.3
  32.1 0.1 slice_bitcast_fusion
  32.2 0.6 fusion.34
  32.8 0.0 copy-start.11
  32.8 1.0 fusion.30
  33.8 0.1 copy-done.11
  33.8 0.7 convolution_convert_fusion
  34.6 0.6 copy-done.13
  35.2 5.0 %collective-permute-start.2 = (bf16[4,15,512]{2,1,0:T(8,128)(2,1)S(1)}, bf16[4,15,512]{2,1,0:T(8,128)(2,1)S(1)}, u32[]{:S(2)}, u32[]{:S(2)}) collective-permute-start(bf16[4,15,512]{2,1,0:T(8,128)(2,1)S(1)} %get-tuple-element.60), channel_id=1, source_target_pairs={{0,1},{1,2},{2,3},{3,4},{4,5},{5,6},{6,7},{8,9},{9,10},{10,11},{11... | collective-permute-start | bytes 184328 | tf_op jit(solution)/shard_map/ppermute | solution.py:449
  40.3 1.9 %collective-permute-start.3 = (bf16[4,15,512]{2,1,0:T(8,128)(2,1)S(1)}, bf16[4,15,512]{2,1,0:T(8,128)(2,1)S(1)}, u32[]{:S(2)}, u32[]{:S(2)}) collective-permute-start(bf16[4,15,512]{2,1,0:T(8,128)(2,1)S(1)} %get-tuple-element.61), channel_id=1, source_target_pairs={{1,0},{2,1},{3,2},{4,3},{5,4},{6,5},{7,6},{9,8},{10,9},{11,10},{12... | collective-permute-start | bytes 184328 | tf_op jit(solution)/shard_map/ppermute | solution.py:451
  42.2 1.2 pad_maximum_fusion.1
  43.4 1.0 fusion.29
  44.4 0.1 copy-done.9
  44.5 1.8 fusion.2
  46.3 1.2 pad_maximum_fusion
  47.5 0.5 fusion
  48.0 0.3 reverse.3
  48.3 0.6 copy.13.inv_ref
  48.9 1.6 maximum_maximum_fusion.win_ref
  50.5 6.0 %shard_map.120 = (f32[4,256,128]{2,1,0:T(8,128)}, f32[4,256,128]{2,1,0:T(8,128)}) custom-call(bf16[4,256,512]{2,1,0:T(8,128)(2,1)} %get-tuple-element.74.ev_ref, bf16[4,384,512]{2,1,0:T(8,128)(2,1)} %maximum_maximum_fusion.win_ref, f32[4,1,384]{2,1,0:T(1,128)} %copy.13.inv_ref), custom_call_target="tpu_custom_call" | custom-call | tf_op jit(solution)/shard_map/pallas_call | solution.py:377
  56.5 1.9 multiply_reduce_fusion
  58.4 0.7 select_reduce_fusion
  59.1 2.6 %multiply_reduce_fusion.1 = (f32[4,256]{1,0:T(4,128)S(1)}, f32[4,256,128]{2,1,0:T(8,128)S(1)}, bf16[4,256,128]{2,1,0:T(8,128)(2,1)}) fusion(f32[4,256,128]{2,1,0:T(8,128)} %get-tuple-element.40, f32[4,256,128]{2,1,0:T(8,128)} %get-tuple-element.39, f32[4,128]{1,0:T(4,128)S(1)} %compare_convert_fusion, f32[4,256]{1,0:T(4,128)S(1)} %get-tuple-element.52, ...), kind=kLoop, calls=%fused_computation.46 | loop fusion | flops 2096128 | bytes 2022544 | tf_op jit(solution)/shard_map/reduce_sum | solution.py:576
  61.8 0.0 copy-start.1
  61.8 1.0 broadcast_multiply_fusion.at_ref
  62.8 5.4 %shard_map.121 = (f32[4,256,512]{2,1,0:T(8,128)}, f32[4,384,512]{2,1,0:T(8,128)}, f32[4,1,384]{2,1,0:T(1,128)}) custom-call(bf16[4,256,128]{2,1,0:T(8,128)(2,1)} %get-tuple-element.57.gd_ref, f32[4,256,128]{2,1,0:T(8,128)} %broadcast_multiply_fusion.at_ref, bf16[4,256,512]{2,1,0:T(8,128)(2,1)} %get-tuple-element.74.ev_ref, ...), custom_call_target="tpu_custom_call" | custom-call | tf_op jit(solution)/shard_map/pallas_call | solution.py:414
  68.2 2.1 %fusion.4 = bf16[4,256,512]{2,1,0:T(8,128)(2,1)S(1)} fusion(f32[4,256,512]{2,1,0:T(8,128)} %get-tuple-element.43, bf16[4,256,512]{2,1,0:T(8,128)(2,1)S(1)} %copy-done.1, f32[4,256]{1,0:T(4,128)S(1)} %fusion.26), kind=kLoop, calls=%fused_computation.8 | loop fusion | flops 2097152 | bytes 4198400 | tf_op jit(solution)/shard_map/convert_element_type | solution.py:592
  70.3 0.1 copy-done.16
  70.4 0.8 convolution_bitcast_fusion.refs_3_
  71.3 1.1 copy-done.2
  72.3 0.5 fusion.1
  72.9 1.9 %collective-permute-start.4 = (f32[4,15,512]{2,1,0:T(8,128)S(1)}, f32[4,15,512]{2,1,0:T(8,128)S(1)}, u32[]{:S(2)}, u32[]{:S(2)}) collective-permute-start(f32[4,15,512]{2,1,0:T(8,128)S(1)} %get-tuple-element.55), channel_id=1, source_target_pairs={{1,0},{2,1},{3,2},{4,3},{5,4},{6,5},{7,6},{9,8},{10,9},{11,10},{12... | collective-permute-start | bytes 368648 | tf_op jit(solution)/shard_map/ppermute | solution.py:462
  74.8 3.8 %collective-permute-start.5 = (f32[4,15,512]{2,1,0:T(8,128)S(1)}, f32[4,15,512]{2,1,0:T(8,128)S(1)}, u32[]{:S(2)}, u32[]{:S(2)}) collective-permute-start(f32[4,15,512]{2,1,0:T(8,128)S(1)} %get-tuple-element.56), channel_id=1, source_target_pairs={{0,1},{1,2},{2,3},{3,4},{4,5},{5,6},{6,7},{8,9},{9,10},{10,11},{11... | collective-permute-start | bytes 368648 | tf_op jit(solution)/shard_map/ppermute | solution.py:462
  78.7 1.2 fusion.13
  79.8 0.2 copy-done.4
  80.1 2.1 %fusion.37.refs_1_ = f32[768,512]{1,0:T(8,128)} fusion(bf16[1024,768]{1,0:T(8,128)(2,1)S(1)} %bitcast.98, bf16[1024,512]{1,0:T(8,128)(2,1)S(1)} %fusion.13), kind=kOutput, calls=%fused_computation.85 | convolution fusion | flops 805306368 | bytes 4194304 | tf_op jit(solution)/shard_map/rk,re->ke/dot_general | solution.py:518
  82.2 0.8 scatter.9.refs_4_
  83.1 0.3 fusion.6
  83.4 0.4 copy-done.14
  83.8 0.8 convolution_bitcast_fusion.1.refs_2_
  84.6 0.3 copy-done.12
  84.8 1.2 fusion.20
  86.0 0.2 copy-done.3
  86.2 2.1 %fusion.36.refs_0_ = f32[768,512]{1,0:T(8,128)} fusion(bf16[1024,768]{1,0:T(8,128)(2,1)S(1)} %bitcast.97, bf16[1024,512]{1,0:T(8,128)(2,1)S(1)} %fusion.20), kind=kOutput, calls=%fused_computation.84 | convolution fusion | flops 805306368 | bytes 4194304 | tf_op jit(solution)/shard_map/rk,re->ke/dot_general | solution.py:518
  88.4 91.6 %shard_map.122 = (bf16[768,512]{1,0:T(8,128)(2,1)S(1)}, bf16[768,512]{1,0:T(8,128)(2,1)S(1)}, bf16[512,512]{1,0:T(8,128)(2,1)S(1)}, bf16[512,512]{1,0:T(8,128)(2,1)S(1)}, f32[8,128]{1,0:T(8,128)S(1)}) custom-call(f32[768,512]{1,0:T(8,128)} %fusion.36.refs_0_, f32[768,512]{1,0:T(8,128)} %fusion.37.refs_1_, f32[512,512]{1,0:T(8,128)S(1)} %convolution_bitcast_fusion.1.refs_2_, ...), custom_call_target="tpu_custom_call" | custom-call | tf_op jit(solution)/shard_map/pallas_call | solution.py:325
  180.0 1.4 convert.2
  181.4 1.3 convert.3
  182.7 1.1 convert_element_type.73
  183.8 1.1 convert_element_type.74
  184.9 0.5 slice.109
  (38 shorter events, 0.2 us)
Async XLA Ops:
  0.6 32.2 %copy-start = (bf16[3,256,512]{2,1,0:T(8,128)(2,1)S(1)}, bf16[3,256,512]{2,1,0:T(8,128)(2,1)}, u32[]{:S(2)}) copy-start(bf16[3,256,512]{2,1,0:T(8,128)(2,1)} %param.16) | copy-start | bytes 2359300
  1.5 29.1 %collective-permute-start = (bf16[2,4,1,256]{3,2,1,0:T(2,128)(2,1)S(1)}, bf16[2,4,1,256]{3,2,1,0:T(2,128)(2,1)S(1)}, u32[]{:S(2)}, u32[]{:S(2)}) collective-permute-start(bf16[2,4,1,256]{3,2,1,0:T(2,128)(2,1)S(1)} %get-tuple-element.62), channel_id=1, source_target_pairs={{0,1},{1,2},{2,3},{3,4},{4,5},{5,6},{6,7},{8,9},{9,10},{10,11},{11... | collective-permute-start | bytes 12296 | tf_op jit(solution)/shard_map/ppermute | solution.py:449
  6.5 24.2 %collective-permute-start.1 = (bf16[2,4,1,256]{3,2,1,0:T(2,128)(2,1)S(1)}, bf16[2,4,1,256]{3,2,1,0:T(2,128)(2,1)S(1)}, u32[]{:S(2)}, u32[]{:S(2)}) collective-permute-start(bf16[2,4,1,256]{3,2,1,0:T(2,128)(2,1)S(1)} %get-tuple-element.63), channel_id=1, source_target_pairs={{1,0},{2,1},{3,2},{4,3},{5,4},{6,5},{7,6},{9,8},{10,9},{11,10},{12... | collective-permute-start | bytes 12296 | tf_op jit(solution)/shard_map/ppermute | solution.py:451
  32.8 1.0 copy-start.11
  33.8 1.4 copy-start.13
  35.2 8.2 %copy-start.8 = (bf16[3,256,512]{2,1,0:T(8,128)(2,1)S(1)}, bf16[3,256,512]{2,1,0:T(8,128)(2,1)}, u32[]{:S(2)}) copy-start(bf16[3,256,512]{2,1,0:T(8,128)(2,1)} %param.18) | copy-start | bytes 2359300
  35.2 12.3 %collective-permute-start.2 = (bf16[4,15,512]{2,1,0:T(8,128)(2,1)S(1)}, bf16[4,15,512]{2,1,0:T(8,128)(2,1)S(1)}, u32[]{:S(2)}, u32[]{:S(2)}) collective-permute-start(bf16[4,15,512]{2,1,0:T(8,128)(2,1)S(1)} %get-tuple-element.60), channel_id=1, source_target_pairs={{0,1},{1,2},{2,3},{3,4},{4,5},{5,6},{6,7},{8,9},{9,10},{10,11},{11... | collective-permute-start | bytes 184328 | tf_op jit(solution)/shard_map/ppermute | solution.py:449
  40.3 7.3 %collective-permute-start.3 = (bf16[4,15,512]{2,1,0:T(8,128)(2,1)S(1)}, bf16[4,15,512]{2,1,0:T(8,128)(2,1)S(1)}, u32[]{:S(2)}, u32[]{:S(2)}) collective-permute-start(bf16[4,15,512]{2,1,0:T(8,128)(2,1)S(1)} %get-tuple-element.61), channel_id=1, source_target_pairs={{1,0},{2,1},{3,2},{4,3},{5,4},{6,5},{7,6},{9,8},{10,9},{11,10},{12... | collective-permute-start | bytes 184328 | tf_op jit(solution)/shard_map/ppermute | solution.py:451
  43.4 1.0 copy-start.9
  44.5 1.8 copy-start.15
  48.9 7.6 %copy-start.5 = (s32[4]{0:T(128)S(1)}, s32[4]{0:T(128)}, u32[]{:S(2)}) copy-start(s32[4]{0:T(128)} %param.14) | copy-start | bytes 52
  50.5 7.8 %copy-start.7 = (s32[4]{0:T(128)S(1)}, s32[4]{0:T(128)}, u32[]{:S(2)}) copy-start(s32[4]{0:T(128)} %param.15) | copy-start | bytes 52
  61.8 6.5 %copy-start.1 = (bf16[4,256,512]{2,1,0:T(8,128)(2,1)S(1)}, bf16[4,256,512]{2,1,0:T(8,128)(2,1)}, u32[]{:S(2)}) copy-start(bf16[4,256,512]{2,1,0:T(8,128)(2,1)} %get-tuple-element.74.ev_ref) | copy-start | bytes 3145732
  68.2 2.2 %copy-start.16 = (f32[4,256,512]{2,1,0:T(8,128)S(1)}, f32[4,256,512]{2,1,0:T(8,128)}, u32[]{:S(2)}) copy-start(f32[4,256,512]{2,1,0:T(8,128)} %copy-done.15) | copy-start | bytes 6291460
  70.4 0.8 copy-start.6
  70.4 1.9 %copy-start.2 = (f32[4,384,512]{2,1,0:T(8,128)S(1)}, f32[4,384,512]{2,1,0:T(8,128)}, u32[]{:S(2)}) copy-start(f32[4,384,512]{2,1,0:T(8,128)} %get-tuple-element.41) | copy-start | bytes 9437188
  72.3 6.3 %copy-start.10 = (bf16[512,512]{1,0:T(8,128)(2,1)S(1)}, bf16[512,512]{1,0:T(8,128)(2,1)}, u32[]{:S(2)}) copy-start(bf16[512,512]{1,0:T(8,128)(2,1)} %param.19) | copy-start | bytes 1572868
  72.9 10.2 %collective-permute-start.4 = (f32[4,15,512]{2,1,0:T(8,128)S(1)}, f32[4,15,512]{2,1,0:T(8,128)S(1)}, u32[]{:S(2)}, u32[]{:S(2)}) collective-permute-start(f32[4,15,512]{2,1,0:T(8,128)S(1)} %get-tuple-element.55), channel_id=1, source_target_pairs={{1,0},{2,1},{3,2},{4,3},{5,4},{6,5},{7,6},{9,8},{10,9},{11,10},{12... | collective-permute-start | bytes 368648 | tf_op jit(solution)/shard_map/ppermute | solution.py:462
  74.8 8.2 %collective-permute-start.5 = (f32[4,15,512]{2,1,0:T(8,128)S(1)}, f32[4,15,512]{2,1,0:T(8,128)S(1)}, u32[]{:S(2)}, u32[]{:S(2)}) collective-permute-start(f32[4,15,512]{2,1,0:T(8,128)S(1)} %get-tuple-element.56), channel_id=1, source_target_pairs={{0,1},{1,2},{2,3},{3,4},{4,5},{5,6},{6,7},{8,9},{9,10},{10,11},{11... | collective-permute-start | bytes 368648 | tf_op jit(solution)/shard_map/ppermute | solution.py:462
  78.6 1.4 copy-start.4
  82.2 1.6 copy-start.14
  83.8 1.0 copy-start.12
  84.8 1.4 copy-start.3
